TPU v7x, 32 devices: a whole 2x2x4 slice. The times are simulated.
32 devices in a mesh: seg: 8 (over y, x, core), head: 4 (over z).
Axes of the slice: x: 2, y: 2, z: 4, core: 2. Of those that a mesh axis runs over, the one named last changes fastest.
Arguments:
- tokens: bfloat16 [8192, 2048], P(('seg', 'head')), may hold values from -6 to 6
- cotangent: bfloat16 [8192, 2048], P(('seg', 'head')), may hold values from -6 to 6
- gain_attn: float32 [2048], replicated, may hold values from 0.5 to 1.5
- gain_mlp: float32 [2048], replicated, may hold values from 0.5 to 1.5
- w_query: bfloat16 [2048, 2048], P(None, 'head'), may hold values from -0.1875 to 0.1875
- w_key: bfloat16 [2048, 2048], P(None, 'head'), may hold values from -0.125 to 0.125
- w_value: bfloat16 [2048, 2048], P(None, 'head'), may hold values from -0.125 to 0.125
- w_out: bfloat16 [2048, 2048], P('head'), may hold values from -0.5 to 0.5
- w_gate: bfloat16 [2048, 8192], P(None, 'head'), may hold values from -0.125 to 0.125
- w_up: bfloat16 [2048, 8192], P(None, 'head'), may hold values from -0.125 to 0.125
- w_down: bfloat16 [8192, 2048], P('head'), may hold values from -0.0625 to 0.0625
- mem_gate: float32 [16], P('head'), may hold values from -2 to 2
- lengths: int32 [2], replicated, may hold values from 256 to 768, as said below
Outputs:
- output: bfloat16 [8192, 2048], P(('seg', 'head'))
- grad_tokens: bfloat16 [8192, 2048], P(('seg', 'head'))
- memory_after: float32 [8, 16, 128, 128], P('seg', 'head')
- normal_after: float32 [8, 16, 128], P('seg', 'head')
- grad_gain_attn: float32 [2048], replicated
- grad_gain_mlp: float32 [2048], replicated
- grad_query: float32 [2048, 2048], P(None, 'head')
- grad_key: float32 [2048, 2048], P(None, 'head')
- grad_value: float32 [2048, 2048], P(None, 'head')
- grad_out: float32 [2048, 2048], P('head')
- grad_gate: float32 [2048, 8192], P(None, 'head')
- grad_up: float32 [2048, 8192], P(None, 'head')
- grad_down: float32 [8192, 2048], P('head')
- grad_mem_gate: float32 [16], P('head')
Inputs may be any that keep to these rules, and one draw needn't show every extreme that they name: The last segment of sequence b holds valid tokens in its first lengths[b] places; the other places are padding. Some sequence has exactly 768.
All inputs are finite; a program needn't handle non-finite values.
Results may differ from a plain program's by a relative error of at most 0.014.
Values may be sent and summed in bfloat16 or wider, within the bound.
A program may use at most 320 MiB of HBM per device.

v0:
```python
import jax
import jax.numpy as jnp
from jax import lax
from jax.sharding import PartitionSpec as P

DH = 128
SEG_LEN = 1024
SEGS = 4


epsilon = 1e-05
masked_score = -1e30
highest = lax.Precision.HIGHEST


def from_behind(value, axis, steps):
    count = lax.axis_size(axis)
    initial, last = (max(0, -steps), min(count, count - steps))
    return lax.ppermute(value, axis, [(source, source + steps) for source in range(initial, last)])


def elu_plus(values):
    return jnp.where(values > 0, values + 1.0, jnp.exp(jnp.minimum(values, 0.0)))


def elu_slope(values):
    return jnp.where(values > 0, 1.0, jnp.exp(jnp.minimum(values, 0.0)))


def inverse_rms(values):
    return lax.rsqrt(jnp.mean(values * values, axis=-1, keepdims=True) + epsilon)


def norm_backward(values, inverse, gain_vec, grad_out):
    normal = values * inverse
    scaled = gain_vec * grad_out
    grad_in = inverse * (scaled - normal * jnp.mean(scaled * normal, axis=-1, keepdims=True))
    return (grad_in, jnp.sum(grad_out * normal, axis=0))


def attention_scores(query_block, key_rows, block_start, valid_len, score_scale):
    row_count = query_block.shape[0]
    key_total = key_rows.shape[0]
    scores = (
        jnp.einsum("qhd,khd->hqk", query_block, key_rows, preferred_element_type=jnp.float32)
        * score_scale
    )
    row_pos = block_start + lax.iota(jnp.int32, row_count)
    col_pos = lax.iota(jnp.int32, key_total)
    allowed = (row_pos[:, None] >= col_pos[None, :]) & (col_pos[None, :] < valid_len)
    return jnp.where(allowed[None], scores, masked_score)


def per_device(
    tokens,
    cotangent,
    gain_attn,
    gain_mlp,
    w_query,
    w_key,
    w_value,
    w_out,
    w_gate,
    w_up,
    w_down,
    mem_gate,
    lengths,
):
    seg_index = lax.axis_index("seg")
    position = seg_index % SEGS
    sequence = seg_index // SEGS
    seq_length = jnp.sum(jnp.where(lax.iota(jnp.int32, lengths.shape[0]) == sequence, lengths, 0))
    valid_len = jnp.where(position == SEGS - 1, seq_length, SEG_LEN)
    valid_rows = (lax.iota(jnp.int32, SEG_LEN) < valid_len).astype(jnp.float32)[:, None, None]
    local_heads = mem_gate.shape[0]
    head_cols = w_query.shape[1]
    score_scale = DH ** (-0.5)
    block_rows = min(512, SEG_LEN)
    block_count = SEG_LEN // block_rows
    token_vals = tokens.astype(jnp.float32)
    inverse_attn = inverse_rms(token_vals)
    normed_attn = (token_vals * inverse_attn * gain_attn).astype(jnp.bfloat16)
    gathered_attn = lax.all_gather(normed_attn, "head", axis=0, tiled=True)

    def project(weight):
        product = jnp.dot(gathered_attn, weight, preferred_element_type=jnp.float32)
        return product.astype(jnp.bfloat16).reshape(SEG_LEN, local_heads, DH)

    query_rows = project(w_query)
    key_rows = project(w_key)
    value_rows = project(w_value)
    query_vals = query_rows.astype(jnp.float32)
    key_vals = key_rows.astype(jnp.float32)
    value_vals = value_rows.astype(jnp.float32)
    query_feat = elu_plus(query_vals)
    key_feat = elu_plus(key_vals) * valid_rows
    update_memory = jnp.einsum("lhd,lhe->hde", key_feat, value_vals, precision=highest)
    update_normal = jnp.sum(key_feat, axis=0)
    memory_prev = jnp.zeros_like(update_memory)
    normal_prev = jnp.zeros_like(update_normal)
    for distance in range(1, SEGS):
        moved = from_behind((update_memory, update_normal), "seg", distance)
        take = (position >= distance).astype(jnp.float32)
        memory_prev = memory_prev + take * moved[0]
        normal_prev = normal_prev + take * moved[1]
    memory_after = ((memory_prev + update_memory) * SEG_LEN ** (-0.5))[None]
    normal_after = ((normal_prev + update_normal) / SEG_LEN)[None]
    numerator = jnp.einsum("lhd,hde->lhe", query_feat, memory_prev, precision=highest)
    denominator = jnp.einsum("lhd,hd->lh", query_feat, normal_prev, precision=highest) + 1.0
    retrieved = numerator / denominator[..., None]

    def block_forward(block_index):
        block_start = block_index * block_rows
        query_block = lax.dynamic_slice_in_dim(query_rows, block_start, block_rows, 0)
        scores = attention_scores(query_block, key_rows, block_start, valid_len, score_scale)
        row_max = jnp.max(scores, axis=-1, keepdims=True)
        weights = jnp.exp(scores - row_max)
        row_total = jnp.sum(weights, axis=-1, keepdims=True)
        soft_weights = (weights / row_total).astype(jnp.bfloat16)
        local_block = jnp.einsum(
            "hqk,khd->qhd", soft_weights, value_rows, preferred_element_type=jnp.float32
        )
        return (local_block, (row_max + jnp.log(row_total))[..., 0])

    local_blocks, log_totals = lax.map(block_forward, lax.iota(jnp.int32, block_count))
    local_attn = local_blocks.reshape(SEG_LEN, local_heads, DH)
    mix_sig = jax.nn.sigmoid(mem_gate)
    mix_weight = mix_sig[None, :, None]
    mixed_attn = (
        (mix_weight * retrieved + (1.0 - mix_weight) * local_attn)
        .astype(jnp.bfloat16)
        .reshape(SEG_LEN, head_cols)
    )
    rows = mixed_attn
    attn_out = lax.psum_scatter(
        jnp.dot(rows, w_out, preferred_element_type=jnp.float32),
        "head",
        scatter_dimension=0,
        tiled=True,
    )
    hidden_res = token_vals + attn_out
    inverse_mlp = inverse_rms(hidden_res)
    normed_mlp = (hidden_res * inverse_mlp * gain_mlp).astype(jnp.bfloat16)
    gathered_mlp = lax.all_gather(normed_mlp, "head", axis=0, tiled=True)
    gate_pre = jnp.dot(gathered_mlp, w_gate, preferred_element_type=jnp.float32)
    up_proj = jnp.dot(gathered_mlp, w_up, preferred_element_type=jnp.float32)
    gate_sig = jax.nn.sigmoid(gate_pre)
    silu_gate = gate_pre * gate_sig
    activation = (silu_gate * up_proj).astype(jnp.bfloat16)
    rows = activation
    mlp_out = lax.psum_scatter(
        jnp.dot(rows, w_down, preferred_element_type=jnp.float32),
        "head",
        scatter_dimension=0,
        tiled=True,
    )
    output = (hidden_res + mlp_out).astype(jnp.bfloat16)
    gathered_grad = lax.all_gather(cotangent, "head", axis=0, tiled=True)
    grad_down = jnp.einsum(
        "lf,ld->fd", activation, gathered_grad, preferred_element_type=jnp.float32
    )
    d_act = jnp.einsum("ld,fd->lf", gathered_grad, w_down, preferred_element_type=jnp.float32)
    d_gate = (d_act * up_proj * gate_sig * (1.0 + gate_pre * (1.0 - gate_sig))).astype(jnp.bfloat16)
    d_up = (d_act * silu_gate).astype(jnp.bfloat16)
    grad_gate = jnp.einsum("ld,lf->df", gathered_mlp, d_gate, preferred_element_type=jnp.float32)
    grad_up = jnp.einsum("ld,lf->df", gathered_mlp, d_up, preferred_element_type=jnp.float32)
    d_normed_mlp = lax.psum_scatter(
        jnp.einsum("lf,df->ld", d_gate, w_gate, preferred_element_type=jnp.float32)
        + jnp.einsum("lf,df->ld", d_up, w_up, preferred_element_type=jnp.float32),
        "head",
        scatter_dimension=0,
        tiled=True,
    )
    grad_in_mlp, gain_mlp_part = norm_backward(hidden_res, inverse_mlp, gain_mlp, d_normed_mlp)
    d_hidden = cotangent.astype(jnp.float32) + grad_in_mlp
    gathered_hidden = lax.all_gather(d_hidden.astype(jnp.bfloat16), "head", axis=0, tiled=True)
    grad_out = jnp.einsum(
        "lc,ld->cd", mixed_attn, gathered_hidden, preferred_element_type=jnp.float32
    )
    d_mixed = jnp.einsum("ld,cd->lc", gathered_hidden, w_out, preferred_element_type=jnp.float32)
    d_mixed = d_mixed.reshape(SEG_LEN, local_heads, DH)
    grad_mem_gate = (
        mix_sig * (1.0 - mix_sig) * jnp.sum(d_mixed * (retrieved - local_attn), axis=(0, 2))
    )
    d_local = ((1.0 - mix_weight) * d_mixed).astype(jnp.bfloat16)
    d_retrieved = mix_weight * d_mixed
    d_numerator = d_retrieved / denominator[..., None]
    d_denominator = -jnp.sum(d_retrieved * retrieved, axis=-1) / denominator
    d_query_feat = (
        jnp.einsum("lhe,hde->lhd", d_numerator, memory_prev, precision=highest)
        + d_denominator[..., None] * normal_prev[None]
    )
    d_memory_prev = jnp.einsum("lhd,lhe->hde", query_feat, d_numerator, precision=highest)
    d_normal_prev = jnp.einsum("lh,lhd->hd", d_denominator, query_feat, precision=highest)
    d_update_memory = jnp.zeros_like(d_memory_prev)
    d_update_normal = jnp.zeros_like(d_normal_prev)
    for distance in range(1, SEGS):
        moved_back = (
            from_behind(d_memory_prev.astype(jnp.bfloat16), "seg", -distance).astype(
                d_memory_prev.dtype
            ),
            from_behind(d_normal_prev.astype(jnp.bfloat16), "seg", -distance).astype(
                d_normal_prev.dtype
            ),
        )
        take_back = (position + distance <= SEGS - 1).astype(jnp.float32)
        d_update_memory = d_update_memory + take_back * moved_back[0]
        d_update_normal = d_update_normal + take_back * moved_back[1]
    d_key_feat = (
        jnp.einsum("lhe,hde->lhd", value_vals, d_update_memory, precision=highest)
        + d_update_normal[None]
    ) * valid_rows
    value_memory = jnp.einsum("lhd,hde->lhe", key_feat, d_update_memory, precision=highest)

    def block_backward(carried, inputs):
        key_grad, value_grad = carried
        block_index, log_block = inputs
        block_start = block_index * block_rows
        query_block = lax.dynamic_slice_in_dim(query_rows, block_start, block_rows, 0)
        dlocal_block = lax.dynamic_slice_in_dim(d_local, block_start, block_rows, 0)
        scores = attention_scores(query_block, key_rows, block_start, valid_len, score_scale)
        probs_full = jnp.exp(scores - log_block[..., None])
        d_probs = jnp.einsum(
            "qhd,khd->hqk", dlocal_block, value_rows, preferred_element_type=jnp.float32
        )
        row_dot = jnp.sum(probs_full * d_probs, axis=-1, keepdims=True)
        d_scores = (probs_full * (d_probs - row_dot) * score_scale).astype(jnp.bfloat16)
        soft_weights = probs_full.astype(jnp.bfloat16)
        query_grad = jnp.einsum(
            "hqk,khd->qhd", d_scores, key_rows, preferred_element_type=jnp.float32
        )
        key_grad = key_grad + jnp.einsum(
            "hqk,qhd->khd", d_scores, query_block, preferred_element_type=jnp.float32
        )
        value_grad = value_grad + jnp.einsum(
            "hqk,qhd->khd", soft_weights, dlocal_block, preferred_element_type=jnp.float32
        )
        return ((key_grad, value_grad), query_grad)

    zero_state = jnp.zeros((SEG_LEN, local_heads, DH), jnp.float32)
    (key_dot, value_dot), query_blocks = lax.scan(
        block_backward, (zero_state, zero_state), (lax.iota(jnp.int32, block_count), log_totals)
    )
    query_dot = query_blocks.reshape(SEG_LEN, local_heads, DH)
    d_queries = (
        (query_dot + d_query_feat * elu_slope(query_vals))
        .astype(jnp.bfloat16)
        .reshape(SEG_LEN, head_cols)
    )
    d_keys = (
        (key_dot + d_key_feat * elu_slope(key_vals))
        .astype(jnp.bfloat16)
        .reshape(SEG_LEN, head_cols)
    )
    d_values = (value_dot + value_memory).astype(jnp.bfloat16).reshape(SEG_LEN, head_cols)
    grad_query = jnp.einsum(
        "ld,lc->dc", gathered_attn, d_queries, preferred_element_type=jnp.float32
    )
    grad_key = jnp.einsum("ld,lc->dc", gathered_attn, d_keys, preferred_element_type=jnp.float32)
    grad_value = jnp.einsum(
        "ld,lc->dc", gathered_attn, d_values, preferred_element_type=jnp.float32
    )
    d_normed_attn = lax.psum_scatter(
        jnp.einsum("lc,dc->ld", d_queries, w_query, preferred_element_type=jnp.float32)
        + jnp.einsum("lc,dc->ld", d_keys, w_key, preferred_element_type=jnp.float32)
        + jnp.einsum("lc,dc->ld", d_values, w_value, preferred_element_type=jnp.float32),
        "head",
        scatter_dimension=0,
        tiled=True,
    )
    grad_in_attn, gain_attn_part = norm_backward(token_vals, inverse_attn, gain_attn, d_normed_attn)
    grad_tokens = (d_hidden + grad_in_attn).astype(jnp.bfloat16)
    gain_totals = lax.psum((gain_attn_part, gain_mlp_part), ("seg", "head"))
    summed = lax.psum(
        (grad_query, grad_key, grad_value, grad_out, grad_mem_gate, grad_gate, grad_up, grad_down),
        "seg",
    )
    return (
        output,
        grad_tokens,
        memory_after,
        normal_after,
        gain_totals[0],
        gain_totals[1],
        summed[0],
        summed[1],
        summed[2],
        summed[3],
        summed[5],
        summed[6],
        summed[7],
        summed[4],
    )


def solution(mesh):
    return jax.shard_map(
        per_device,
        mesh=mesh,
        in_specs=(
            P(("seg", "head"), None),
            P(("seg", "head"), None),
            P(),
            P(),
            P(None, "head"),
            P(None, "head"),
            P(None, "head"),
            P("head", None),
            P(None, "head"),
            P(None, "head"),
            P("head", None),
            P("head"),
            P(),
        ),
        out_specs=(
            P(("seg", "head"), None),
            P(("seg", "head"), None),
            P("seg", "head", None, None),
            P("seg", "head", None),
            P(),
            P(),
            P(None, "head"),
            P(None, "head"),
            P(None, "head"),
            P("head", None),
            P(None, "head"),
            P(None, "head"),
            P("head", None),
            P("head"),
        ),
        check_vma=False,
    )
```

profile of v0, /device:TPU:0, one launch (start us, length us, event | category | flops | bytes accessed | tf_op | source)
XLA Modules:
  0.0 2164.3 jit_solution(5555047049759841362)
XLA Ops:
  12.9 82.1 %all-gather.5.cloned.1.call-done = bf16[1024,2048]{1,0:T(8,128)(2,1)} async-done(((bf16[256,2048]{1,0:T(8,128)(2,1)}), bf16[1024,2048]{1,0:T(8,128)(2,1)}) %all-gather.5.cloned.1.call-update) | async-done | bytes 4194320 | tf_op jit(solution)/shard_map/all_gather | solution.py:83
  95.1 5.1 fusion.101
  103.0 3.4 collective-permute-start.4
  108.8 3.5 convolution_convert_fusion.1
  117.3 3.4 collective-permute-start.2
  124.8 6.2 convolution_convert_fusion
  135.1 67.8 %while.27 = (s32[]{:T(128)}, f32[2,512,4,128]{1,0,3,2:T(2,128)}, f32[2,4,512]{2,1,0:T(4,128)S(1)}, s32[2]{0:T(128)S(1)}, s32[]{:T(128)}, /*index=5*/bf16[1024,4,...) while((s32[]{:T(128)}, f32[2,512,4,128]{1,0,3,2:T(2,128)}, ...), condition=%wide.region_6.7_spmd, body=%wide.region_3.6_spmd.sunk | while | flops 1099955712 | bytes 39393512 | solution.py:125
  142.0 3.7 fusion.243
  145.7 3.6 copy.81
  149.3 19.6 dynamic_update_slice.17
  175.9 3.7 fusion.243
  179.6 3.6 copy.81
  183.2 19.6 dynamic_update_slice.17
  202.9 4.0 reshape.216
  209.4 2.9 fusion.114
  214.2 4.0 add_convert_fusion.1
  219.1 5.8 fusion.151
  225.0 142.7 %reduce-scatter.5.cloned.1.call-done = f32[256,2048]{1,0:T(8,128)} async-done(((f32[1024,2048]{1,0:T(8,128)}), f32[256,2048]{1,0:T(8,128)}) %reduce-scatter.5.cloned.1.call-update) | async-done | bytes 2097168 | tf_op jit(solution)/shard_map/reduce_scatter | solution.py:135
  373.5 80.6 %all-gather.7.cloned.1.call-done = bf16[1024,2048]{1,0:T(8,128)(2,1)} async-done(((bf16[256,2048]{1,0:T(8,128)(2,1)}), bf16[1024,2048]{1,0:T(8,128)(2,1)}) %all-gather.7.cloned.1.call-update) | async-done | bytes 4194320 | tf_op jit(solution)/shard_map/all_gather | solution.py:144
  454.1 15.5 fusion.153
  469.6 13.3 fusion.152
  482.9 52.0 %all-gather.9.cloned.1.call-done = bf16[1024,2048]{1,0:T(8,128)(2,1)} async-done(((bf16[256,2048]{1,0:T(8,128)(2,1)}), bf16[1024,2048]{1,0:T(8,128)(2,1)}) %all-gather.9.cloned.1.call-update) | async-done | bytes 4194320 | tf_op jit(solution)/shard_map/all_gather | solution.py:158
  534.9 21.8 %multiply_convert_fusion.1 = (bf16[1024,2048]{1,0:T(8,128)(2,1)}, bf16[1024,2048]{1,0:T(8,128)(2,1)}, bf16[1024,2048]{1,0:T(8,128)(2,1)}) fusion(f32[1024,2048]{1,0:T(8,128)} %fusion.152, f32[1024,2048]{1,0:T(8,128)} %fusion.153, bf16[1024,2048]{1,0:T(8,128)(2,1)} %all-gather.9.cloned.1.call-done, bf16[2048,2048]{1,0:T(8,128)(2,1)} %param.27), kind=kOutput, calls=%fused_computation.65 | convolution fusion | flops 8621391872 | bytes 41943040 | tf_op jit(solution)/shard_map/ld,fd->lf/dot_general | solution.py:162
  556.7 12.9 fusion.155
  569.6 13.5 convolution_add_fusion
  583.2 143.1 %reduce-scatter.9.cloned.1.call-done = f32[256,2048]{1,0:T(8,128)} async-done(((f32[1024,2048]{1,0:T(8,128)}), f32[256,2048]{1,0:T(8,128)}) %reduce-scatter.9.cloned.1.call-update) | async-done | bytes 2097168 | tf_op jit(solution)/shard_map/reduce_scatter | solution.py:167
  726.3 3.5 multiply_reduce_fusion.2
  733.1 81.4 %all-gather.11.cloned.1.call-done = bf16[1024,2048]{1,0:T(8,128)(2,1)} async-done(((bf16[256,2048]{1,0:T(8,128)(2,1)}), bf16[1024,2048]{1,0:T(8,128)(2,1)}) %all-gather.11.cloned.1.call-update) | async-done | bytes 4194320 | tf_op jit(solution)/shard_map/all_gather | solution.py:176
  814.4 5.3 fusion.156
  819.8 3.3 fusion.117
  836.3 169.5 %while.28 = (s32[]{:T(128)}, f32[1024,4,128]{0,2,1:T(8,128)}, f32[1024,4,128]{0,2,1:T(8,128)}, f32[2,512,4,128]{1,0,3,2:T(2,128)}, s32[2]{0:T(128)S(1)}, /*index...) while((s32[]{:T(128)}, f32[1024,4,128]{0,2,1:T(8,128)}, ...), condition=%wide.region_14.15_spmd.clone, body=%wide.region_12.14_spmd.clone.sunk | while | flops 2742033920 | bytes 157866416 | solution.py:241
  845.8 4.7 fusion.254
  850.5 23.2 %fusion.257 = f32[1,512,4,128]{3,1,2,0:T(8,128)} fusion(bf16[1024,4,128]{2,0,1:T(8,128)(2,1)S(1)} %get-tuple-element.442, f32[4,512,1024]{2,1,0:T(8,128)} %fusion.254, f32[4,512,1024]{2,1,0:T(8,128)} %copy-done.1, f32[4,512]{1,0:T(4,128)S(1)} %dynamic-slice_bitcast_fusion.2, pred[512,1024]{1,0:T(8,128)(4,1)} %copy-done.8), kind=kOutput, calls=%fused_computation.42.clone.1 | convolution fusion | flops 559942656 | bytes 19406848 | tf_op jit(solution)/shard_map/while/body/eval_jaxpr/hqk,khd->qhd/dot_general | solution.py:229
  873.6 24.4 %bitcast_add_fusion.7 = f32[1024,4,128]{0,2,1:T(8,128)} fusion(f32[1024,4,128]{0,2,1:T(8,128)} %get-tuple-element.421, f32[4,512,1024]{2,1,0:T(8,128)} %fusion.254, f32[4,512,1024]{2,1,0:T(8,128)} %copy-done.1, f32[4,512]{1,0:T(4,128)S(1)} %dynamic-slice_bitcast_fusion.2, pred[512,1024]{1,0:T(8,128)(4,1)} %copy-done.8, pred[]{:T(512)S(6)} %compare.6, ...), kind=kOutput, calls=%fused_computation.39.clone.1 | convolution fusion | flops 560991232 | bytes 39337988 | tf_op jit(solution)/shard_map/while/body/eval_jaxpr/hqk,qhd->khd/dot_general | solution.py:232
  898.1 3.6 copy.82
  901.7 19.6 dynamic_update_slice.18
  925.5 2.9 bitcast_add_fusion.8
  930.2 4.7 fusion.254
  934.9 23.2 %fusion.257 = f32[1,512,4,128]{3,1,2,0:T(8,128)} fusion(bf16[1024,4,128]{2,0,1:T(8,128)(2,1)S(1)} %get-tuple-element.442, f32[4,512,1024]{2,1,0:T(8,128)} %fusion.254, f32[4,512,1024]{2,1,0:T(8,128)} %copy-done.1, f32[4,512]{1,0:T(4,128)S(1)} %dynamic-slice_bitcast_fusion.2, pred[512,1024]{1,0:T(8,128)(4,1)} %copy-done.8), kind=kOutput, calls=%fused_computation.42.clone.1 | convolution fusion | flops 559942656 | bytes 19406848 | tf_op jit(solution)/shard_map/while/body/eval_jaxpr/hqk,khd->qhd/dot_general | solution.py:229
  958.1 24.4 %bitcast_add_fusion.7 = f32[1024,4,128]{0,2,1:T(8,128)} fusion(f32[1024,4,128]{0,2,1:T(8,128)} %get-tuple-element.421, f32[4,512,1024]{2,1,0:T(8,128)} %fusion.254, f32[4,512,1024]{2,1,0:T(8,128)} %copy-done.1, f32[4,512]{1,0:T(4,128)S(1)} %dynamic-slice_bitcast_fusion.2, pred[512,1024]{1,0:T(8,128)(4,1)} %copy-done.8, pred[]{:T(512)S(6)} %compare.6, ...), kind=kOutput, calls=%fused_computation.39.clone.1 | convolution fusion | flops 560991232 | bytes 39337988 | tf_op jit(solution)/shard_map/while/body/eval_jaxpr/hqk,qhd->khd/dot_general | solution.py:232
  982.5 3.6 copy.82
  986.1 19.6 dynamic_update_slice.18
  1005.9 4.1 reshape.219
  1010.0 5.0 fusion.98
  1026.7 3.7 fusion.103
  1030.4 5.8 add_add_fusion
  1036.3 14.4 fusion.154
  1051.2 15.5 fusion.165
  1066.8 11.8 fusion.164
  1078.6 11.9 fusion.163
  1090.5 4.4 fusion.162
  1094.9 4.5 fusion.159
  1099.4 4.5 fusion.160
  1103.9 4.5 fusion.161
  1109.1 20.6 psum.79
  1129.7 56.7 %reduce-scatter.11.cloned.1.call-done = f32[256,2048]{1,0:T(8,128)} async-done(((f32[1024,2048]{1,0:T(8,128)}), f32[256,2048]{1,0:T(8,128)}) %reduce-scatter.11.cloned.1.call-update) | async-done | bytes 2097168 | tf_op jit(solution)/shard_map/reduce_scatter | solution.py:263
  1188.7 46.5 %all-reduce = (f32[2048]{0:T(1024)}, f32[2048]{0:T(1024)}) all-reduce(f32[2048]{0:T(1024)S(1)} %get-tuple-element.178, f32[2048]{0:T(1024)S(1)} %copy-done.30), channel_id=1, replica_groups=mesh['seg'=8,'head'=4] {'seg','head'}, use_global_device_ids=true, to_apply=%region_19.20 | all-reduce | flops 4096 | bytes 32768 | tf_op jit(solution)/shard_map/psum | solution.py:273
  1235.3 99.7 %reduce-scatter.7.cloned.1.call-done = f32[256,2048]{1,0:T(8,128)} async-done(((f32[1024,2048]{1,0:T(8,128)}), f32[256,2048]{1,0:T(8,128)}) %reduce-scatter.7.cloned.1.call-update) | async-done | bytes 2097168 | tf_op jit(solution)/shard_map/reduce_scatter | solution.py:151
  1335.0 6.2 fusion.83
  1341.2 768.8 %all-reduce.4.cloned.1.call-done = (f32[2048,512]{1,0:T(8,128)}, f32[2048,512]{1,0:T(8,128)}, f32[2048,512]{1,0:T(8,128)}, f32[512,2048]{1,0:T(8,128)}, f32[2048...) async-done(((f32[2048,512]{1,0:T(8,128)}, f32[2048,512]{1,0:T(8,128)}, f32[2048,512]{1,0:T(8,128)}, f32[512,2048]{1,0:T(8,128)}, f32[2048,2048]{1,0:T(8,128)}, ...) | async-done | bytes 67108880 | tf_op jit(solution)/shard_map/psum | solution.py:274
  2110.0 4.8 copy.114
  2124.4 14.0 copy.118
  2140.5 8.5 copy.119
  2151.4 6.2 copy.120
  (266 shorter events, 105.7 us)
Async XLA Ops:
  7.2 87.9 %copy-start = (bf16[2048,512]{1,0:T(8,128)(2,1)S(1)}, bf16[2048,512]{1,0:T(8,128)(2,1)}, u32[]{:S(2)}) copy-start(bf16[2048,512]{1,0:T(8,128)(2,1)} %param.22) | copy-start | bytes 6291460
  7.2 5.7 copy-start.50
  7.2 87.9 %all-gather.5.cloned.1.call-start = ((), (), s32[]{:S(2)}) async-start(), calls=%async_computation.4 | async-start | bytes 5242880 | tf_op jit(solution)/shard_map/all_gather | solution.py:83
  11.5 356.2 %reduce-scatter.5.cloned.1.call-start = ((), (), s32[]{:S(2)}) async-start(), calls=%async_computation.5 | async-start | bytes 10485760 | tf_op jit(solution)/shard_map/reduce_scatter | solution.py:135
  12.9 101.6 %copy-start.37 = (f32[1024]{0:T(1024)}, f32[1024]{0:T(1024)S(1)}, u32[]{:S(2)}) copy-start(f32[1024]{0:T(1024)S(1)} %fusion.136) | copy-start | bytes 12292
  95.1 13.7 copy-start.16
  95.1 13.7 copy-start.42
  100.2 14.3 copy-start.19
  100.2 106.7 %collective-permute-start.5 = (f32[4,128]{1,0:T(4,128)S(1)}, f32[4,128]{1,0:T(4,128)S(1)}, u32[]{:S(2)}, u32[]{:S(2)}) collective-permute-start(f32[4,128]{1,0:T(4,128)S(1)} %bitcast.168), channel_id=1, source_target_pairs={{0,12},{4,16},{8,20},{12,24},{16,28},{1,13},{5,17},{9,21},{13,25},... | collective-permute-start | bytes 6152 | tf_op jit(solution)/shard_map/ppermute | solution.py:19
  103.0 105.8 %collective-permute-start.4 = (f32[4,128]{1,0:T(4,128)S(1)}, f32[4,128]{1,0:T(4,128)S(1)}, u32[]{:S(2)}, u32[]{:S(2)}) collective-permute-start(f32[4,128]{1,0:T(4,128)S(1)} %bitcast.169), channel_id=1, source_target_pairs={{0,8},{4,12},{8,16},{12,20},{16,24},{20,28},{1,9},{5,13},{9,17},{1... | collective-permute-start | bytes 6152 | tf_op jit(solution)/shard_map/ppermute | solution.py:19
  106.4 102.4 %collective-permute-start.3 = (f32[4,128]{1,0:T(4,128)S(1)}, f32[4,128]{1,0:T(4,128)S(1)}, u32[]{:S(2)}, u32[]{:S(2)}) collective-permute-start(f32[4,128]{1,0:T(4,128)S(1)} %bitcast.170), channel_id=1, source_target_pairs={{0,4},{4,8},{8,12},{12,16},{16,20},{20,24},{24,28},{1,5},{5,9},{9,... | collective-permute-start | bytes 6152 | tf_op jit(solution)/shard_map/ppermute | solution.py:19
  117.3 95.0 %collective-permute-start.2 = (f32[4,128,128]{2,1,0:T(8,128)S(1)}, f32[4,128,128]{2,1,0:T(8,128)}, u32[]{:S(2)}, u32[]{:S(2)}) collective-permute-start(f32[4,128,128]{2,1,0:T(8,128)S(1)} %fusion.106), channel_id=1, source_target_pairs={{0,12},{4,16},{8,20},{12,24},{16,28},{1,13},{5,17},{9,21},{13,25},... | collective-permute-start | bytes 786440 | tf_op jit(solution)/shard_map/ppermute | solution.py:19
  120.7 91.6 %collective-permute-start.1 = (f32[4,128,128]{2,1,0:T(8,128)S(1)}, f32[4,128,128]{2,1,0:T(8,128)}, u32[]{:S(2)}, u32[]{:S(2)}) collective-permute-start(f32[4,128,128]{2,1,0:T(8,128)S(1)} %fusion.106), channel_id=1, source_target_pairs={{0,8},{4,12},{8,16},{12,20},{16,24},{20,28},{1,9},{5,13},{9,17},{1... | collective-permute-start | bytes 786440 | tf_op jit(solution)/shard_map/ppermute | solution.py:19
  206.9 5.5 collective-permute-start
  209.4 4.8 copy-start.39
  209.4 4.8 copy-start.11
  209.4 4.8 copy-start.22
  214.2 5.0 copy-start.47
  225.0 146.3 %copy-start.27 = (f32[2048]{0:T(1024)S(1)}, f32[2048]{0:T(1024)}, u32[]{:S(2)}) copy-start(f32[2048]{0:T(1024)} %param.20) | copy-start | bytes 24580
  225.0 229.2 %all-gather.7.cloned.1.call-start = ((), (), s32[]{:S(2)}) async-start(), calls=%async_computation.6 | async-start | bytes 5242880 | tf_op jit(solution)/shard_map/all_gather | solution.py:144
  369.9 359.9 %copy-start.31 = (f32[256]{0:T(256)}, f32[256]{0:T(256)S(1)}, u32[]{:S(2)}) copy-start(f32[256]{0:T(256)S(1)} %add_rsqrt_fusion) | copy-start | bytes 3076
  372.5 162.4 %all-gather.9.cloned.1.call-start = ((), (), s32[]{:S(2)}) async-start(), calls=%async_computation.8 | async-start | bytes 5242880 | tf_op jit(solution)/shard_map/all_gather | solution.py:158
  373.1 353.2 %reduce-scatter.9.cloned.1.call-start = ((), (), s32[]{:S(2)}) async-start(), calls=%async_computation.9 | async-start | bytes 10485760 | tf_op jit(solution)/shard_map/reduce_scatter | solution.py:167
  454.1 15.5 copy-start.44
  556.7 12.9 copy-start.61
  583.2 231.3 %all-gather.11.cloned.1.call-start = ((), (), s32[]{:S(2)}) async-start(), calls=%async_computation.10 | async-start | bytes 5242880 | tf_op jit(solution)/shard_map/all_gather | solution.py:176
  732.8 453.7 %reduce-scatter.11.cloned.1.call-start = ((), (), s32[]{:S(2)}) async-start(), calls=%async_computation.11 | async-start | bytes 10485760 | tf_op jit(solution)/shard_map/reduce_scatter | solution.py:263
  814.4 5.3 copy-start.23
  827.9 189.6 %collective-permute-start.11 = (bf16[4,128]{1,0:T(4,128)(2,1)S(1)}, bf16[4,128]{1,0:T(4,128)(2,1)S(1)}, u32[]{:S(2)}, u32[]{:S(2)}) collective-permute-start(bf16[4,128]{1,0:T(4,128)(2,1)S(1)} %convert_element_type.155), channel_id=1, source_target_pairs={{12,0},{16,4},{20,8},{24,12},{28,16},{13,1},{17,5},{21,9},{25,13},... | collective-permute-start | bytes 3080 | tf_op jit(solution)/shard_map/ppermute | solution.py:19
  829.2 189.6 %collective-permute-start.10 = (bf16[4,128]{1,0:T(4,128)(2,1)S(1)}, bf16[4,128]{1,0:T(4,128)(2,1)S(1)}, u32[]{:S(2)}, u32[]{:S(2)}) collective-permute-start(bf16[4,128]{1,0:T(4,128)(2,1)S(1)} %convert_element_type.155), channel_id=1, source_target_pairs={{8,0},{12,4},{16,8},{20,12},{24,16},{28,20},{9,1},{13,5},{17,9},{2... | collective-permute-start | bytes 3080 | tf_op jit(solution)/shard_map/ppermute | solution.py:19
  830.5 188.3 %collective-permute-start.9 = (bf16[4,128]{1,0:T(4,128)(2,1)S(1)}, bf16[4,128]{1,0:T(4,128)(2,1)S(1)}, u32[]{:S(2)}, u32[]{:S(2)}) collective-permute-start(bf16[4,128]{1,0:T(4,128)(2,1)S(1)} %convert_element_type.155), channel_id=1, source_target_pairs={{4,0},{8,4},{12,8},{16,12},{20,16},{24,20},{28,24},{5,1},{9,5},{13... | collective-permute-start | bytes 3080 | tf_op jit(solution)/shard_map/ppermute | solution.py:19
  831.8 187.1 %collective-permute-start.8 = (bf16[4,128,128]{2,1,0:T(8,128)(2,1)}, bf16[4,128,128]{2,1,0:T(8,128)(2,1)}, u32[]{:S(2)}, u32[]{:S(2)}) collective-permute-start(bf16[4,128,128]{2,1,0:T(8,128)(2,1)} %fusion.117), channel_id=1, source_target_pairs={{12,0},{16,4},{20,8},{24,12},{28,16},{13,1},{17,5},{21,9},{25,13},... | collective-permute-start | bytes 393224 | tf_op jit(solution)/shard_map/ppermute | solution.py:19
  833.1 185.8 %collective-permute-start.7 = (bf16[4,128,128]{2,1,0:T(8,128)(2,1)}, bf16[4,128,128]{2,1,0:T(8,128)(2,1)}, u32[]{:S(2)}, u32[]{:S(2)}) collective-permute-start(bf16[4,128,128]{2,1,0:T(8,128)(2,1)} %fusion.117), channel_id=1, source_target_pairs={{8,0},{12,4},{16,8},{20,12},{24,16},{28,20},{9,1},{13,5},{17,9},{2... | collective-permute-start | bytes 393224 | tf_op jit(solution)/shard_map/ppermute | solution.py:19
  841.1 4.7 copy-start.5
  925.5 4.7 copy-start.5
  1010.0 5.1 copy-start.48
  1015.1 6.6 copy-start.20
  1015.1 6.5 copy-start.21
  1015.1 6.5 copy-start.38
  1015.1 6.5 copy-start.54
  1017.6 4.1 collective-permute-start.6
  1036.2 298.8 %reduce-scatter.7.cloned.1.call-start = ((), (), s32[]{:S(2)}) async-start(), calls=%async_computation.7 | async-start | bytes 10485760 | tf_op jit(solution)/shard_map/reduce_scatter | solution.py:151
  1050.7 1059.3 %all-reduce.4.cloned.1.call-start = ((), (), s32[]{:S(2)}) async-start(), calls=%async_computation.12 | async-start | bytes 134217728 | tf_op jit(solution)/shard_map/psum | solution.py:274
  1051.2 15.6 copy-start.45
  1051.2 15.6 copy-start.62
  1066.7 11.8 copy-start.63
  1078.5 11.9 copy-start.46
  1078.6 12.0 copy-start.56
  1108.4 78.0 %copy-start.6 = (bf16[256,2048]{1,0:T(8,128)(2,1)S(1)}, bf16[256,2048]{1,0:T(8,128)(2,1)}, u32[]{:S(2)}) copy-start(bf16[256,2048]{1,0:T(8,128)(2,1)} %param.17) | copy-start | bytes 3145732
  1108.4 78.0 %copy-start.29 = (f32[2048]{0:T(1024)S(1)}, f32[2048]{0:T(1024)}, u32[]{:S(2)}) copy-start(f32[2048]{0:T(1024)} %param.19) | copy-start | bytes 24580
  1108.4 78.0 %copy-start.34 = (f32[256]{0:T(256)S(1)}, f32[256]{0:T(256)}, u32[]{:S(2)}) copy-start(f32[256]{0:T(256)} %copy-done.33) | copy-start | bytes 3076
  1108.5 80.2 %copy-start.30 = (f32[2048]{0:T(1024)S(1)}, f32[2048]{0:T(1024)}, u32[]{:S(2)}) copy-start(f32[2048]{0:T(1024)} %get-tuple-element.176) | copy-start | bytes 24580
  1108.5 226.5 %copy-start.28 = (f32[2048]{0:T(1024)S(1)}, f32[2048]{0:T(1024)}, u32[]{:S(2)}) copy-start(f32[2048]{0:T(1024)} %param.20) | copy-start | bytes 24580
  1108.5 226.5 %copy-start.32 = (f32[256]{0:T(256)S(1)}, f32[256]{0:T(256)}, u32[]{:S(2)}) copy-start(f32[256]{0:T(256)} %copy-done.31) | copy-start | bytes 3076
  1108.5 226.5 %copy-start.36 = (f32[256]{0:T(256)S(1)}, f32[256]{0:T(256)}, u32[]{:S(2)}) copy-start(f32[256]{0:T(256)} %copy-done.35) | copy-start | bytes 3076
  2110.0 4.8 copy-start.15
  2122.3 16.2 slice-start.4
  2124.4 14.1 slice-start.5
  2124.4 14.1 slice-start.6
  2124.4 16.0 slice-start.7
  2124.4 24.5 %slice-start = ((s8[16777216]{0:T(1024)(128)(4,1)}), s8[4194304]{0:T(1024)(128)(4,1)S(1)}, s32[]{:S(2)}) async-start(s8[16777216]{0:T(1024)(128)(4,1)} %bitcast.144), calls=%async_computation.13 | async-start | bytes 8388608
  2124.4 24.5 %slice-start.1 = ((s8[16777216]{0:T(1024)(128)(4,1)}), s8[4194304]{0:T(1024)(128)(4,1)S(1)}, s32[]{:S(2)}) async-start(s8[16777216]{0:T(1024)(128)(4,1)} %bitcast.144), calls=%async_computation.14 | async-start | bytes 8388608
  2140.4 9.6 slice-start.2
  2140.5 10.9 slice-start.3
  (36 other events, 109.2 us)
Sparse Core Ops, SparseCore 0:
  11.6 83.4 all-gather.4
  225.1 142.5 reduce-scatter.4
  372.6 81.4 all-gather.6
  455.6 79.2 all-gather.8
  583.3 142.9 reduce-scatter.8
  732.9 81.4 all-gather.10
  1036.4 150.0 reduce-scatter.10
  1188.8 146.1 reduce-scatter.6
  1341.2 768.7 all-reduce.3
where the time goes:
time: 2180 us; the launch traced here: 2160 us
  waiting for transfers between devices  1510 us (69%)
  matrix products  340 us (16%)
  local copies, waits for them, and re-layouts  167 us (8%)
  blocking collectives  67.1 us (3%)
  other arithmetic  34.6 us (2%)
  starting transfers between devices  25.4 us (1%)
    psum x1, waiting for transfers between devices, per_device(): lax.psum((grad_query, grad_key, grad_value, grad_out, grad_mem_gate, grad...  769 us
    reduce_scatter x1, waiting for transfers between devices, per_device(): lax.psum_scatter(jnp.einsum('lf,df->ld', d_gate, w_gate, preferred_elemen...  143 us
    reduce_scatter x1, waiting for transfers between devices, per_device(): lax.psum_scatter(jnp.dot(rows, w_out, preferred_element_type=jnp.float32)...  143 us
    reduce_scatter x1, waiting for transfers between devices, per_device(): lax.psum_scatter(jnp.dot(rows, w_down, preferred_element_type=jnp.float32...  99.7 us
    dynamic_update_slice x8, local copies, waits for them, and re-layouts, per_device(): lax.map(block_forward, lax.iota(jnp.int32, block_count))  92.8 us
    all_gather x1, waiting for transfers between devices, per_device(): gathered_attn = lax.all_gather(normed_attn, 'head', axis=0, tiled=True)  82.1 us
    all_gather x1, waiting for transfers between devices, per_device(): lax.all_gather(d_hidden.astype(jnp.bfloat16), 'head', axis=0, tiled=True)  81.4 us
    all_gather x1, waiting for transfers between devices, per_device(): gathered_mlp = lax.all_gather(normed_mlp, 'head', axis=0, tiled=True)  80.6 us
  transfers between devices with their start and end apart: 21, of which 10 were waited for; matrix products, arithmetic and copies ran while one was open for 18% of the time, Pallas kernels for 0%

commit v1 on v0

v1 whole, which is shorter than its diff:
```python
import functools

import jax
import jax.numpy as jnp
from jax import lax
from jax.experimental import pallas as pl
from jax.experimental.pallas import tpu as pltpu
from jax.sharding import PartitionSpec as P

DH = 128
SEG_LEN = 1024
SEGS = 4
MEM_ROWS = DH + 8
BLOCK = 256

epsilon = 1e-05
masked_score = -1e30
highest = lax.Precision.HIGHEST
F32 = jnp.float32
BF16 = jnp.bfloat16


MESH = pl.DeviceIdType.MESH
LAND_SLOTS = 8
RESULT_SLOTS = 12
SUM_SEMS = 8
SUM_HOP = 2


def bits_of(size):
    return size.bit_length() - 1


def flip(index, power):
    return index + power - 2 * power * lax.rem(index // power, 2)


def sum_engine(arrays, outs, tile, seg_bits, scratch):
    mine, result, send_sem, recv_sem, load_sem, store_sem, *lands = scratch
    seg = lax.axis_index("seg")
    planes = seg_bits - 1
    high, wide = tile
    shapes = [array.shape for array in arrays]
    counts = [(rows // high) * (cols // wide) for rows, cols in shapes]
    starts = [sum(counts[:i]) for i in range(len(counts))]
    total = sum(counts)

    def power(k, level):
        if level == 0:
            return 1
        which = lax.rem(k + level - 1, planes)
        value = 2
        for bit in range(1, planes):
            value = jnp.where(which == bit, 2 << bit, value)
        return value

    def my_bit(k, level):
        return lax.rem(seg // power(k, level), 2)

    def part(k, level, own):
        half = high >> (level + 1)
        bit = my_bit(k, level) if own else 1 - my_bit(k, level)
        return pl.ds(pl.multiple_of(bit * half, half), half)

    def kept(k, levels):
        first = 0
        for level in range(levels):
            first = first + my_bit(k, level) * (high >> (level + 1))
        return pl.ds(pl.multiple_of(first, high >> levels), high >> levels)

    def pick(k, act):
        for i in range(len(arrays)):

            @pl.when((k >= starts[i]) & (k < starts[i] + counts[i]))
            def _(i=i):
                across = shapes[i][1] // wide
                place = k - starts[i]
                row = pl.multiple_of((place // across) * high, high)
                col = pl.multiple_of(lax.rem(place, across) * wide, wide)
                act(i, row, col)

    def halving(k, level, source):
        return pltpu.make_async_remote_copy(
            src_ref=source,
            dst_ref=lands[level].at[lax.rem(k, LAND_SLOTS)],
            send_sem=send_sem.at[level, lax.rem(k, SUM_SEMS)],
            recv_sem=recv_sem.at[level, lax.rem(k, SUM_SEMS)],
            device_id={"seg": flip(seg, power(k, level))},
            device_id_type=MESH,
        )

    def first_source(k, i, row, col, own):
        half = high // 2
        bit = my_bit(k, 0) if own else 1 - my_bit(k, 0)
        return arrays[i].at[pl.ds(pl.multiple_of(row + bit * half, half), half), pl.ds(col, wide)]

    def keep(k, i, row, col):
        slot = lax.rem(k, 4)
        return pltpu.make_async_copy(
            first_source(k, i, row, col, True), mine.at[slot], load_sem.at[slot]
        )

    def level_source(k, level):
        return lands[level - 1].at[lax.rem(k, LAND_SLOTS), part(k, level, False)]

    def doubling(k, level):
        ref = result.at[lax.rem(k, RESULT_SLOTS), kept(k, level + 1)]
        return pltpu.make_async_remote_copy(
            src_ref=ref,
            dst_ref=ref,
            send_sem=send_sem.at[seg_bits + level, lax.rem(k, SUM_SEMS)],
            recv_sem=recv_sem.at[seg_bits + level, lax.rem(k, SUM_SEMS)],
            device_id={"seg": flip(seg, power(k, level))},
            device_id_type=MESH,
        )

    def store(k, i, row, col):
        slot = lax.rem(k, 4)
        return pltpu.make_async_copy(
            result.at[lax.rem(k, RESULT_SLOTS)],
            outs[i].at[pl.ds(row, high), pl.ds(col, wide)],
            store_sem.at[slot],
        )

    def do_first(k):
        def go(i, row, col):
            halving(k, 0, first_source(k, i, row, col, False)).start()
            keep(k, i, row, col).start()

        pick(k, go)

    def arrived(k, level):
        slot = lax.rem(k, LAND_SLOTS)
        if level == 0:
            halving(k, 0, first_source(k, 0, 0, 0, False)).wait()
            keep(k, 0, 0, 0).wait()
            other = mine[lax.rem(k, 4)]
        else:
            halving(k, level, level_source(k, level)).wait()
            other = lands[level - 1][slot, part(k, level, True)]
        return (lands[level][slot].astype(F32) + other.astype(F32)).astype(BF16)

    def do_level(k, level):
        lands[level - 1][lax.rem(k, LAND_SLOTS)] = arrived(k, level - 1)
        halving(k, level, level_source(k, level)).start()

    def do_total(k):
        result[lax.rem(k, RESULT_SLOTS), kept(k, seg_bits)] = arrived(k, seg_bits - 1)
        doubling(k, seg_bits - 1).start()

    def do_spread(k, level):
        doubling(k, level + 1).wait()
        doubling(k, level).start()

    def do_finish(k):
        doubling(k, 0).wait()
        pick(k, lambda i, row, col: store(k, i, row, col).start())

    def do_store(k):
        store(k, 0, 0, 0).wait()

    stages = [(0, do_first), (1, functools.partial(do_level, level=1))]
    when = 1
    for level in range(2, seg_bits):
        when += SUM_HOP
        stages.append((when, functools.partial(do_level, level=level)))
    when += SUM_HOP
    stages.append((when, do_total))
    for level in range(seg_bits - 2, -1, -1):
        when += SUM_HOP
        stages.append((when, functools.partial(do_spread, level=level)))
    stages.append((when + 1, do_finish))
    stages.append((when + 3, do_store))

    def step(t):
        for delay, act in reversed(stages):
            k = t - delay

            @pl.when((k >= 0) & (k < total))
            def _(act=act, k=k):
                act(k)

    return step, total + when + 3


def engine_scratch(tile, seg_bits):
    high, wide = tile
    return [
        pltpu.VMEM((4, high // 2, wide), BF16),
        pltpu.VMEM((RESULT_SLOTS, high, wide), BF16),
        pltpu.SemaphoreType.DMA((2 * seg_bits, SUM_SEMS)),
        pltpu.SemaphoreType.DMA((2 * seg_bits, SUM_SEMS)),
        pltpu.SemaphoreType.DMA((4,)),
        pltpu.SemaphoreType.DMA((4,)),
    ] + [pltpu.VMEM((LAND_SLOTS, high >> (l + 1), wide), BF16) for l in range(seg_bits)]


def greet_seg(seg_bits):
    barrier = pltpu.get_barrier_semaphore()
    seg = lax.axis_index("seg")
    for bit in range(seg_bits):
        pl.semaphore_signal(
            barrier, inc=1, device_id={"seg": flip(seg, 1 << bit)}, device_id_type=MESH
        )


def grad_sum_kernel(count, tile, seg_bits, head_bits, *refs):
    small_in, arrays = refs[0], refs[1 : 1 + count]
    small_out, outs = refs[1 + count], refs[2 + count : 2 + 2 * count]
    small_buf, small_land, small_send, small_recv, *scratch = refs[2 + 2 * count :]
    seg, head = lax.axis_index("seg"), lax.axis_index("head")
    greet_seg(seg_bits)
    barrier = pltpu.get_barrier_semaphore()
    for bit in range(head_bits):
        pl.semaphore_signal(
            barrier, inc=1, device_id={"head": flip(head, 1 << bit)}, device_id_type=MESH
        )
    pl.semaphore_wait(barrier, seg_bits + head_bits)
    rounds = seg_bits + head_bits

    def small_copy(j):
        if j < seg_bits:
            where = {"seg": flip(seg, 1 << j)}
        else:
            where = {"head": flip(head, 1 << (j - seg_bits))}
        return pltpu.make_async_remote_copy(
            src_ref=small_buf.at[j],
            dst_ref=small_land.at[j],
            send_sem=small_send.at[j],
            recv_sem=small_recv.at[j],
            device_id=where,
            device_id_type=MESH,
        )

    engine_step, steps = sum_engine(arrays, outs, tile, seg_bits, scratch)

    def step(t, carry):
        engine_step(t)
        for j in range(rounds + 1):

            @pl.when(t == 3 * j)
            def _(j=j):
                if j == 0:
                    small_buf[0] = small_in[...]
                else:
                    small_copy(j - 1).wait()
                    value = small_buf[j - 1] + small_land[j - 1]
                    if j < rounds:
                        small_buf[j] = value
                    else:
                        small_out[...] = value
                if j < rounds:
                    small_copy(j).start()

        return carry

    lax.fori_loop(0, max(steps, 3 * rounds + 1), step, 0)


def grad_sum(small, arrays, tile, seg_size, head_size, cid):
    seg_bits, head_bits = bits_of(seg_size), bits_of(head_size)
    rounds = seg_bits + head_bits
    count = len(arrays)
    moved = sum(rows * cols for rows, cols in (array.shape for array in arrays))
    any_, vmem = pl.BlockSpec(memory_space=pltpu.HBM), pl.BlockSpec(memory_space=pltpu.VMEM)
    return pl.pallas_call(
        functools.partial(grad_sum_kernel, count, tile, seg_bits, head_bits),
        in_specs=[vmem] + [any_] * count,
        out_specs=[vmem] + [any_] * count,
        out_shape=[jax.ShapeDtypeStruct(small.shape, F32)]
        + [jax.ShapeDtypeStruct(array.shape, BF16) for array in arrays],
        scratch_shapes=[
            pltpu.VMEM((rounds, *small.shape), F32),
            pltpu.VMEM((rounds, *small.shape), F32),
            pltpu.SemaphoreType.DMA((rounds,)),
            pltpu.SemaphoreType.DMA((rounds,)),
        ]
        + engine_scratch(tile, seg_bits),
        cost_estimate=pl.CostEstimate(flops=0, bytes_accessed=moved * 60, transcendentals=0),
        compiler_params=pltpu.CompilerParams(
            collective_id=cid, has_side_effects=True, vmem_limit_bytes=48 * 2**20
        ),
    )(small, *arrays)


ROWS = 32
HOP = 2
SEND_SLOTS = 4
BLOCK_ROWS = 256
LINE_REFS = 8


def line_exchange(own, finish, before, scratch, extra=None, extra_steps=0):
    up_land, down_land, up_send, down_send, up_recv_sem, down_recv_sem, up_send_sem, down_send_sem = scratch
    size = lax.axis_size("head")
    place = lax.axis_index("head")
    slots = up_land.shape[0]
    chunks = own.shape[0] // ROWS
    last = size - 1

    def up_copy(k):
        return pltpu.make_async_remote_copy(
            src_ref=up_send.at[lax.rem(k, SEND_SLOTS)],
            dst_ref=up_land.at[lax.rem(k, slots)],
            send_sem=up_send_sem.at[lax.rem(k, SEND_SLOTS)],
            recv_sem=up_recv_sem.at[lax.rem(k, slots)],
            device_id={"head": lax.rem(place + 1, size)},
            device_id_type=MESH,
        )

    def down_copy(k):
        return pltpu.make_async_remote_copy(
            src_ref=down_send.at[lax.rem(k, SEND_SLOTS)],
            dst_ref=down_land.at[lax.rem(k, slots)],
            send_sem=down_send_sem.at[lax.rem(k, SEND_SLOTS)],
            recv_sem=down_recv_sem.at[lax.rem(k, slots)],
            device_id={"head": lax.rem(place + last, size)},
            device_id_type=MESH,
        )

    def rows_of(k):
        return pl.ds(pl.multiple_of(k * ROWS, ROWS), ROWS)

    def pass_on(k, copy, land, send, has_source, has_target):
        @pl.when(has_source)
        def _():
            copy(k).wait_recv()

        @pl.when(has_target)
        def _():
            slot = lax.rem(k, SEND_SLOTS)

            @pl.when(k >= SEND_SLOTS)
            def _():
                copy(k - SEND_SLOTS).wait_send()

            @pl.when(has_source)
            def _():
                send[slot] = (own[rows_of(k)] + land[lax.rem(k, slots)].astype(F32)).astype(BF16)

            @pl.when(jnp.logical_not(has_source))
            def _():
                send[slot] = own[rows_of(k)].astype(BF16)

            copy(k).start()

    far = jnp.maximum(place, last - place)

    def step(t, carry):
        before(t)
        down = t - (last - place) * HOP

        @pl.when((down >= 0) & (down < chunks))
        def _():
            pass_on(down, down_copy, down_land, down_send, place < last, place > 0)

        up = t - place * HOP

        @pl.when((up >= 0) & (up < chunks))
        def _():
            pass_on(up, up_copy, up_land, up_send, place > 0, place < last)

        k = t - far * HOP

        @pl.when((k >= 0) & (k < chunks))
        def _():
            slot = lax.rem(k, slots)

            @pl.when(place == 0)
            def _():
                finish(k, own[rows_of(k)] + down_land[slot].astype(F32))

            @pl.when(place == last)
            def _():
                finish(k, own[rows_of(k)] + up_land[slot].astype(F32))

            @pl.when((place > 0) & (place < last))
            def _():
                finish(
                    k,
                    own[rows_of(k)] + up_land[slot].astype(F32) + down_land[slot].astype(F32),
                )

        if extra is not None:
            extra(t)
        return carry

    lax.fori_loop(0, max(chunks + last * HOP, extra_steps), step, 0)
    for k in range(chunks - SEND_SLOTS, chunks):

        @pl.when(place < last)
        def _(k=k):
            up_copy(k).wait_send()

        @pl.when(place > 0)
        def _(k=k):
            down_copy(k).wait_send()


def line_barrier(others=0):
    size = lax.axis_size("head")
    place = lax.axis_index("head")
    barrier = pltpu.get_barrier_semaphore()
    inner = (place > 0) & (place < size - 1)

    def greet(near):
        pl.semaphore_signal(
            barrier, inc=1, device_id={"head": lax.rem(near, size)}, device_id_type=MESH
        )

    @pl.when(place > 0)
    def _():
        greet(place + size - 1)

    @pl.when(place < size - 1)
    def _():
        greet(place + 1)

    @pl.when(inner)
    def _():
        pl.semaphore_wait(barrier, 2 + others)

    @pl.when(jnp.logical_not(inner))
    def _():
        pl.semaphore_wait(barrier, 1 + others)


def line_scratch(size, width):
    slots = (size - 1) * HOP + 2
    return [
        pltpu.VMEM((slots, ROWS, width), BF16),
        pltpu.VMEM((slots, ROWS, width), BF16),
        pltpu.VMEM((SEND_SLOTS, ROWS, width), BF16),
        pltpu.VMEM((SEND_SLOTS, ROWS, width), BF16),
        pltpu.SemaphoreType.DMA((slots,)),
        pltpu.SemaphoreType.DMA((slots,)),
        pltpu.SemaphoreType.DMA((SEND_SLOTS,)),
        pltpu.SemaphoreType.DMA((SEND_SLOTS,)),
    ]


def attn_out_kernel(
    mixed_ref, weight_ref, token_ref, gain_ref, hidden_ref, normed_ref,
    hidden, normed, hidden_sem, normed_sem, *scratch
):
    line_barrier()
    per_block = BLOCK_ROWS // ROWS
    blocks = hidden.shape[0] // BLOCK_ROWS

    def block_rows(b):
        return pl.ds(pl.multiple_of(b * BLOCK_ROWS, BLOCK_ROWS), BLOCK_ROWS)

    def before(t):
        @pl.when((lax.rem(t, per_block) == 0) & (t < blocks * per_block))
        def _():
            rows = block_rows(t // per_block)
            hidden[rows] = dot(mixed_ref[rows], weight_ref[...], NN)

    def stores(b):
        rows = block_rows(b)
        return (
            pltpu.make_async_copy(hidden.at[rows], hidden_ref.at[rows], hidden_sem.at[b]),
            pltpu.make_async_copy(normed.at[rows], normed_ref.at[rows], normed_sem.at[b]),
        )

    def finish(k, total):
        rows = pl.ds(pl.multiple_of(k * ROWS, ROWS), ROWS)
        value = token_ref[rows].astype(F32) + total
        hidden[rows] = value
        normed[rows] = (value * inverse_rms(value) * gain_ref[...]).astype(BF16)

        @pl.when(lax.rem(k, per_block) == per_block - 1)
        def _():
            for copy in stores(k // per_block):
                copy.start()

    line_exchange(hidden, finish, before, scratch)
    for b in range(blocks):
        for copy in stores(b):
            copy.wait()


def attn_out_sum(mixed, weight, tokens, gain, size, cid):
    rows, width = tokens.shape
    vmem, any_ = pl.BlockSpec(memory_space=pltpu.VMEM), pl.BlockSpec(memory_space=pl.ANY)
    blocks = rows // BLOCK_ROWS
    return pl.pallas_call(
        attn_out_kernel,
        in_specs=[vmem] * 4,
        out_specs=[any_] * 2,
        out_shape=[jax.ShapeDtypeStruct((rows, width), F32), jax.ShapeDtypeStruct((rows, width), BF16)],
        scratch_shapes=[
            pltpu.VMEM((rows, width), F32),
            pltpu.VMEM((rows, width), BF16),
            pltpu.SemaphoreType.DMA((blocks,)),
            pltpu.SemaphoreType.DMA((blocks,)),
        ]
        + line_scratch(size, width),
        cost_estimate=pl.CostEstimate(
            flops=2 * rows * width * mixed.shape[1], bytes_accessed=150 * 2**20, transcendentals=0
        ),
        compiler_params=pltpu.CompilerParams(
            collective_id=cid, has_side_effects=True, vmem_limit_bytes=48 * 2**20
        ),
    )(mixed, weight, tokens, gain.reshape(1, width))


def mlp_back_kernel(
    tile, seg_bits,
    d_gate_hbm, d_up_hbm, w_gate_hbm, w_up_hbm, hidden_hbm, grad_hbm, gain_ref, sum_in,
    d_out_ref, d_own_ref, gain_part_ref, sum_out,
    d_gate, d_up, w_gate, w_up, hidden, grad, own, load_sem, store_sem, *scratch
):
    per_block = BLOCK_ROWS // ROWS
    blocks = own.shape[0] // BLOCK_ROWS
    size = lax.axis_size("head")
    place = lax.axis_index("head")
    per_device = own.shape[0] // ROWS // size
    loads = [
        pltpu.make_async_copy(source, target, load_sem.at[i])
        for i, (source, target) in enumerate(
            ((d_gate_hbm, d_gate), (w_gate_hbm, w_gate), (d_up_hbm, d_up), (w_up_hbm, w_up),
             (hidden_hbm, hidden), (grad_hbm, grad))
        )
    ]
    for load in loads:
        load.start()
    gain_part_ref[...] = jnp.zeros_like(gain_part_ref)
    greet_seg(seg_bits)
    line_barrier(seg_bits)
    engine_step, steps = sum_engine(
        [sum_in], [sum_out], tile, seg_bits, scratch[LINE_REFS:]
    )

    def block_rows(b):
        return pl.ds(pl.multiple_of(b * BLOCK_ROWS, BLOCK_ROWS), BLOCK_ROWS)

    for load in loads[:4]:
        load.wait()

    def before(t):
        @pl.when((lax.rem(t, per_block) == 0) & (t < blocks * per_block))
        def _():
            rows = block_rows(t // per_block)
            own[rows] = dot(d_gate[rows], w_gate[...], NT) + dot(d_up[rows], w_up[...], NT)

        @pl.when(t == 0)
        def _():
            for load in loads[4:]:
                load.wait()

    def store(b):
        rows = block_rows(b)
        return pltpu.make_async_copy(grad.at[rows], d_out_ref.at[rows], store_sem.at[b])

    def finish(k, total):
        rows = pl.ds(pl.multiple_of(k * ROWS, ROWS), ROWS)
        value = hidden[rows]
        inverse = inverse_rms(value)
        normal = value * inverse
        scaled = gain_ref[...] * total
        mean = jnp.mean(scaled * normal, axis=-1, keepdims=True)
        d_hidden = grad[rows].astype(F32) + inverse * (scaled - normal * mean)
        grad[rows] = d_hidden.astype(BF16)

        @pl.when(k // per_device == place)
        def _():
            mine = pl.ds(pl.multiple_of(lax.rem(k, per_device) * ROWS, ROWS), ROWS)
            d_own_ref[mine] = d_hidden
            gain_part_ref[...] += jnp.sum((total * normal).reshape(ROWS // 8, 8, -1), axis=0)

        @pl.when(lax.rem(k, per_block) == per_block - 1)
        def _():
            store(k // per_block).start()

    line_exchange(own, finish, before, scratch[:LINE_REFS], engine_step, steps)
    for b in range(blocks):
        store(b).wait()


def mlp_back_sum(d_gate, d_up, w_gate, w_up, hidden, grad, gain, summed, tile, seg_size, size, cid):
    rows, width = hidden.shape
    units = d_gate.shape[1]
    seg_bits = bits_of(seg_size)
    vmem, any_ = pl.BlockSpec(memory_space=pltpu.VMEM), pl.BlockSpec(memory_space=pltpu.HBM)
    blocks = rows // BLOCK_ROWS
    return pl.pallas_call(
        functools.partial(mlp_back_kernel, tile, seg_bits),
        in_specs=[any_] * 6 + [vmem, any_],
        out_specs=[any_, vmem, vmem, any_],
        out_shape=[
            jax.ShapeDtypeStruct((rows, width), BF16),
            jax.ShapeDtypeStruct((rows // size, width), F32),
            jax.ShapeDtypeStruct((8, width), F32),
            jax.ShapeDtypeStruct(summed.shape, BF16),
        ],
        scratch_shapes=[
            pltpu.VMEM((rows, units), BF16),
            pltpu.VMEM((rows, units), BF16),
            pltpu.VMEM((width, units), BF16),
            pltpu.VMEM((width, units), BF16),
            pltpu.VMEM((rows, width), F32),
            pltpu.VMEM((rows, width), BF16),
            pltpu.VMEM((rows, width), F32),
            pltpu.SemaphoreType.DMA((6,)),
            pltpu.SemaphoreType.DMA((blocks,)),
        ]
        + line_scratch(size, width)
        + engine_scratch(tile, seg_bits),
        cost_estimate=pl.CostEstimate(
            flops=4 * rows * width * units, bytes_accessed=250 * 2**20, transcendentals=0
        ),
        compiler_params=pltpu.CompilerParams(
            collective_id=cid, has_side_effects=True, vmem_limit_bytes=62 * 2**20
        ),
    )(d_gate, d_up, w_gate, w_up, hidden, grad, gain.reshape(1, width), summed)


MLP_BLOCK = 256
MLP_ROWS = 1024


def mlp_kernel(
    rows_ref, grad_ref, w_gate_ref, w_up_ref, w_down_ref,
    d_gate_ref, d_up_ref, grad_gate_ref, grad_up_top, grad_up_low, grad_down_ref, out_ref,
    flipped, act, total,
):
    count, width = rows_ref.shape
    first = pl.program_id(0) == 0
    last = pl.program_id(0) == pl.num_programs(0) - 1

    @pl.when(first)
    def _():
        total[...] = jnp.zeros_like(total)

        @pl.loop(0, width // MLP_ROWS)
        def _(i):
            part = pl.ds(pl.multiple_of(i * MLP_ROWS, MLP_ROWS), MLP_ROWS)
            flipped[part] = rows_ref[:, part].T

    @pl.loop(0, count // MLP_ROWS)
    def _(i):
        part = pl.ds(pl.multiple_of(i * MLP_ROWS, MLP_ROWS), MLP_ROWS)
        rows = rows_ref[part]
        gate_pre = dot(rows, w_gate_ref[...], NN)
        up_proj = dot(rows, w_up_ref[...], NN)
        d_act = dot(grad_ref[part], w_down_ref[...], NT)
        gate_sig = jax.nn.sigmoid(gate_pre)
        silu_gate = gate_pre * gate_sig
        activation = (silu_gate * up_proj).astype(BF16)
        act[part] = activation
        d_gate_ref[part] = (
            d_act * up_proj * gate_sig * (1.0 + gate_pre * (1.0 - gate_sig))
        ).astype(BF16)
        d_up_ref[part] = (d_act * silu_gate).astype(BF16)
        total[part] += dot(activation, w_down_ref[...], NN)

    @pl.loop(0, width // MLP_ROWS)
    def _(i):
        part = pl.ds(pl.multiple_of(i * MLP_ROWS, MLP_ROWS), MLP_ROWS)
        grad_gate_ref[part] = dot(flipped[part], d_gate_ref[...], NN).astype(BF16)
        grad_down_ref[:, part] = dot(act[...], grad_ref[:, part], TN).astype(BF16)

    top = grad_up_top.shape[0]
    grad_up_top[...] = dot(flipped[:top], d_up_ref[...], NN).astype(BF16)
    grad_up_low[...] = dot(flipped[top:], d_up_ref[...], NN).astype(BF16)

    @pl.when(last)
    def _():
        out_ref[...] = total[...].astype(BF16)


def mlp_both(rows, grad, w_gate, w_up, w_down):
    count, width = rows.shape
    units = w_gate.shape[1]
    block = min(MLP_BLOCK, units)
    once = pl.Buffered(1)
    whole = pl.BlockSpec((count, width), lambda j: (0, 0), pipeline_mode=once)
    side = pl.BlockSpec((count, block), lambda j: (0, j))
    tall = pl.BlockSpec((width, block), lambda j: (0, j))
    wide = pl.BlockSpec((block, width), lambda j: (j, 0))
    top = width // 4
    parts = [pl.BlockSpec((rows, block), lambda j: (0, j)) for rows in (top, width - top)]
    return pl.pallas_call(
        mlp_kernel,
        grid=(units // block,),
        in_specs=[whole, whole, tall, tall, wide],
        out_specs=[side, side, tall, *parts, wide, whole],
        out_shape=[
            jax.ShapeDtypeStruct((count, units), BF16),
            jax.ShapeDtypeStruct((count, units), BF16),
            jax.ShapeDtypeStruct((width, units), BF16),
            jax.ShapeDtypeStruct((top, units), BF16),
            jax.ShapeDtypeStruct((width - top, units), BF16),
            jax.ShapeDtypeStruct((units, width), BF16),
            jax.ShapeDtypeStruct((count, width), BF16),
        ],
        scratch_shapes=[
            pltpu.VMEM((width, count), BF16),
            pltpu.VMEM((count, block), BF16),
            pltpu.VMEM((count, width), F32),
        ],
        cost_estimate=pl.CostEstimate(
            flops=14 * count * width * units,
            bytes_accessed=2 * (3 * count * width + 6 * width * units + 2 * count * units),
            transcendentals=count * units,
        ),
        compiler_params=pltpu.CompilerParams(vmem_limit_bytes=56 * 2**20),
    )(rows, grad, w_gate, w_up, w_down)


WIDEN_SLOTS = 4


def widen_kernel(shapes, places, wide_count, tile, *refs):
    count = len(shapes)
    sources, targets = refs[:count], refs[count : count + wide_count]
    narrow, wide, load_sem, store_sem = refs[count + wide_count :]
    high, broad = tile
    counts = [(rows // high) * (width // broad) for rows, width in shapes]
    total = sum(counts)

    def pick(k, act):
        first = 0
        for i in range(count):
            @pl.when((k >= first) & (k < first + counts[i]))
            def _(i=i, first=first):
                across = shapes[i][1] // broad
                place = k - first
                row = pl.multiple_of((place // across) * high, high)
                col = pl.multiple_of(lax.rem(place, across) * broad, broad)
                act(i, (pl.ds(row, high), pl.ds(col, broad)))
            first += counts[i]

    def load(k, i, where):
        slot = lax.rem(k, WIDEN_SLOTS)
        return pltpu.make_async_copy(sources[i].at[where], narrow.at[slot], load_sem.at[slot])

    def store(k, i, where):
        slot = lax.rem(k, WIDEN_SLOTS)
        target, first = places[i]
        rows = pl.ds(pl.multiple_of(first + where[0].start, high), high)
        return pltpu.make_async_copy(
            wide.at[slot], targets[target].at[rows, where[1]], store_sem.at[slot]
        )

    zero = (pl.ds(0, high), pl.ds(0, broad))
    ahead = WIDEN_SLOTS - 1
    for k in range(ahead):
        pick(k, lambda i, where, k=k: load(k, i, where).start())

    def step(k, carry):
        @pl.when(k + ahead < total)
        def _():
            pick(k + ahead, lambda i, where: load(k + ahead, i, where).start())

        @pl.when(k >= WIDEN_SLOTS)
        def _():
            store(k - WIDEN_SLOTS, 0, zero).wait()

        load(k, 0, zero).wait()
        slot = lax.rem(k, WIDEN_SLOTS)
        wide[slot] = narrow[slot].astype(F32)
        pick(k, lambda i, where: store(k, i, where).start())
        return carry

    lax.fori_loop(0, total, step, 0)
    for k in range(total - WIDEN_SLOTS, total):
        store(k, 0, zero).wait()


def widen(groups, tile):
    arrays, places, targets = [], [], []
    for group in groups:
        rows = 0
        for value in group:
            arrays.append(value)
            places.append((len(targets), rows))
            rows += value.shape[0]
        targets.append((rows, group[0].shape[1]))
    shapes = [value.shape for value in arrays]
    any_ = pl.BlockSpec(memory_space=pltpu.HBM)
    return pl.pallas_call(
        functools.partial(widen_kernel, shapes, places, len(targets), tile),
        in_specs=[any_] * len(arrays),
        out_specs=[any_] * len(targets),
        out_shape=[jax.ShapeDtypeStruct(shape, F32) for shape in targets],
        scratch_shapes=[
            pltpu.VMEM((WIDEN_SLOTS, *tile), BF16),
            pltpu.VMEM((WIDEN_SLOTS, *tile), F32),
            pltpu.SemaphoreType.DMA((WIDEN_SLOTS,)),
            pltpu.SemaphoreType.DMA((WIDEN_SLOTS,)),
        ],
        cost_estimate=pl.CostEstimate(
            flops=0, bytes_accessed=6 * sum(r * c for r, c in shapes), transcendentals=0
        ),
        compiler_params=pltpu.CompilerParams(vmem_limit_bytes=40 * 2**20),
    )(*arrays)


def attn_weights_kernel(
    rows_ref, d_out_ref, mixed_ref, d_query_ref, d_key_ref, d_value_ref,
    w_query_ref, w_key_ref, w_value_ref,
    d_rows_ref, grad_query_ref, grad_key_ref, grad_value_ref, grad_out_ref, gain_part_ref,
    flipped_mixed, flipped_rows,
):
    @pl.when(pl.program_id(0) == 0)
    def _():
        flipped_mixed[...] = mixed_ref[...].T

    flipped_rows[...] = rows_ref[...].T
    d_rows = (
        dot(d_query_ref[...], w_query_ref[...], NT)
        + dot(d_key_ref[...], w_key_ref[...], NT)
        + dot(d_value_ref[...], w_value_ref[...], NT)
    )
    d_rows_ref[...] = d_rows.astype(BF16)
    product = d_rows * rows_ref[...].astype(F32)
    gain_part_ref[...] = jnp.sum(product.reshape(-1, 8, product.shape[1]), axis=0)
    grad_query_ref[...] = dot(flipped_rows[...], d_query_ref[...], NN).astype(BF16)
    grad_key_ref[...] = dot(flipped_rows[...], d_key_ref[...], NN).astype(BF16)
    grad_value_ref[...] = dot(flipped_rows[...], d_value_ref[...], NN).astype(BF16)
    grad_out_ref[...] = dot(flipped_mixed[...], d_out_ref[...], NN).astype(BF16)


def attn_weights(rows, d_out, mixed, d_query, d_key, d_value, w_query, w_key, w_value):
    count, width = rows.shape
    cols = mixed.shape[1]
    block = 512
    once = pl.Buffered(1)
    slim = pl.BlockSpec((count, cols), lambda j: (0, 0), pipeline_mode=once)
    side = pl.BlockSpec((count, block), lambda j: (0, j))
    tall = pl.BlockSpec((block, cols), lambda j: (j, 0))
    wide = pl.BlockSpec((cols, block), lambda j: (0, j))
    tall_type = jax.ShapeDtypeStruct((width, cols), BF16)
    return pl.pallas_call(
        attn_weights_kernel,
        grid=(width // block,),
        in_specs=[side, side, slim, slim, slim, slim, tall, tall, tall],
        out_specs=[side, tall, tall, tall, wide, pl.BlockSpec((8, block), lambda j: (0, j))],
        out_shape=[
            jax.ShapeDtypeStruct((count, width), BF16),
            tall_type,
            tall_type,
            tall_type,
            jax.ShapeDtypeStruct((cols, width), BF16),
            jax.ShapeDtypeStruct((8, width), F32),
        ],
        scratch_shapes=[pltpu.VMEM((cols, count), BF16), pltpu.VMEM((block, count), BF16)],
        cost_estimate=pl.CostEstimate(
            flops=14 * count * width * cols,
            bytes_accessed=2 * (3 * count * width + 4 * count * cols + 7 * width * cols),
            transcendentals=0,
        ),
        compiler_params=pltpu.CompilerParams(vmem_limit_bytes=48 * 2**20),
    )(rows, d_out, mixed, d_query, d_key, d_value, w_query, w_key, w_value)


def from_behind(value, axis, steps):
    count = lax.axis_size(axis)
    initial, last = (max(0, -steps), min(count, count - steps))
    return lax.ppermute(value, axis, [(source, source + steps) for source in range(initial, last)])


def elu_plus(values):
    return jnp.where(values > 0, values + 1.0, jnp.exp(jnp.minimum(values, 0.0)))


def elu_slope(values):
    return jnp.where(values > 0, 1.0, jnp.exp(jnp.minimum(values, 0.0)))


def inverse_rms(values):
    return lax.rsqrt(jnp.mean(values * values, axis=-1, keepdims=True) + epsilon)


def norm_backward(values, inverse, gain_vec, grad_out):
    normal = values * inverse
    scaled = gain_vec * grad_out
    grad_in = inverse * (scaled - normal * jnp.mean(scaled * normal, axis=-1, keepdims=True))
    return grad_in


def dot(left, right, dims, precision=None):
    return lax.dot_general(
        left, right, (dims, ((), ())), precision=precision, preferred_element_type=F32
    )


NN = ((1,), (0,))
NT = ((1,), (1,))
TN = ((0,), (0,))


def valid_column(valid_len):
    return (lax.broadcasted_iota(jnp.int32, (SEG_LEN, 1), 0) < valid_len).astype(F32)


def update_kernel(valid_ref, key_ref, value_ref, out_ref):
    key_feat = elu_plus(key_ref[...].astype(F32)) * valid_column(valid_ref[0])
    out_ref[0, :DH] = dot(key_feat, value_ref[...].astype(F32), TN, highest)
    out_ref[0, DH:] = jnp.broadcast_to(jnp.sum(key_feat, axis=0, keepdims=True), (8, DH))


def block_probs(query_block, key_ref, start, valid_len):
    cols = start + query_block.shape[0]
    scores = dot(query_block, key_ref[:cols], NT) * (DH**-0.5)
    row_pos = start + lax.broadcasted_iota(jnp.int32, scores.shape, 0)
    col_pos = lax.broadcasted_iota(jnp.int32, scores.shape, 1)
    allowed = (row_pos >= col_pos) & (col_pos < valid_len)
    scores = jnp.where(allowed, scores, masked_score)
    weights = jnp.exp(scores - jnp.max(scores, axis=-1, keepdims=True))
    return weights / jnp.sum(weights, axis=-1, keepdims=True)


def local_kernel(valid_ref, query_ref, key_ref, value_ref, out_ref):
    for start in range(0, SEG_LEN, BLOCK):
        rows = slice(start, start + BLOCK)
        probs = block_probs(query_ref[rows], key_ref, start, valid_ref[0])
        out_ref[rows] = dot(probs.astype(BF16), value_ref[: start + BLOCK], NN)


def retrieve(query_feat, memory, normal):
    numerator = dot(query_feat, memory, NN, highest)
    denominator = jnp.sum(query_feat * normal, axis=-1, keepdims=True) + 1.0
    return numerator / denominator, denominator


def mix_kernel(gate_ref, query_ref, local_ref, memory_ref, out_ref):
    gate = gate_ref[pl.program_id(0)]
    query_feat = elu_plus(query_ref[...].astype(F32))
    retrieved, _ = retrieve(query_feat, memory_ref[0, :DH], memory_ref[0, DH : DH + 1])
    out_ref[...] = (gate * retrieved + (1.0 - gate) * local_ref[...]).astype(BF16)


def memory_back_kernel(
    gate_ref, query_ref, local_ref, memory_ref, d_mixed_ref, feat_ref, back_ref, gate_grad_ref
):
    gate = gate_ref[pl.program_id(0)]
    query_vals = query_ref[...].astype(F32)
    query_feat = elu_plus(query_vals)
    memory, normal = memory_ref[0, :DH], memory_ref[0, DH : DH + 1]
    retrieved, denominator = retrieve(query_feat, memory, normal)
    d_mixed = d_mixed_ref[...]
    gate_grad_ref[0] = jnp.broadcast_to(
        jnp.sum(d_mixed * (retrieved - local_ref[...]), axis=0, keepdims=True), (8, DH)
    )
    d_retrieved = gate * d_mixed
    d_numerator = d_retrieved / denominator
    d_denominator = -jnp.sum(d_retrieved * retrieved, axis=-1, keepdims=True) / denominator
    d_feat = dot(d_numerator, memory, NT, highest) + d_denominator * normal
    feat_ref[...] = d_feat * elu_slope(query_vals)
    back_ref[0, :DH] = dot(query_feat, d_numerator, TN, highest)
    back_ref[0, DH:] = jnp.broadcast_to(
        jnp.sum(d_denominator * query_feat, axis=0, keepdims=True), (8, DH)
    )


def local_back_kernel(
    gate_ref,
    valid_ref,
    query_ref,
    key_ref,
    value_ref,
    d_mixed_ref,
    feat_ref,
    d_query_ref,
    d_key_ref,
    d_value_ref,
):
    keep = 1.0 - gate_ref[pl.program_id(0)]
    d_key_ref[...] = jnp.zeros_like(d_key_ref)
    d_value_ref[...] = jnp.zeros_like(d_value_ref)
    for start in range(0, SEG_LEN, BLOCK):
        rows = slice(start, start + BLOCK)
        cols = slice(0, start + BLOCK)
        query_block = query_ref[rows]
        probs = block_probs(query_block, key_ref, start, valid_ref[0])
        d_local = (keep * d_mixed_ref[rows]).astype(BF16)
        d_probs = dot(d_local, value_ref[cols], NT)
        row_dot = jnp.sum(probs * d_probs, axis=-1, keepdims=True)
        d_scores = (probs * (d_probs - row_dot) * (DH**-0.5)).astype(BF16)
        d_query_ref[rows] = (dot(d_scores, key_ref[cols], NN) + feat_ref[rows]).astype(BF16)
        d_key_ref[cols] += dot(d_scores, query_block, TN)
        d_value_ref[cols] += dot(probs.astype(BF16), d_local, TN)


def finish_back_kernel(
    valid_ref, key_ref, value_ref, d_key_in, d_value_in, memory_ref, d_key_ref, d_value_ref
):
    valid = valid_column(valid_ref[0])
    key_vals = key_ref[...].astype(F32)
    memory, normal = memory_ref[0, :DH], memory_ref[0, DH : DH + 1]
    d_feat = (dot(value_ref[...].astype(F32), memory, NT, highest) + normal) * valid
    d_key_ref[...] = (d_key_in[...] + d_feat * elu_slope(key_vals)).astype(BF16)
    key_feat = elu_plus(key_vals) * valid
    d_value_ref[...] = (d_value_in[...] + dot(key_feat, memory, NN, highest)).astype(BF16)


SCALAR = pl.BlockSpec(memory_space=pltpu.SMEM)
COLUMN = pl.BlockSpec((SEG_LEN, DH), lambda head: (0, head))
MEMORY = pl.BlockSpec((1, MEM_ROWS, DH), lambda head: (head, 0, 0))
SMALL = pl.BlockSpec((1, 8, DH), lambda head: (head, 0, 0))


def per_head(kernel, heads, in_specs, out_specs, out_types, flops, transcendentals=0):
    moved = heads * SEG_LEN * DH * 4 * len(in_specs)
    return pl.pallas_call(
        kernel,
        grid=(heads,),
        in_specs=in_specs,
        out_specs=out_specs,
        out_shape=out_types,
        cost_estimate=pl.CostEstimate(
            flops=flops, bytes_accessed=moved, transcendentals=transcendentals
        ),
        compiler_params=pltpu.CompilerParams(vmem_limit_bytes=40 * 1024 * 1024),
    )


def per_device(
    tokens,
    cotangent,
    gain_attn,
    gain_mlp,
    w_query,
    w_key,
    w_value,
    w_out,
    w_gate,
    w_up,
    w_down,
    mem_gate,
    lengths,
):
    seg_index = lax.axis_index("seg")
    head_index = lax.axis_index("head")
    head_groups = lax.axis_size("head")
    seg_size = lax.axis_size("seg")
    position = seg_index % SEGS
    sequence = seg_index // SEGS
    seq_length = jnp.sum(jnp.where(lax.iota(jnp.int32, lengths.shape[0]) == sequence, lengths, 0))
    valid_len = jnp.where(position == SEGS - 1, seq_length, SEG_LEN).reshape(1)
    heads = mem_gate.shape[0]
    cols = heads * DH
    col_f32 = jax.ShapeDtypeStruct((SEG_LEN, cols), F32)
    col_bf16 = jax.ShapeDtypeStruct((SEG_LEN, cols), BF16)
    mem_f32 = jax.ShapeDtypeStruct((heads, MEM_ROWS, DH), F32)
    small_f32 = jax.ShapeDtypeStruct((heads, 8, DH), F32)
    unit = 2 * heads * SEG_LEN * DH * DH
    pairs = heads * SEG_LEN * SEG_LEN

    token_vals = tokens.astype(F32)
    gathered_tokens = lax.all_gather(tokens, "head", axis=0, tiled=True)
    gathered_grad = lax.all_gather(cotangent, "head", axis=0, tiled=True)
    all_tokens = gathered_tokens.astype(F32)
    gathered_attn = (all_tokens * inverse_rms(all_tokens) * gain_attn).astype(BF16)

    def project(weight):
        return jnp.dot(gathered_attn, weight, preferred_element_type=F32).astype(BF16)

    key_rows = project(w_key)
    value_rows = project(w_value)
    update = per_head(update_kernel, heads, [SCALAR, COLUMN, COLUMN], MEMORY, mem_f32, 6 * unit)(
        valid_len, key_rows, value_rows
    )
    query_rows = project(w_query)
    memory_prev = jnp.zeros_like(update)
    for distance in range(1, SEGS):
        moved = from_behind(update, "seg", distance)
        memory_prev = memory_prev + jnp.where(position >= distance, moved, 0.0)
    local_attn = per_head(
        local_kernel, heads, [SCALAR, COLUMN, COLUMN, COLUMN], COLUMN, col_f32, 4 * pairs * DH, pairs
    )(valid_len, query_rows, key_rows, value_rows)
    after = memory_prev + update
    memory_after = (after[:, :DH] * SEG_LEN ** (-0.5))[None]
    normal_after = (after[:, DH] / SEG_LEN)[None]
    mix_sig = jax.nn.sigmoid(mem_gate)
    mixed_attn = per_head(
        mix_kernel, heads, [SCALAR, COLUMN, COLUMN, MEMORY], COLUMN, col_bf16, 6 * unit
    )(mix_sig, query_rows, local_attn, memory_prev)
    all_hidden, gathered_mlp = attn_out_sum(
        mixed_attn, w_out, gathered_tokens, gain_mlp, head_groups, 1
    )
    own_rows = tokens.shape[0]
    hidden_res = lax.dynamic_slice_in_dim(all_hidden, head_index * own_rows, own_rows, 0)
    d_gate, d_up, grad_gate, up_top, up_low, grad_down, mlp_part = mlp_both(
        gathered_mlp, gathered_grad, w_gate, w_up, w_down
    )
    sum_gate, sum_up_top = lax.psum((grad_gate, up_top), "seg")
    gathered_hidden, d_hidden, gain_mlp_rows, summed_down = mlp_back_sum(
        d_gate,
        d_up,
        w_gate,
        w_up,
        all_hidden,
        gathered_grad,
        gain_mlp,
        grad_down,
        (BLOCK, cols),
        seg_size,
        head_groups,
        2,
    )
    mlp_out = lax.psum_scatter(mlp_part, "head", scatter_dimension=0, tiled=True)
    output = (hidden_res + mlp_out.astype(F32)).astype(BF16)
    d_mixed = dot(gathered_hidden, w_out, NT)
    feat_grad, back, gate_cols = per_head(
        memory_back_kernel,
        heads,
        [SCALAR, COLUMN, COLUMN, MEMORY, COLUMN],
        [COLUMN, MEMORY, SMALL],
        [col_f32, mem_f32, small_f32],
        18 * unit,
    )(mix_sig, query_rows, local_attn, memory_prev, d_mixed)
    back_update = jnp.zeros_like(back)
    for distance in range(1, SEGS):
        moved = from_behind(back, "seg", -distance)
        back_update = back_update + jnp.where(position + distance <= SEGS - 1, moved, 0.0)
    d_queries, key_local, value_local = per_head(
        local_back_kernel,
        heads,
        [SCALAR, SCALAR] + [COLUMN] * 5,
        [COLUMN] * 3,
        [col_bf16, col_f32, col_f32],
        10 * pairs * DH,
        pairs,
    )(mix_sig, valid_len, query_rows, key_rows, value_rows, d_mixed, feat_grad)
    d_keys, d_values = per_head(
        finish_back_kernel,
        heads,
        [SCALAR] + [COLUMN] * 4 + [MEMORY],
        [COLUMN] * 2,
        [col_bf16, col_bf16],
        12 * unit,
    )(valid_len, key_rows, value_rows, key_local, value_local, back_update)
    d_part, grad_query, grad_key, grad_value, grad_out, gain_attn_rows = attn_weights(
        gathered_attn,
        gathered_hidden,
        mixed_attn,
        d_queries,
        d_keys,
        d_values,
        w_query,
        w_key,
        w_value,
    )
    d_normed_attn = lax.psum_scatter(d_part, "head", scatter_dimension=0, tiled=True).astype(F32)
    grad_in_attn = norm_backward(token_vals, inverse_rms(token_vals), gain_attn, d_normed_attn)
    grad_tokens = (d_hidden + grad_in_attn).astype(BF16)
    gate_part = mix_sig * (1.0 - mix_sig) * jnp.sum(gate_cols[:, 0], axis=-1)
    slots = jnp.where(
        (lax.iota(jnp.int32, head_groups) == head_index)[:, None], gate_part[None], 0.0
    )
    width = gain_attn.shape[0]
    gain_attn_part = jnp.sum(gain_attn_rows, axis=0) / gain_attn
    gain_mlp_part = jnp.sum(gain_mlp_rows, axis=0)
    parts = jnp.concatenate([gain_attn_part, gain_mlp_part, slots.reshape(-1)])
    lines = -(-parts.shape[0] // (8 * DH)) * 8
    parts = jnp.pad(parts, (0, lines * DH - parts.shape[0])).reshape(lines, DH)
    small, *late = grad_sum(
        parts,
        [up_low, grad_out, grad_query, grad_key, grad_value],
        (cols, cols),
        seg_size,
        head_groups,
        0,
    )
    small = small.reshape(-1)
    grad_mem_gate = lax.dynamic_slice(small, (2 * width + head_index * heads,), (heads,))
    grads = widen(
        [(sum_gate,), (sum_up_top, late[0]), (summed_down,)] + [(grad,) for grad in late[1:]],
        (cols, cols),
    )
    return (
        output,
        grad_tokens,
        memory_after,
        normal_after,
        small[:width],
        small[width : 2 * width],
        grads[4],
        grads[5],
        grads[6],
        grads[3],
        grads[0],
        grads[1],
        grads[2],
        grad_mem_gate,
    )


def solution(mesh):
    return jax.shard_map(
        per_device,
        mesh=mesh,
        in_specs=(
            P(("seg", "head"), None),
            P(("seg", "head"), None),
            P(),
            P(),
            P(None, "head"),
            P(None, "head"),
            P(None, "head"),
            P("head", None),
            P(None, "head"),
            P(None, "head"),
            P("head", None),
            P("head"),
            P(),
        ),
        out_specs=(
            P(("seg", "head"), None),
            P(("seg", "head"), None),
            P("seg", "head", None, None),
            P("seg", "head", None),
            P(),
            P(),
            P(None, "head"),
            P(None, "head"),
            P(None, "head"),
            P("head", None),
            P(None, "head"),
            P(None, "head"),
            P("head", None),
            P("head"),
        ),
        check_vma=False,
    )
```

time: 2180 us -> 771 us (0.35)
  waiting for transfers between devices: 1510 us -> 85 us
  Pallas kernels: 0 us -> 611 us
  matrix products: 340 us -> 12.7 us
  local copies, waits for them, and re-layouts: 167 us -> 11.9 us
  blocking collectives: 67.1 us -> 0 us
    psum x1, waiting for transfers between devices: 769 us -> 0.01 us  [per_device(): sum_gate, sum_up_top = lax.psum((grad_gate, up_top), 'seg')]
    pallas_call x0 -> x12, Pallas kernels: none -> 611 us  [the longest x1 151 us: mlp_back_sum(): pl.pallas_call(functools.partial(mlp_back_kernel, tile, seg_bits), in_spe...]
    reduce_scatter x4 -> x2, waiting for transfers between devices: 442 us -> 0.02 us  [the longest x1 0.02 us: per_device(): lax.psum_scatter(mlp_part, 'head', scatter_dimension=0, tiled=True)]
    dot_general x43 -> x4, matrix products: 340 us -> 12.7 us  [the longest x3 6.97 us: project(): jnp.dot(gathered_attn, weight, preferred_element_type=F32).astype(BF16)]
    all_gather x3 -> x1, waiting for transfers between devices: 244 us -> 83 us  [per_device(): gathered_tokens = lax.all_gather(tokens, 'head', axis=0, tiled=True)]
    dynamic_update_slice x8 -> x0, local copies, waits for them, and re-layouts: 92.8 us -> none  [per_device(): lax.map(block_forward, lax.iota(jnp.int32, block_count))]
    psum x2 -> x0, blocking collectives: 67.1 us -> none  [the longest x1 46.5 us: per_device(): gain_totals = lax.psum((gain_attn_part, gain_mlp_part), ('seg', 'head'))]
    all_gather x1, waiting for transfers between devices: 52 us -> 0.02 us  [per_device(): gathered_grad = lax.all_gather(cotangent, 'head', axis=0, tiled=True)]
  transfers between devices with their start and end apart: 21 -> 11, of which waited for: 10 -> 1; matrix products, arithmetic and copies ran while one was open for 18% -> 3% of each run, Pallas kernels for 0% -> 70%
where the time goes in v1:
time: 771 us; the launch traced here: 763 us
  Pallas kernels  611 us (79%)
  waiting for transfers between devices  85 us (11%)
  between operations  15.5 us (2%)
  other arithmetic  13.7 us (2%)
  starting transfers between devices  12.8 us (2%)
  matrix products  12.7 us (2%)
  local copies, waits for them, and re-layouts  11.9 us (2%)
    pallas_call x1, Pallas kernels, mlp_back_sum(): pl.pallas_call(functools.partial(mlp_back_kernel, tile, seg_bits), in_spe...  151 us
    pallas_call x1, Pallas kernels, attn_out_sum(): pl.pallas_call(attn_out_kernel, in_specs=[vmem] * 4, out_specs=[any_] * 2...  143 us
    pallas_call x1, Pallas kernels, grad_sum(): pl.pallas_call(functools.partial(grad_sum_kernel, count, tile, seg_bits,...  142 us
    all_gather x1, waiting for transfers between devices, per_device(): gathered_tokens = lax.all_gather(tokens, 'head', axis=0, tiled=True)  83 us
    pallas_call x1, Pallas kernels, mlp_both(): pl.pallas_call(mlp_kernel, grid=(units // block,), in_specs=[whole, whole...  78.3 us
    pallas_call x1, Pallas kernels, widen(): pl.pallas_call(functools.partial(widen_kernel, shapes, places, len(target...  30.8 us
    pallas_call x1, Pallas kernels, attn_weights(): pl.pallas_call(attn_weights_kernel, grid=(width // block,), in_specs=[sid...  19.5 us
    pallas_call x1, Pallas kernels, per_device(): per_head(local_back_kernel, heads, [SCALAR, SCALAR] + [COLUMN] * 5, [COLU...  15.9 us
  transfers between devices with their start and end apart: 11, of which 1 were waited for; matrix products, arithmetic and copies ran while one was open for 3% of the time, Pallas kernels for 70%

profile of v1, /device:TPU:0, one launch (start us, length us, event | category | flops | bytes accessed | tf_op | source)
XLA Modules:
  0.0 762.9 jit_solution(8197152816087895285)
XLA Ops:
  7.2 0.0 all-gather.3.cloned.1.call-start
  7.2 0.7 all-gather.3.cloned.1.call-update
  7.9 0.0 all-gather.5.cloned.1.call-start
  8.0 0.7 all-gather.5.cloned.1.call-update
  8.7 0.0 all-reduce.4.cloned.1.call-start
  8.8 0.6 fusion.14
  10.1 0.0 copy-start.20
  10.1 83.0 %all-gather.3.cloned.1.call-done.token_ref = bf16[1024,2048]{1,0:T(8,128)(2,1)} async-done(((bf16[256,2048]{1,0:T(8,128)(2,1)}), bf16[1024,2048]{1,0:T(8,128)(2,1)}) %all-gather.3.cloned.1.call-update) | async-done | bytes 4194320 | tf_op jit(solution)/shard_map/all_gather | solution.py:1054
  93.1 3.2 fusion
  96.3 0.2 copy-done.16
  96.5 1.0 fusion.2.rows_ref
  97.6 0.6 copy-done.24
  98.1 2.3 convolution_convert_fusion.value_ref
  100.5 0.9 copy-done.23
  101.3 2.3 convolution_convert_fusion.1.key_ref
  103.7 0.0 copy-start.11
  103.7 3.3 shard_map.237
  107.0 2.8 collective-permute-start.2
  109.8 3.4 collective-permute-start.1
  113.2 2.3 collective-permute-start
  115.6 2.3 convolution_convert_fusion.2.query_ref
  117.9 0.0 copy-start.7
  117.9 9.7 %shard_map.236.local_ref = f32[1024,512]{1,0:T(8,128)S(1)} custom-call(s32[1]{0:T(128)} %bitcast.valid_ref, bf16[1024,512]{1,0:T(8,128)(2,1)S(1)} %convolution_convert_fusion.2.query_ref, bf16[1024,512]{1,0:T(8,128)(2,1)S(1)} %convolution_convert_fusion.1.key_ref, bf16[1024,512]{1,0:T(8,128)(2,1)S(1)} %convolution_convert_fusion.value_ref), custom_call_target="tpu_custom_call" | custom-call | flops 2147483648 | bytes 8388608 | tf_op jit(solution)/shard_map/pallas_call | solution.py:1072
  127.7 0.1 fusion.15
  127.8 0.0 copy-start.13
  127.8 3.6 shard_map.238.mixed_ref
  131.5 142.6 %shard_map.239 = (f32[1024,2048]{1,0:T(8,128)}, bf16[1024,2048]{1,0:T(8,128)(2,1)}) custom-call(bf16[1024,512]{1,0:T(8,128)(2,1)S(1)} %shard_map.238.mixed_ref, bf16[512,2048]{1,0:T(8,128)(2,1)S(1)} %copy-done.13, bf16[1024,2048]{1,0:T(8,128)(2,1)} %all-gather.3.cloned.1.call-done.token_ref, f32[1,2048]{1,0:T(1,128)S(1)} %bitcast.22), custom_call_target="tpu_custom_call" | custom-call | flops 2147483648 | bytes 157286400 | tf_op jit(solution)/shard_map/pallas_call | solution.py:487
  274.0 0.0 all-gather.5.cloned.1.call-done.grad_ref.grad_hbm
  274.1 78.3 %shard_map.240 = (bf16[1024,2048]{1,0:T(8,128)(2,1)}, bf16[1024,2048]{1,0:T(8,128)(2,1)}, bf16[2048,2048]{1,0:T(8,128)(2,1)}, bf16[512,2048]{1,0:T(8,128)(2,1)},...) custom-call(bf16[1024,2048]{1,0:T(8,128)(2,1)} %get-tuple-element.55.rows_ref, ...), custom_call_target="tpu_custom_call" | custom-call | flops 60129542144 | bytes 71303168 | tf_op jit(solution)/shard_map/pallas_call | solution.py:684
  352.3 0.0 all-reduce.4.cloned.1.call-update
  352.4 0.0 reduce-scatter.3.cloned.1.call-start
  352.4 0.5 reduce-scatter.3.cloned.1.call-update
  353.0 0.0 reduce-scatter.5.cloned.1.call-start
  353.0 151.1 %shard_map.241 = (bf16[1024,2048]{1,0:T(8,128)(2,1)}, f32[256,2048]{1,0:T(8,128)}, f32[8,2048]{1,0:T(8,128)}, bf16[2048,2048]{1,0:T(8,128)(2,1)}) custom-call(bf16[1024,2048]{1,0:T(8,128)(2,1)} %get-tuple-element.57.d_gate_hbm, bf16[1024,2048]{1,0:T(8,128)(2,1)} %get-tuple-element.58.d_up_hbm, bf16[2048,2048]{1,0:T(8,128)(2,1)} %w_gate_hbm.1, ...), custom_call_target="tpu_custom_call" | custom-call | flops 17179869184 | bytes 262144000 | tf_op jit(solution)/shard_map/pallas_call | solution.py:587
  504.1 5.7 fusion.16.d_mixed_ref
  509.9 8.3 %shard_map.242 = (f32[1024,512]{1,0:T(8,128)S(1)}, f32[4,136,128]{2,1,0:T(8,128)S(1)}, f32[4,8,128]{2,1,0:T(8,128)S(1)}) custom-call(f32[4]{0:T(128)S(1)} %add_divide_fusion.gate_ref, bf16[1024,512]{1,0:T(8,128)(2,1)S(1)} %copy-done.8, f32[1024,512]{1,0:T(8,128)S(1)} %copy-done.6, f32[4,136,128]{2,1,0:T(8,128)S(1)} %get-tuple-element.97.memory_ref, ...), custom_call_target="tpu_custom_call" | custom-call | flops 2415919104 | bytes 10485760 | tf_op jit(solution)/shard_map/pallas_call | solution.py:1108
  518.2 1.3 collective-permute-start.5
  519.5 1.3 collective-permute-start.4
  520.8 1.5 collective-permute-start.3
  522.4 15.9 %shard_map.243 = (bf16[1024,512]{1,0:T(8,128)(2,1)S(1)}, f32[1024,512]{1,0:T(8,128)S(1)}, f32[1024,512]{1,0:T(8,128)S(1)}) custom-call(f32[4]{0:T(128)S(1)} %add_divide_fusion.gate_ref, s32[1]{0:T(128)} %bitcast.valid_ref, bf16[1024,512]{1,0:T(8,128)(2,1)S(1)} %copy-done.8, bf16[1024,512]{1,0:T(8,128)(2,1)S(1)} %copy-done.12, ...), custom_call_target="tpu_custom_call" | custom-call | flops 5368709120 | bytes 14680064 | tf_op jit(solution)/shard_map/pallas_call | solution.py:1120
  538.3 0.1 select_add_fusion.memory_ref
  538.4 6.1 shard_map.244
  544.4 19.5 %shard_map.245 = (bf16[1024,2048]{1,0:T(8,128)(2,1)}, bf16[2048,512]{1,0:T(8,128)(2,1)}, bf16[2048,512]{1,0:T(8,128)(2,1)}, bf16[2048,512]{1,0:T(8,128)(2,1)}, b...) custom-call(bf16[1024,2048]{1,0:T(8,128)(2,1)} %copy-done.18, bf16[1024,2048]{1,0:T(8,128)(2,1)} %get-tuple-element.61.d_out_ref, ...), custom_call_target="tpu_custom_call" | custom-call | flops 15032385536 | bytes 31457280 | tf_op jit(solution)/shard_map/pallas_call | solution.py:836
  563.9 0.0 reduce-scatter.5.cloned.1.call-update
  564.0 1.2 copy-done.15
  565.1 0.3 fusion.10
  565.4 0.1 slice_reduce_fusion
  565.6 0.1 broadcast_select_fusion
  565.6 0.1 select_n.89
  565.8 0.6 slice_multiply_fusion.1
  566.3 0.7 fusion.11
  567.1 142.2 %shard_map.246 = (f32[40,128]{1,0:T(8,128)S(1)}, bf16[1536,2048]{1,0:T(8,128)(2,1)}, bf16[512,2048]{1,0:T(8,128)(2,1)S(1)}, bf16[2048,512]{1,0:T(8,128)(2,1)S(1)...) custom-call(f32[40,128]{1,0:T(8,128)S(1)} %fusion.12.refs_0_, bf16[1536,2048]{1,0:T(8,128)(2,1)} %get-tuple-element.73.refs_1_, ...), custom_call_target="tpu_custom_call" | custom-call | bytes 440401920 | tf_op jit(solution)/shard_map/pallas_call | solution.py:266
  709.3 1.3 copy-done.1
  710.7 0.6 dynamic_slice.7
  711.2 0.6 slice_bitcast_fusion
  711.9 1.6 copy-done
  713.4 1.6 copy-done.2
  715.0 1.6 copy-done.3
  716.7 1.6 copy-done.4
  718.3 30.8 %shard_map.247 = (f32[2048,2048]{1,0:T(8,128)}, f32[2048,2048]{1,0:T(8,128)}, f32[2048,2048]{1,0:T(8,128)}, f32[512,2048]{1,0:T(8,128)}, f32[2048,512]{1,0:T(8,1...) custom-call(bf16[2048,2048]{1,0:T(8,128)(2,1)} %get-tuple-element.94.refs_0_, bf16[512,2048]{1,0:T(8,128)(2,1)S(1)} %copy-done, ...), custom_call_target="tpu_custom_call" | custom-call | bytes 100663296 | tf_op jit(solution)/shard_map/pallas_call | solution.py:783
  749.1 0.0 reduce-scatter.3.cloned.1.call-done
  749.1 3.3 add_convert_fusion
  752.5 1.9 fusion.5
  754.3 1.6 fusion.9
  (59 shorter events, 0.2 us)
Async XLA Ops:
  7.2 1.6 copy-start.25
  7.2 2.9 copy-start.26
  7.2 85.9 %all-gather.3.cloned.1.call-start = ((), (), s32[]{:S(2)}) async-start(), calls=%async_computation.2 | async-start | bytes 5242880 | tf_op jit(solution)/shard_map/all_gather | solution.py:1054
  7.9 266.1 %all-gather.5.cloned.1.call-start = ((), (), s32[]{:S(2)}) async-start(), calls=%async_computation.3 | async-start | bytes 5242880 | tf_op jit(solution)/shard_map/all_gather | solution.py:1055
  8.7 703.2 %all-reduce.4.cloned.1.call-start = ((), (), s32[]{:S(2)}) async-start(), calls=%async_computation.6 | async-start | bytes 20971520 | tf_op jit(solution)/shard_map/psum | solution.py:1090
  10.1 86.3 %copy-start.20 = (f32[2048]{0:T(1024)S(1)}, f32[2048]{0:T(1024)}, u32[]{:S(2)}) copy-start(f32[2048]{0:T(1024)} %param.15) | copy-start | bytes 24580
  93.1 3.4 copy-start.16
  96.5 1.6 copy-start.24
  98.1 17.4 %copy-start.18 = (bf16[1024,2048]{1,0:T(8,128)(2,1)}, bf16[1024,2048]{1,0:T(8,128)(2,1)S(1)}, u32[]{:S(2)}) copy-start(bf16[1024,2048]{1,0:T(8,128)(2,1)S(1)} %fusion.2.rows_ref) | copy-start | bytes 12582916
  98.1 3.2 copy-start.23
  101.3 16.6 %copy-start.9 = (bf16[1024,512]{1,0:T(8,128)(2,1)}, bf16[1024,512]{1,0:T(8,128)(2,1)S(1)}, u32[]{:S(2)}) copy-start(bf16[1024,512]{1,0:T(8,128)(2,1)S(1)} %convolution_convert_fusion.value_ref) | copy-start | bytes 3145732
  103.7 14.2 %copy-start.11 = (bf16[1024,512]{1,0:T(8,128)(2,1)}, bf16[1024,512]{1,0:T(8,128)(2,1)S(1)}, u32[]{:S(2)}) copy-start(bf16[1024,512]{1,0:T(8,128)(2,1)S(1)} %convolution_convert_fusion.1.key_ref) | copy-start | bytes 3145732
  103.7 11.9 %copy-start.22 = (bf16[2048,512]{1,0:T(8,128)(2,1)S(1)}, bf16[2048,512]{1,0:T(8,128)(2,1)}, u32[]{:S(2)}) copy-start(bf16[2048,512]{1,0:T(8,128)(2,1)} %w_query_ref.1) | copy-start | bytes 6291460
  107.0 20.7 %collective-permute-start.2 = (f32[4,136,128]{2,1,0:T(8,128)S(1)}, f32[4,136,128]{2,1,0:T(8,128)S(1)}, u32[]{:S(2)}, u32[]{:S(2)}) collective-permute-start(f32[4,136,128]{2,1,0:T(8,128)S(1)} %shard_map.237), channel_id=1, source_target_pairs={{0,12},{4,16},{8,20},{12,24},{16,28},{1,13},{5,17},{9,21},{13,25},... | collective-permute-start | bytes 835592 | tf_op jit(solution)/shard_map/ppermute | solution.py:862
  109.8 17.9 %collective-permute-start.1 = (f32[4,136,128]{2,1,0:T(8,128)S(1)}, f32[4,136,128]{2,1,0:T(8,128)S(1)}, u32[]{:S(2)}, u32[]{:S(2)}) collective-permute-start(f32[4,136,128]{2,1,0:T(8,128)S(1)} %shard_map.237), channel_id=1, source_target_pairs={{0,8},{4,12},{8,16},{12,20},{16,24},{20,28},{1,9},{5,13},{9,17},{1... | collective-permute-start | bytes 835592 | tf_op jit(solution)/shard_map/ppermute | solution.py:862
  113.2 14.5 %collective-permute-start = (f32[4,136,128]{2,1,0:T(8,128)S(1)}, f32[4,136,128]{2,1,0:T(8,128)S(1)}, u32[]{:S(2)}, u32[]{:S(2)}) collective-permute-start(f32[4,136,128]{2,1,0:T(8,128)S(1)} %shard_map.237), channel_id=1, source_target_pairs={{0,4},{4,8},{8,12},{12,16},{16,20},{20,24},{24,28},{1,5},{5,9},{9,... | collective-permute-start | bytes 835592 | tf_op jit(solution)/shard_map/ppermute | solution.py:862
  117.9 9.8 %copy-start.7 = (bf16[1024,512]{1,0:T(8,128)(2,1)}, bf16[1024,512]{1,0:T(8,128)(2,1)S(1)}, u32[]{:S(2)}) copy-start(bf16[1024,512]{1,0:T(8,128)(2,1)S(1)} %convolution_convert_fusion.2.query_ref) | copy-start | bytes 3145732
  127.6 3.8 copy-start.5
  127.8 3.7 copy-start.13
  127.8 3.7 copy-start.14
  352.4 396.7 %reduce-scatter.3.cloned.1.call-start = ((), (), s32[]{:S(2)}) async-start(), calls=%async_computation.4 | async-start | bytes 5242880 | tf_op jit(solution)/shard_map/reduce_scatter | solution.py:1105
  353.0 399.5 %reduce-scatter.5.cloned.1.call-start = ((), (), s32[]{:S(2)}) async-start(), calls=%async_computation.5 | async-start | bytes 5242880 | tf_op jit(solution)/shard_map/reduce_scatter | solution.py:1148
  504.1 5.7 copy-start.6
  504.1 5.7 copy-start.8
  509.9 12.5 %copy-start.10 = (bf16[1024,512]{1,0:T(8,128)(2,1)S(1)}, bf16[1024,512]{1,0:T(8,128)(2,1)}, u32[]{:S(2)}) copy-start(bf16[1024,512]{1,0:T(8,128)(2,1)} %copy-done.9) | copy-start | bytes 3145732
  509.9 12.5 %copy-start.12 = (bf16[1024,512]{1,0:T(8,128)(2,1)S(1)}, bf16[1024,512]{1,0:T(8,128)(2,1)}, u32[]{:S(2)}) copy-start(bf16[1024,512]{1,0:T(8,128)(2,1)} %copy-done.11) | copy-start | bytes 3145732
  518.2 20.0 %collective-permute-start.5 = (f32[4,136,128]{2,1,0:T(8,128)S(1)}, f32[4,136,128]{2,1,0:T(8,128)S(1)}, u32[]{:S(2)}, u32[]{:S(2)}) collective-permute-start(f32[4,136,128]{2,1,0:T(8,128)S(1)} %get-tuple-element.66), channel_id=1, source_target_pairs={{12,0},{16,4},{20,8},{24,12},{28,16},{13,1},{17,5},{21,9},{25,13},... | collective-permute-start | bytes 835592 | tf_op jit(solution)/shard_map/ppermute | solution.py:862
  519.5 18.7 %collective-permute-start.4 = (f32[4,136,128]{2,1,0:T(8,128)S(1)}, f32[4,136,128]{2,1,0:T(8,128)S(1)}, u32[]{:S(2)}, u32[]{:S(2)}) collective-permute-start(f32[4,136,128]{2,1,0:T(8,128)S(1)} %get-tuple-element.66), channel_id=1, source_target_pairs={{8,0},{12,4},{16,8},{20,12},{24,16},{28,20},{9,1},{13,5},{17,9},{2... | collective-permute-start | bytes 835592 | tf_op jit(solution)/shard_map/ppermute | solution.py:862
  520.8 17.5 %collective-permute-start.3 = (f32[4,136,128]{2,1,0:T(8,128)S(1)}, f32[4,136,128]{2,1,0:T(8,128)S(1)}, u32[]{:S(2)}, u32[]{:S(2)}) collective-permute-start(f32[4,136,128]{2,1,0:T(8,128)S(1)} %get-tuple-element.66), channel_id=1, source_target_pairs={{4,0},{8,4},{12,8},{16,12},{20,16},{24,20},{28,24},{5,1},{9,5},{13... | collective-permute-start | bytes 835592 | tf_op jit(solution)/shard_map/ppermute | solution.py:862
  563.9 1.2 copy-start.15
  563.9 1.8 copy-start.21
  709.3 1.3 copy-start.1
  711.8 1.6 copy-start
  713.4 1.6 copy-start.2
  715.0 1.6 copy-start.3
  716.7 1.6 copy-start.4
  749.1 5.2 copy-start.19
  752.4 1.9 copy-start.17
Sparse Core Ops, SparseCore 0:
  9.6 83.4 all-gather.2
  94.7 108.8 all-gather.4
  352.5 211.7 all-reduce.3
  566.5 80.7 reduce-scatter.2
  649.5 77.2 reduce-scatter.4

commit v2 on v1

--- a/solution.py
+++ b/solution.py
@@ -10,7 +10,7 @@
 DH = 128
 SEG_LEN = 1024
 SEGS = 4
-MEM_ROWS = DH + 8
+MEM_ROWS = DH + 16
 BLOCK = 256
 
 epsilon = 1e-05
@@ -287,6 +287,7 @@
 HOP = 2
 SEND_SLOTS = 4
 BLOCK_ROWS = 256
+UNIT_GROUP = 512
 LINE_REFS = 8
 
 
@@ -440,21 +441,77 @@
 
 
 def attn_out_kernel(
-    mixed_ref, weight_ref, token_ref, gain_ref, hidden_ref, normed_ref,
-    hidden, normed, hidden_sem, normed_sem, *scratch
+    mixed_ref, weight_ref, token_ref, gain_ref, w_gate_hbm, w_up_hbm,
+    hidden_ref, normed_ref, silu_ref, slope_ref, act_ref,
+    hidden, normed, w_gate, w_up, silu, slope, act,
+    hidden_sem, normed_sem, load_sem, out_sem, *scratch
 ):
+    loads = [
+        pltpu.make_async_copy(source, target, load_sem.at[i])
+        for i, (source, target) in enumerate(((w_gate_hbm, w_gate), (w_up_hbm, w_up)))
+    ]
+    for load in loads:
+        load.start()
     line_barrier()
     per_block = BLOCK_ROWS // ROWS
     blocks = hidden.shape[0] // BLOCK_ROWS
+    groups = w_gate.shape[1] // UNIT_GROUP
+    slots = act.shape[0]
+    lag = per_block + (lax.axis_size("head") - 1) * HOP
+    pace = per_block // groups
 
     def block_rows(b):
         return pl.ds(pl.multiple_of(b * BLOCK_ROWS, BLOCK_ROWS), BLOCK_ROWS)
 
+    def unit_copies(u):
+        slot = lax.rem(u, slots)
+        where = (block_rows(u // groups), unit_cols(u))
+        return [
+            pltpu.make_async_copy(source.at[slot], target.at[where], out_sem.at[i, slot])
+            for i, (source, target) in enumerate(
+                ((silu, silu_ref), (slope, slope_ref), (act, act_ref))
+            )
+        ]
+
+    def unit_cols(u):
+        return pl.ds(pl.multiple_of(lax.rem(u, groups) * UNIT_GROUP, UNIT_GROUP), UNIT_GROUP)
+
+    def forward(u):
+        slot = lax.rem(u, slots)
+
+        @pl.when(u >= slots)
+        def _():
+            for copy in unit_copies(u - slots):
+                copy.wait()
+
+        rows, cols = normed[block_rows(u // groups)], unit_cols(u)
+        gate_pre = dot(rows, w_gate[:, cols], NN)
+        up_proj = dot(rows, w_up[:, cols], NN)
+        gate_sig = jax.nn.sigmoid(gate_pre)
+        silu_gate = gate_pre * gate_sig
+        silu[slot] = silu_gate
+        slope[slot] = up_proj * gate_sig * (1.0 + gate_pre * (1.0 - gate_sig))
+        act[slot] = (silu_gate * up_proj).astype(BF16)
+        for copy in unit_copies(u):
+            copy.start()
+
     def before(t):
         @pl.when((lax.rem(t, per_block) == 0) & (t < blocks * per_block))
         def _():
             rows = block_rows(t // per_block)
             hidden[rows] = dot(mixed_ref[rows], weight_ref[...], NN)
+
+    def after(t):
+        @pl.when(t == lag)
+        def _():
+            for load in loads:
+                load.wait()
+
+        late = t - lag
+
+        @pl.when((late >= 0) & (lax.rem(late, pace) == 0) & (late // pace < blocks * groups))
+        def _():
+            forward(late // pace)
 
     def stores(b):
         rows = block_rows(b)
@@ -474,35 +531,54 @@
             for copy in stores(k // per_block):
                 copy.start()
 
-    line_exchange(hidden, finish, before, scratch)
+    line_exchange(hidden, finish, before, scratch, after, lag + blocks * per_block)
     for b in range(blocks):
         for copy in stores(b):
             copy.wait()
-
-
-def attn_out_sum(mixed, weight, tokens, gain, size, cid):
+    for u in range(blocks * groups - slots, blocks * groups):
+        for copy in unit_copies(u):
+            copy.wait()
+
+
+def attn_out_sum(mixed, weight, tokens, gain, w_gate, w_up, size, cid):
     rows, width = tokens.shape
-    vmem, any_ = pl.BlockSpec(memory_space=pltpu.VMEM), pl.BlockSpec(memory_space=pl.ANY)
-    blocks = rows // BLOCK_ROWS
+    units = w_gate.shape[1]
+    vmem, any_ = pl.BlockSpec(memory_space=pltpu.VMEM), pl.BlockSpec(memory_space=pltpu.HBM)
+    blocks, slots = rows // BLOCK_ROWS, 2
     return pl.pallas_call(
         attn_out_kernel,
-        in_specs=[vmem] * 4,
-        out_specs=[any_] * 2,
-        out_shape=[jax.ShapeDtypeStruct((rows, width), F32), jax.ShapeDtypeStruct((rows, width), BF16)],
+        in_specs=[vmem] * 4 + [any_] * 2,
+        out_specs=[any_] * 5,
+        out_shape=[
+            jax.ShapeDtypeStruct((rows, width), F32),
+            jax.ShapeDtypeStruct((rows, width), BF16),
+            jax.ShapeDtypeStruct((rows, units), F32),
+            jax.ShapeDtypeStruct((rows, units), F32),
+            jax.ShapeDtypeStruct((rows, units), BF16),
+        ],
         scratch_shapes=[
             pltpu.VMEM((rows, width), F32),
             pltpu.VMEM((rows, width), BF16),
+            pltpu.VMEM((width, units), BF16),
+            pltpu.VMEM((width, units), BF16),
+            pltpu.VMEM((slots, BLOCK_ROWS, UNIT_GROUP), F32),
+            pltpu.VMEM((slots, BLOCK_ROWS, UNIT_GROUP), F32),
+            pltpu.VMEM((slots, BLOCK_ROWS, UNIT_GROUP), BF16),
             pltpu.SemaphoreType.DMA((blocks,)),
             pltpu.SemaphoreType.DMA((blocks,)),
+            pltpu.SemaphoreType.DMA((2,)),
+            pltpu.SemaphoreType.DMA((3, slots)),
         ]
         + line_scratch(size, width),
         cost_estimate=pl.CostEstimate(
-            flops=2 * rows * width * mixed.shape[1], bytes_accessed=150 * 2**20, transcendentals=0
+            flops=2 * rows * width * (mixed.shape[1] + 2 * units),
+            bytes_accessed=250 * 2**20,
+            transcendentals=rows * units,
         ),
         compiler_params=pltpu.CompilerParams(
-            collective_id=cid, has_side_effects=True, vmem_limit_bytes=48 * 2**20
+            collective_id=cid, has_side_effects=True, vmem_limit_bytes=60 * 2**20
         ),
-    )(mixed, weight, tokens, gain.reshape(1, width))
+    )(mixed, weight, tokens, gain.reshape(1, width), w_gate, w_up)
 
 
 def mlp_back_kernel(
@@ -617,50 +693,33 @@
 
 
 MLP_BLOCK = 256
-MLP_ROWS = 1024
 
 
 def mlp_kernel(
-    rows_ref, grad_ref, w_gate_ref, w_up_ref, w_down_ref,
+    rows_ref, grad_ref, silu_ref, slope_ref, act_ref, w_down_ref,
     d_gate_ref, d_up_ref, grad_gate_ref, grad_up_top, grad_up_low, grad_down_ref, out_ref,
-    flipped, act, total,
+    flipped, total,
 ):
-    count, width = rows_ref.shape
+    width = rows_ref.shape[1]
     first = pl.program_id(0) == 0
     last = pl.program_id(0) == pl.num_programs(0) - 1
+    half = width // 2
 
     @pl.when(first)
     def _():
         total[...] = jnp.zeros_like(total)
-
-        @pl.loop(0, width // MLP_ROWS)
-        def _(i):
-            part = pl.ds(pl.multiple_of(i * MLP_ROWS, MLP_ROWS), MLP_ROWS)
+        for i in range(2):
+            part = slice(i * half, (i + 1) * half)
             flipped[part] = rows_ref[:, part].T
 
-    @pl.loop(0, count // MLP_ROWS)
-    def _(i):
-        part = pl.ds(pl.multiple_of(i * MLP_ROWS, MLP_ROWS), MLP_ROWS)
-        rows = rows_ref[part]
-        gate_pre = dot(rows, w_gate_ref[...], NN)
-        up_proj = dot(rows, w_up_ref[...], NN)
-        d_act = dot(grad_ref[part], w_down_ref[...], NT)
-        gate_sig = jax.nn.sigmoid(gate_pre)
-        silu_gate = gate_pre * gate_sig
-        activation = (silu_gate * up_proj).astype(BF16)
-        act[part] = activation
-        d_gate_ref[part] = (
-            d_act * up_proj * gate_sig * (1.0 + gate_pre * (1.0 - gate_sig))
-        ).astype(BF16)
-        d_up_ref[part] = (d_act * silu_gate).astype(BF16)
-        total[part] += dot(activation, w_down_ref[...], NN)
-
-    @pl.loop(0, width // MLP_ROWS)
-    def _(i):
-        part = pl.ds(pl.multiple_of(i * MLP_ROWS, MLP_ROWS), MLP_ROWS)
+    d_act = dot(grad_ref[...], w_down_ref[...], NT)
+    d_gate_ref[...] = (d_act * slope_ref[...]).astype(BF16)
+    d_up_ref[...] = (d_act * silu_ref[...]).astype(BF16)
+    total[...] += dot(act_ref[...], w_down_ref[...], NN)
+    for i in range(2):
+        part = slice(i * half, (i + 1) * half)
         grad_gate_ref[part] = dot(flipped[part], d_gate_ref[...], NN).astype(BF16)
-        grad_down_ref[:, part] = dot(act[...], grad_ref[:, part], TN).astype(BF16)
-
+        grad_down_ref[:, part] = dot(act_ref[...], grad_ref[:, part], TN).astype(BF16)
     top = grad_up_top.shape[0]
     grad_up_top[...] = dot(flipped[:top], d_up_ref[...], NN).astype(BF16)
     grad_up_low[...] = dot(flipped[top:], d_up_ref[...], NN).astype(BF16)
@@ -670,9 +729,9 @@
         out_ref[...] = total[...].astype(BF16)
 
 
-def mlp_both(rows, grad, w_gate, w_up, w_down):
+def mlp_both(rows, grad, silu, slope, act, w_down):
     count, width = rows.shape
-    units = w_gate.shape[1]
+    units = act.shape[1]
     block = min(MLP_BLOCK, units)
     once = pl.Buffered(1)
     whole = pl.BlockSpec((count, width), lambda j: (0, 0), pipeline_mode=once)
@@ -684,7 +743,7 @@
     return pl.pallas_call(
         mlp_kernel,
         grid=(units // block,),
-        in_specs=[whole, whole, tall, tall, wide],
+        in_specs=[whole, whole, side, side, side, wide],
         out_specs=[side, side, tall, *parts, wide, whole],
         out_shape=[
             jax.ShapeDtypeStruct((count, units), BF16),
@@ -695,18 +754,14 @@
             jax.ShapeDtypeStruct((units, width), BF16),
             jax.ShapeDtypeStruct((count, width), BF16),
         ],
-        scratch_shapes=[
-            pltpu.VMEM((width, count), BF16),
-            pltpu.VMEM((count, block), BF16),
-            pltpu.VMEM((count, width), F32),
-        ],
+        scratch_shapes=[pltpu.VMEM((width, count), BF16), pltpu.VMEM((count, width), F32)],
         cost_estimate=pl.CostEstimate(
-            flops=14 * count * width * units,
-            bytes_accessed=2 * (3 * count * width + 6 * width * units + 2 * count * units),
-            transcendentals=count * units,
+            flops=10 * count * width * units,
+            bytes_accessed=2 * (3 * count * width + 4 * width * units + 7 * count * units),
+            transcendentals=0,
         ),
         compiler_params=pltpu.CompilerParams(vmem_limit_bytes=56 * 2**20),
-    )(rows, grad, w_gate, w_up, w_down)
+    )(rows, grad, silu, slope, act, w_down)
 
 
 WIDEN_SLOTS = 4
@@ -899,12 +954,13 @@
 def update_kernel(valid_ref, key_ref, value_ref, out_ref):
     key_feat = elu_plus(key_ref[...].astype(F32)) * valid_column(valid_ref[0])
     out_ref[0, :DH] = dot(key_feat, value_ref[...].astype(F32), TN, highest)
-    out_ref[0, DH:] = jnp.broadcast_to(jnp.sum(key_feat, axis=0, keepdims=True), (8, DH))
-
-
-def block_probs(query_block, key_ref, start, valid_len):
-    cols = start + query_block.shape[0]
-    scores = dot(query_block, key_ref[:cols], NT) * (DH**-0.5)
+    out_ref[0, DH:] = jnp.broadcast_to(
+        jnp.sum(key_feat, axis=0, keepdims=True), (MEM_ROWS - DH, DH)
+    )
+
+
+def block_probs(query_block, key_rows, start, valid_len):
+    scores = dot(query_block, key_rows, NT) * (DH**-0.5)
     row_pos = start + lax.broadcasted_iota(jnp.int32, scores.shape, 0)
     col_pos = lax.broadcasted_iota(jnp.int32, scores.shape, 1)
     allowed = (row_pos >= col_pos) & (col_pos < valid_len)
@@ -916,7 +972,8 @@
 def local_kernel(valid_ref, query_ref, key_ref, value_ref, out_ref):
     for start in range(0, SEG_LEN, BLOCK):
         rows = slice(start, start + BLOCK)
-        probs = block_probs(query_ref[rows], key_ref, start, valid_ref[0])
+        key_rows = key_ref[: start + BLOCK]
+        probs = block_probs(query_ref[rows], key_rows, start, valid_ref[0])
         out_ref[rows] = dot(probs.astype(BF16), value_ref[: start + BLOCK], NN)
 
 
@@ -933,74 +990,162 @@
     out_ref[...] = (gate * retrieved + (1.0 - gate) * local_ref[...]).astype(BF16)
 
 
-def memory_back_kernel(
-    gate_ref, query_ref, local_ref, memory_ref, d_mixed_ref, feat_ref, back_ref, gate_grad_ref
+def greet_sequence():
+    seg = lax.axis_index("seg")
+    place = lax.rem(seg, SEGS)
+    barrier = pltpu.get_barrier_semaphore()
+    for distance in range(1, SEGS):
+        other = seg - place + lax.rem(place + distance, SEGS)
+        pl.semaphore_signal(barrier, inc=1, device_id={"seg": other}, device_id_type=MESH)
+    pl.semaphore_wait(barrier, SEGS - 1)
+
+
+def sequence_copies(source, land, send_sem, recv_sem, sign):
+    seg = lax.axis_index("seg")
+    count = lax.axis_size("seg")
+    place = lax.rem(seg, SEGS)
+    copies = []
+    for distance in range(1, SEGS):
+        copy = pltpu.make_async_remote_copy(
+            src_ref=source,
+            dst_ref=land.at[distance - 1],
+            send_sem=send_sem.at[distance - 1],
+            recv_sem=recv_sem.at[distance - 1],
+            device_id={"seg": lax.rem(seg + count + sign * distance, count)},
+            device_id_type=MESH,
+        )
+        after, before = place + distance < SEGS, place >= distance
+        copies.append((copy, after, before) if sign > 0 else (copy, before, after))
+    return copies
+
+
+def head_cols(head):
+    return pl.ds(pl.multiple_of(head * DH, DH), DH)
+
+
+def attn_back_kernel(
+    gate_ref, valid_ref, d_out_ref, weight_ref, query_ref, key_ref, value_ref, local_ref, memory_ref,
+    d_query_ref, d_key_ref, d_value_ref, gate_grad_ref,
+    d_mixed, feat, d_key_sum, d_value_sum, back, land, update, send_sem, recv_sem,
 ):
-    gate = gate_ref[pl.program_id(0)]
-    query_vals = query_ref[...].astype(F32)
-    query_feat = elu_plus(query_vals)
-    memory, normal = memory_ref[0, :DH], memory_ref[0, DH : DH + 1]
-    retrieved, denominator = retrieve(query_feat, memory, normal)
-    d_mixed = d_mixed_ref[...]
-    gate_grad_ref[0] = jnp.broadcast_to(
-        jnp.sum(d_mixed * (retrieved - local_ref[...]), axis=0, keepdims=True), (8, DH)
-    )
-    d_retrieved = gate * d_mixed
-    d_numerator = d_retrieved / denominator
-    d_denominator = -jnp.sum(d_retrieved * retrieved, axis=-1, keepdims=True) / denominator
-    d_feat = dot(d_numerator, memory, NT, highest) + d_denominator * normal
-    feat_ref[...] = d_feat * elu_slope(query_vals)
-    back_ref[0, :DH] = dot(query_feat, d_numerator, TN, highest)
-    back_ref[0, DH:] = jnp.broadcast_to(
-        jnp.sum(d_denominator * query_feat, axis=0, keepdims=True), (8, DH)
-    )
-
-
-def local_back_kernel(
-    gate_ref,
-    valid_ref,
-    query_ref,
-    key_ref,
-    value_ref,
-    d_mixed_ref,
-    feat_ref,
-    d_query_ref,
-    d_key_ref,
-    d_value_ref,
-):
-    keep = 1.0 - gate_ref[pl.program_id(0)]
-    d_key_ref[...] = jnp.zeros_like(d_key_ref)
-    d_value_ref[...] = jnp.zeros_like(d_value_ref)
-    for start in range(0, SEG_LEN, BLOCK):
-        rows = slice(start, start + BLOCK)
-        cols = slice(0, start + BLOCK)
-        query_block = query_ref[rows]
-        probs = block_probs(query_block, key_ref, start, valid_ref[0])
-        d_local = (keep * d_mixed_ref[rows]).astype(BF16)
-        d_probs = dot(d_local, value_ref[cols], NT)
-        row_dot = jnp.sum(probs * d_probs, axis=-1, keepdims=True)
-        d_scores = (probs * (d_probs - row_dot) * (DH**-0.5)).astype(BF16)
-        d_query_ref[rows] = (dot(d_scores, key_ref[cols], NN) + feat_ref[rows]).astype(BF16)
-        d_key_ref[cols] += dot(d_scores, query_block, TN)
-        d_value_ref[cols] += dot(probs.astype(BF16), d_local, TN)
-
-
-def finish_back_kernel(
-    valid_ref, key_ref, value_ref, d_key_in, d_value_in, memory_ref, d_key_ref, d_value_ref
-):
-    valid = valid_column(valid_ref[0])
-    key_vals = key_ref[...].astype(F32)
-    memory, normal = memory_ref[0, :DH], memory_ref[0, DH : DH + 1]
-    d_feat = (dot(value_ref[...].astype(F32), memory, NT, highest) + normal) * valid
-    d_key_ref[...] = (d_key_in[...] + d_feat * elu_slope(key_vals)).astype(BF16)
-    key_feat = elu_plus(key_vals) * valid
-    d_value_ref[...] = (d_value_in[...] + dot(key_feat, memory, NN, highest)).astype(BF16)
+    heads = memory_ref.shape[0]
+    valid_len = valid_ref[0]
+    greet_sequence()
+    copies = sequence_copies(back, land, send_sem, recv_sem, -1)
+    d_mixed[...] = dot(d_out_ref[...], weight_ref[...], NT)
+
+    def memory_back(head, carry):
+        cols = head_cols(head)
+        gate = gate_ref[head]
+        query_vals = query_ref[:, cols].astype(F32)
+        query_feat = elu_plus(query_vals)
+        memory, normal = memory_ref[head, :DH], memory_ref[head, DH : DH + 1]
+        retrieved, denominator = retrieve(query_feat, memory, normal)
+        d_head = d_mixed[:, cols]
+        gate_grad_ref[head] = jnp.broadcast_to(
+            jnp.sum(d_head * (retrieved - local_ref[:, cols]), axis=0, keepdims=True), (8, DH)
+        )
+        d_retrieved = gate * d_head
+        d_numerator = d_retrieved / denominator
+        d_denominator = -jnp.sum(d_retrieved * retrieved, axis=-1, keepdims=True) / denominator
+        d_feat = dot(d_numerator, memory, NT, highest) + d_denominator * normal
+        feat[:, cols] = d_feat * elu_slope(query_vals)
+        back[head, :DH] = dot(query_feat, d_numerator, TN, highest).astype(BF16)
+        d_normal = jnp.sum(d_denominator * query_feat, axis=0, keepdims=True)
+        back[head, DH:] = jnp.broadcast_to(d_normal, (MEM_ROWS - DH, DH)).astype(BF16)
+        return carry
+
+    lax.fori_loop(0, heads, memory_back, 0)
+    for copy, sends, _ in copies:
+
+        @pl.when(sends)
+        def _(copy=copy):
+            copy.start()
+
+    d_key_sum[...] = jnp.zeros_like(d_key_sum)
+    d_value_sum[...] = jnp.zeros_like(d_value_sum)
+
+    def local_back(head, carry):
+        cols = head_cols(head)
+        keep = 1.0 - gate_ref[head]
+        for start in range(0, SEG_LEN, BLOCK):
+            rows, seen = slice(start, start + BLOCK), slice(0, start + BLOCK)
+            query_block = query_ref[rows, cols]
+            probs = block_probs(query_block, key_ref[seen, cols], start, valid_len)
+            d_local = (keep * d_mixed[rows, cols]).astype(BF16)
+            d_probs = dot(d_local, value_ref[seen, cols], NT)
+            row_dot = jnp.sum(probs * d_probs, axis=-1, keepdims=True)
+            d_scores = (probs * (d_probs - row_dot) * (DH**-0.5)).astype(BF16)
+            d_query = dot(d_scores, key_ref[seen, cols], NN) + feat[rows, cols]
+            d_query_ref[rows, cols] = d_query.astype(BF16)
+            d_key_sum[seen, cols] += dot(d_scores, query_block, TN)
+            d_value_sum[seen, cols] += dot(probs.astype(BF16), d_local, TN)
+        return carry
+
+    lax.fori_loop(0, heads, local_back, 0)
+    update[...] = jnp.zeros_like(update)
+    for distance, (copy, sends, gets) in enumerate(copies):
+
+        @pl.when(sends)
+        def _(copy=copy):
+            copy.wait_send()
+
+        @pl.when(gets)
+        def _(copy=copy, distance=distance):
+            copy.wait_recv()
+            update[...] += land[distance].astype(F32)
+
+    def finish_back(head, carry):
+        cols = head_cols(head)
+        valid = valid_column(valid_len)
+        key_vals = key_ref[:, cols].astype(F32)
+        memory, normal = update[head, :DH], update[head, DH : DH + 1]
+        d_feat = (dot(value_ref[:, cols].astype(F32), memory, NT, highest) + normal) * valid
+        d_key_ref[:, cols] = (d_key_sum[:, cols] + d_feat * elu_slope(key_vals)).astype(BF16)
+        key_feat = elu_plus(key_vals) * valid
+        d_value = d_value_sum[:, cols] + dot(key_feat, memory, NN, highest)
+        d_value_ref[:, cols] = d_value.astype(BF16)
+        return carry
+
+    lax.fori_loop(0, heads, finish_back, 0)
+
+
+def attn_back(gate, valid, d_out, weight, query, key, value, local, memory, cid):
+    rows, cols = query.shape
+    heads = cols // DH
+    scalar, vmem = pl.BlockSpec(memory_space=pltpu.SMEM), pl.BlockSpec(memory_space=pltpu.VMEM)
+    wide = pltpu.VMEM((rows, cols), F32)
+    narrow = jax.ShapeDtypeStruct((rows, cols), BF16)
+    return pl.pallas_call(
+        attn_back_kernel,
+        in_specs=[scalar] * 2 + [vmem] * 7,
+        out_specs=[vmem] * 4,
+        out_shape=[narrow, narrow, narrow, jax.ShapeDtypeStruct((heads, 8, DH), F32)],
+        scratch_shapes=[
+            wide,
+            wide,
+            wide,
+            wide,
+            pltpu.VMEM((heads, MEM_ROWS, DH), BF16),
+            pltpu.VMEM((SEGS - 1, heads, MEM_ROWS, DH), BF16),
+            pltpu.VMEM((heads, MEM_ROWS, DH), F32),
+            pltpu.SemaphoreType.DMA((SEGS - 1,)),
+            pltpu.SemaphoreType.DMA((SEGS - 1,)),
+        ],
+        cost_estimate=pl.CostEstimate(
+            flops=10 * rows * rows * cols + 2 * rows * cols * d_out.shape[1],
+            bytes_accessed=100 * 2**20,
+            transcendentals=rows * rows * heads,
+        ),
+        compiler_params=pltpu.CompilerParams(
+            collective_id=cid, has_side_effects=True, vmem_limit_bytes=48 * 2**20
+        ),
+    )(gate, valid, d_out, weight, query, key, value, local, memory)
 
 
 SCALAR = pl.BlockSpec(memory_space=pltpu.SMEM)
 COLUMN = pl.BlockSpec((SEG_LEN, DH), lambda head: (0, head))
 MEMORY = pl.BlockSpec((1, MEM_ROWS, DH), lambda head: (head, 0, 0))
-SMALL = pl.BlockSpec((1, 8, DH), lambda head: (head, 0, 0))
 
 
 def per_head(kernel, heads, in_specs, out_specs, out_types, flops, transcendentals=0):
@@ -1046,7 +1191,6 @@
     col_f32 = jax.ShapeDtypeStruct((SEG_LEN, cols), F32)
     col_bf16 = jax.ShapeDtypeStruct((SEG_LEN, cols), BF16)
     mem_f32 = jax.ShapeDtypeStruct((heads, MEM_ROWS, DH), F32)
-    small_f32 = jax.ShapeDtypeStruct((heads, 8, DH), F32)
     unit = 2 * heads * SEG_LEN * DH * DH
     pairs = heads * SEG_LEN * SEG_LEN
 
@@ -1079,13 +1223,13 @@
     mixed_attn = per_head(
         mix_kernel, heads, [SCALAR, COLUMN, COLUMN, MEMORY], COLUMN, col_bf16, 6 * unit
     )(mix_sig, query_rows, local_attn, memory_prev)
-    all_hidden, gathered_mlp = attn_out_sum(
-        mixed_attn, w_out, gathered_tokens, gain_mlp, head_groups, 1
+    all_hidden, gathered_mlp, silu, slope, act = attn_out_sum(
+        mixed_attn, w_out, gathered_tokens, gain_mlp, w_gate, w_up, head_groups, 1
     )
     own_rows = tokens.shape[0]
     hidden_res = lax.dynamic_slice_in_dim(all_hidden, head_index * own_rows, own_rows, 0)
     d_gate, d_up, grad_gate, up_top, up_low, grad_down, mlp_part = mlp_both(
-        gathered_mlp, gathered_grad, w_gate, w_up, w_down
+        gathered_mlp, gathered_grad, silu, slope, act, w_down
     )
     sum_gate, sum_up_top = lax.psum((grad_gate, up_top), "seg")
     gathered_hidden, d_hidden, gain_mlp_rows, summed_down = mlp_back_sum(
@@ -1104,36 +1248,18 @@
     )
     mlp_out = lax.psum_scatter(mlp_part, "head", scatter_dimension=0, tiled=True)
     output = (hidden_res + mlp_out.astype(F32)).astype(BF16)
-    d_mixed = dot(gathered_hidden, w_out, NT)
-    feat_grad, back, gate_cols = per_head(
-        memory_back_kernel,
-        heads,
-        [SCALAR, COLUMN, COLUMN, MEMORY, COLUMN],
-        [COLUMN, MEMORY, SMALL],
-        [col_f32, mem_f32, small_f32],
-        18 * unit,
-    )(mix_sig, query_rows, local_attn, memory_prev, d_mixed)
-    back_update = jnp.zeros_like(back)
-    for distance in range(1, SEGS):
-        moved = from_behind(back, "seg", -distance)
-        back_update = back_update + jnp.where(position + distance <= SEGS - 1, moved, 0.0)
-    d_queries, key_local, value_local = per_head(
-        local_back_kernel,
-        heads,
-        [SCALAR, SCALAR] + [COLUMN] * 5,
-        [COLUMN] * 3,
-        [col_bf16, col_f32, col_f32],
-        10 * pairs * DH,
-        pairs,
-    )(mix_sig, valid_len, query_rows, key_rows, value_rows, d_mixed, feat_grad)
-    d_keys, d_values = per_head(
-        finish_back_kernel,
-        heads,
-        [SCALAR] + [COLUMN] * 4 + [MEMORY],
-        [COLUMN] * 2,
-        [col_bf16, col_bf16],
-        12 * unit,
-    )(valid_len, key_rows, value_rows, key_local, value_local, back_update)
+    d_queries, d_keys, d_values, gate_cols = attn_back(
+        mix_sig,
+        valid_len,
+        gathered_hidden,
+        w_out,
+        query_rows,
+        key_rows,
+        value_rows,
+        local_attn,
+        memory_prev,
+        3,
+    )
     d_part, grad_query, grad_key, grad_value, grad_out, gain_attn_rows = attn_weights(
         gathered_attn,
         gathered_hidden,

time: 771 us -> 739 us (0.958)
  Pallas kernels: 611 us -> 588 us
    pallas_call x1, Pallas kernels: 78.3 us -> 55.9 us  [mlp_both(): pl.pallas_call(mlp_kernel, grid=(units // block,), in_specs=[whole, whole...]
    pallas_call x1, Pallas kernels: 142 us -> 130 us  [grad_sum(): pl.pallas_call(functools.partial(grad_sum_kernel, count, tile, seg_bits,...]
    pallas_call x4 -> x2, Pallas kernels: 173 us -> 183 us  [the longest x1 147 us: attn_out_sum(): pl.pallas_call(attn_out_kernel, in_specs=[vmem] * 4 + [any_] * 2, out_spe...]
  transfers between devices with their start and end apart: 11 -> 8, of which waited for: 1 -> 1; matrix products, arithmetic and copies ran while one was open for 3% -> 2% of each run, Pallas kernels for 70% -> 73%
where the time goes in v2:
time: 739 us; the launch traced here: 731 us
  Pallas kernels  588 us (80%)
  waiting for transfers between devices  85 us (12%)
  between operations  15.3 us (2%)
  other arithmetic  13.6 us (2%)
  local copies, waits for them, and re-layouts  13.5 us (2%)
  starting transfers between devices  8.73 us (1%)
    pallas_call x1, Pallas kernels, mlp_back_sum(): pl.pallas_call(functools.partial(mlp_back_kernel, tile, seg_bits), in_spe...  152 us
    pallas_call x1, Pallas kernels, attn_out_sum(): pl.pallas_call(attn_out_kernel, in_specs=[vmem] * 4 + [any_] * 2, out_spe...  147 us
    pallas_call x1, Pallas kernels, grad_sum(): pl.pallas_call(functools.partial(grad_sum_kernel, count, tile, seg_bits,...  130 us
    all_gather x1, waiting for transfers between devices, per_device(): gathered_tokens = lax.all_gather(tokens, 'head', axis=0, tiled=True)  83 us
    pallas_call x1, Pallas kernels, mlp_both(): pl.pallas_call(mlp_kernel, grid=(units // block,), in_specs=[whole, whole...  55.9 us
    pallas_call x1, Pallas kernels, attn_back(): pl.pallas_call(attn_back_kernel, in_specs=[scalar] * 2 + [vmem] * 7, out_...  35.7 us
    pallas_call x1, Pallas kernels, widen(): pl.pallas_call(functools.partial(widen_kernel, shapes, places, len(target...  30.8 us
    pallas_call x1, Pallas kernels, attn_weights(): pl.pallas_call(attn_weights_kernel, grid=(width // block,), in_specs=[sid...  19.5 us
  transfers between devices with their start and end apart: 8, of which 1 were waited for; matrix products, arithmetic and copies ran while one was open for 2% of the time, Pallas kernels for 73%

profile of v2, /device:TPU:0, one launch (start us, length us, event | category | flops | bytes accessed | tf_op | source)
XLA Modules:
  0.0 730.7 jit_solution(2116939382097527408)
XLA Ops:
  7.2 0.0 all-gather.3.cloned.1.call-start
  7.2 0.7 all-gather.3.cloned.1.call-update
  7.9 0.0 all-gather.5.cloned.1.call-start
  8.0 0.7 all-gather.5.cloned.1.call-update
  8.7 0.0 all-reduce.4.cloned.1.call-start
  8.8 0.6 fusion.14
  10.1 0.0 copy-start.16
  10.1 83.0 %all-gather.3.cloned.1.call-done.token_ref = bf16[1024,2048]{1,0:T(8,128)(2,1)} async-done(((bf16[256,2048]{1,0:T(8,128)(2,1)}), bf16[1024,2048]{1,0:T(8,128)(2,1)}) %all-gather.3.cloned.1.call-update) | async-done | bytes 4194320 | tf_op jit(solution)/shard_map/all_gather | solution.py:1198
  93.1 3.2 fusion
  96.3 0.2 copy-done.12
  96.5 1.0 fusion.2.rows_ref
  97.6 0.6 copy-done.20
  98.1 2.3 convolution_convert_fusion.value_ref
  100.5 0.9 copy-done.19
  101.3 2.3 convolution_convert_fusion.1.key_ref
  103.7 0.0 copy-start.9
  103.7 0.0 copy-start.18
  103.7 3.3 shard_map.237
  107.0 2.8 collective-permute-start.2
  109.8 3.4 collective-permute-start.1
  113.2 2.3 collective-permute-start
  115.6 2.3 convolution_convert_fusion.2.query_ref
  117.9 9.7 %shard_map.236.local_ref = f32[1024,512]{1,0:T(8,128)S(1)} custom-call(s32[1]{0:T(128)} %bitcast.valid_ref, bf16[1024,512]{1,0:T(8,128)(2,1)S(1)} %convolution_convert_fusion.2.query_ref, bf16[1024,512]{1,0:T(8,128)(2,1)S(1)} %convolution_convert_fusion.1.key_ref, bf16[1024,512]{1,0:T(8,128)(2,1)S(1)} %convolution_convert_fusion.value_ref), custom_call_target="tpu_custom_call" | custom-call | flops 2147483648 | bytes 8388608 | tf_op jit(solution)/shard_map/pallas_call | solution.py:1216
  127.6 0.0 collective-permute-done.2
  127.7 0.1 fusion.15
  127.7 3.6 shard_map.238.mixed_ref
  131.4 0.0 copy-start.6
  131.4 1.0 copy-done.6
  132.4 147.1 %shard_map.239 = (f32[1024,2048]{1,0:T(8,128)}, bf16[1024,2048]{1,0:T(8,128)(2,1)}, f32[1024,2048]{1,0:T(8,128)}, f32[1024,2048]{1,0:T(8,128)}, bf16[1024,2048]{1,0:T(8,128)(2,1)}) custom-call(bf16[1024,512]{1,0:T(8,128)(2,1)} %copy-done.6, bf16[512,2048]{1,0:T(8,128)(2,1)} %weight_ref.3, bf16[1024,2048]{1,0:T(8,128)(2,1)} %all-gather.3.cloned.1.call-done.token_ref, ...), custom_call_target="tpu_custom_call" | custom-call | flops 19327352832 | bytes 262144000 | tf_op jit(solution)/shard_map/pallas_call | solution.py:548
  279.4 0.0 all-gather.5.cloned.1.call-done.grad_ref.grad_hbm
  279.4 55.9 %shard_map.240 = (bf16[1024,2048]{1,0:T(8,128)(2,1)}, bf16[1024,2048]{1,0:T(8,128)(2,1)}, bf16[2048,2048]{1,0:T(8,128)(2,1)}, bf16[512,2048]{1,0:T(8,128)(2,1)},...) custom-call(bf16[1024,2048]{1,0:T(8,128)(2,1)} %get-tuple-element.54.rows_ref, ...), custom_call_target="tpu_custom_call" | custom-call | flops 42949672960 | bytes 75497472 | tf_op jit(solution)/shard_map/pallas_call | solution.py:743
  335.3 0.0 all-reduce.4.cloned.1.call-update
  335.3 0.0 reduce-scatter.5.cloned.1.call-start
  335.4 151.5 %shard_map.241 = (bf16[1024,2048]{1,0:T(8,128)(2,1)}, f32[256,2048]{1,0:T(8,128)}, f32[8,2048]{1,0:T(8,128)}, bf16[2048,2048]{1,0:T(8,128)(2,1)}) custom-call(bf16[1024,2048]{1,0:T(8,128)(2,1)} %get-tuple-element.59.d_gate_hbm, bf16[1024,2048]{1,0:T(8,128)(2,1)} %get-tuple-element.60.d_up_hbm, bf16[2048,2048]{1,0:T(8,128)(2,1)} %w_gate_hbm.3, ...), custom_call_target="tpu_custom_call" | custom-call | flops 17179869184 | bytes 262144000 | tf_op jit(solution)/shard_map/pallas_call | solution.py:663
  486.9 0.0 copy-start.10
  486.9 1.2 copy-done.10
  488.2 35.7 %shard_map.242 = (bf16[1024,512]{1,0:T(8,128)(2,1)S(1)}, bf16[1024,512]{1,0:T(8,128)(2,1)S(1)}, bf16[1024,512]{1,0:T(8,128)(2,1)S(1)}, f32[4,8,128]{2,1,0:T(8,128)S(1)}) custom-call(f32[4]{0:T(128)S(1)} %add_divide_fusion.gate_ref, s32[1]{0:T(128)} %bitcast.valid_ref, bf16[1024,2048]{1,0:T(8,128)(2,1)} %get-tuple-element.63.d_out_ref, ...), custom_call_target="tpu_custom_call" | custom-call | flops 7516192768 | bytes 104857600 | tf_op jit(solution)/shard_map/pallas_call | solution.py:1119
  523.9 19.5 %shard_map.243 = (bf16[1024,2048]{1,0:T(8,128)(2,1)}, bf16[2048,512]{1,0:T(8,128)(2,1)}, bf16[2048,512]{1,0:T(8,128)(2,1)}, bf16[2048,512]{1,0:T(8,128)(2,1)}, b...) custom-call(bf16[1024,2048]{1,0:T(8,128)(2,1)} %copy-done.14, bf16[1024,2048]{1,0:T(8,128)(2,1)} %get-tuple-element.63.d_out_ref, ...), custom_call_target="tpu_custom_call" | custom-call | flops 15032385536 | bytes 31457280 | tf_op jit(solution)/shard_map/pallas_call | solution.py:891
  543.4 0.0 reduce-scatter.5.cloned.1.call-update
  543.5 0.0 reduce-scatter.3.cloned.1.call-start
  543.5 0.0 copy-start.11
  543.5 0.5 reduce-scatter.3.cloned.1.call-update
  544.1 0.7 copy-done.11
  544.7 0.3 fusion.10
  545.0 0.1 slice_reduce_fusion
  545.2 0.1 broadcast_select_fusion
  545.2 0.1 select_n.65
  545.4 130.4 %shard_map.244 = (f32[40,128]{1,0:T(8,128)S(1)}, bf16[1536,2048]{1,0:T(8,128)(2,1)}, bf16[512,2048]{1,0:T(8,128)(2,1)S(1)}, bf16[2048,512]{1,0:T(8,128)(2,1)S(1)...) custom-call(f32[40,128]{1,0:T(8,128)S(1)} %fusion.12.refs_0_, bf16[1536,2048]{1,0:T(8,128)(2,1)} %get-tuple-element.71.refs_1_, ...), custom_call_target="tpu_custom_call" | custom-call | bytes 440401920 | tf_op jit(solution)/shard_map/pallas_call | solution.py:266
  675.8 0.0 copy-start.1
  675.8 1.3 copy-done.1
  677.1 0.6 dynamic_slice.7
  677.7 0.6 slice_multiply_fusion.1
  678.3 0.6 slice_bitcast_fusion
  678.9 0.7 fusion.11
  679.6 1.6 copy-done
  681.2 1.6 copy-done.2
  682.8 1.6 copy-done.3
  684.4 1.6 copy-done.4
  686.0 30.8 %shard_map.245 = (f32[2048,2048]{1,0:T(8,128)}, f32[2048,2048]{1,0:T(8,128)}, f32[2048,2048]{1,0:T(8,128)}, f32[512,2048]{1,0:T(8,128)}, f32[2048,512]{1,0:T(8,1...) custom-call(bf16[2048,2048]{1,0:T(8,128)(2,1)} %get-tuple-element.92.refs_0_, bf16[512,2048]{1,0:T(8,128)(2,1)S(1)} %copy-done, ...), custom_call_target="tpu_custom_call" | custom-call | bytes 100663296 | tf_op jit(solution)/shard_map/pallas_call | solution.py:838
  716.9 0.0 reduce-scatter.5.cloned.1.call-done
  716.9 1.8 fusion.5
  718.7 0.0 reduce-scatter.3.cloned.1.call-done
  718.7 3.3 add_convert_fusion
  722.0 1.7 fusion.9
  (41 shorter events, 0.2 us)
Async XLA Ops:
  7.2 1.6 copy-start.21
  7.2 2.9 copy-start.22
  7.2 85.9 %all-gather.3.cloned.1.call-start = ((), (), s32[]{:S(2)}) async-start(), calls=%async_computation.2 | async-start | bytes 5242880 | tf_op jit(solution)/shard_map/all_gather | solution.py:1198
  7.9 271.5 %all-gather.5.cloned.1.call-start = ((), (), s32[]{:S(2)}) async-start(), calls=%async_computation.3 | async-start | bytes 5242880 | tf_op jit(solution)/shard_map/all_gather | solution.py:1199
  8.7 670.9 %all-reduce.4.cloned.1.call-start = ((), (), s32[]{:S(2)}) async-start(), calls=%async_computation.6 | async-start | bytes 20971520 | tf_op jit(solution)/shard_map/psum | solution.py:1234
  10.1 86.3 %copy-start.16 = (f32[2048]{0:T(1024)S(1)}, f32[2048]{0:T(1024)}, u32[]{:S(2)}) copy-start(f32[2048]{0:T(1024)} %param.15) | copy-start | bytes 24580
  93.1 3.4 copy-start.12
  96.5 1.6 copy-start.20
  98.1 17.4 %copy-start.14 = (bf16[1024,2048]{1,0:T(8,128)(2,1)}, bf16[1024,2048]{1,0:T(8,128)(2,1)S(1)}, u32[]{:S(2)}) copy-start(bf16[1024,2048]{1,0:T(8,128)(2,1)S(1)} %fusion.2.rows_ref) | copy-start | bytes 12582916
  98.1 3.2 copy-start.19
  101.3 16.6 %copy-start.8 = (bf16[1024,512]{1,0:T(8,128)(2,1)}, bf16[1024,512]{1,0:T(8,128)(2,1)S(1)}, u32[]{:S(2)}) copy-start(bf16[1024,512]{1,0:T(8,128)(2,1)S(1)} %convolution_convert_fusion.value_ref) | copy-start | bytes 3145732
  103.7 14.2 %copy-start.9 = (bf16[1024,512]{1,0:T(8,128)(2,1)}, bf16[1024,512]{1,0:T(8,128)(2,1)S(1)}, u32[]{:S(2)}) copy-start(bf16[1024,512]{1,0:T(8,128)(2,1)S(1)} %convolution_convert_fusion.1.key_ref) | copy-start | bytes 3145732
  103.7 11.9 %copy-start.18 = (bf16[2048,512]{1,0:T(8,128)(2,1)S(1)}, bf16[2048,512]{1,0:T(8,128)(2,1)}, u32[]{:S(2)}) copy-start(bf16[2048,512]{1,0:T(8,128)(2,1)} %w_query_ref.1) | copy-start | bytes 6291460
  107.0 20.6 %collective-permute-start.2 = (f32[4,144,128]{2,1,0:T(8,128)S(1)}, f32[4,144,128]{2,1,0:T(8,128)S(1)}, u32[]{:S(2)}, u32[]{:S(2)}) collective-permute-start(f32[4,144,128]{2,1,0:T(8,128)S(1)} %shard_map.237), channel_id=1, source_target_pairs={{0,12},{4,16},{8,20},{12,24},{16,28},{1,13},{5,17},{9,21},{13,25},... | collective-permute-start | bytes 884744 | tf_op jit(solution)/shard_map/ppermute | solution.py:917
  109.8 17.8 %collective-permute-start.1 = (f32[4,144,128]{2,1,0:T(8,128)S(1)}, f32[4,144,128]{2,1,0:T(8,128)S(1)}, u32[]{:S(2)}, u32[]{:S(2)}) collective-permute-start(f32[4,144,128]{2,1,0:T(8,128)S(1)} %shard_map.237), channel_id=1, source_target_pairs={{0,8},{4,12},{8,16},{12,20},{16,24},{20,28},{1,9},{5,13},{9,17},{1... | collective-permute-start | bytes 884744 | tf_op jit(solution)/shard_map/ppermute | solution.py:917
  113.2 14.4 %collective-permute-start = (f32[4,144,128]{2,1,0:T(8,128)S(1)}, f32[4,144,128]{2,1,0:T(8,128)S(1)}, u32[]{:S(2)}, u32[]{:S(2)}) collective-permute-start(f32[4,144,128]{2,1,0:T(8,128)S(1)} %shard_map.237), channel_id=1, source_target_pairs={{0,4},{4,8},{8,12},{12,16},{16,20},{20,24},{24,28},{1,5},{5,9},{9,... | collective-permute-start | bytes 884744 | tf_op jit(solution)/shard_map/ppermute | solution.py:917
  127.6 3.8 copy-start.5
  131.4 1.0 copy-start.6
  335.3 381.6 %reduce-scatter.5.cloned.1.call-start = ((), (), s32[]{:S(2)}) async-start(), calls=%async_computation.5 | async-start | bytes 5242880 | tf_op jit(solution)/shard_map/reduce_scatter | solution.py:1274
  486.9 1.2 copy-start.10
  488.2 35.8 %copy-start.7 = (bf16[1024,512]{1,0:T(8,128)(2,1)S(1)}, bf16[1024,512]{1,0:T(8,128)(2,1)}, u32[]{:S(2)}) copy-start(bf16[1024,512]{1,0:T(8,128)(2,1)} %copy-done.6) | copy-start | bytes 3145732
  543.5 175.2 %reduce-scatter.3.cloned.1.call-start = ((), (), s32[]{:S(2)}) async-start(), calls=%async_computation.4 | async-start | bytes 5242880 | tf_op jit(solution)/shard_map/reduce_scatter | solution.py:1249
  543.5 1.2 copy-start.11
  543.5 1.8 copy-start.17
  675.8 1.3 copy-start.1
  679.6 1.6 copy-start
  681.2 1.6 copy-start.2
  682.8 1.6 copy-start.3
  684.4 1.6 copy-start.4
  718.7 3.4 copy-start.13
  718.7 3.3 copy-start.15
Sparse Core Ops, SparseCore 0:
  9.6 83.4 all-gather.2
  94.7 107.1 all-gather.4
  335.5 205.7 all-reduce.3
  543.6 77.5 reduce-scatter.4
  623.4 77.2 reduce-scatter.2

commit v3 on v2

--- a/solution.py
+++ b/solution.py
@@ -15,16 +15,15 @@
 
 epsilon = 1e-05
 masked_score = -1e30
-highest = lax.Precision.HIGHEST
 F32 = jnp.float32
 BF16 = jnp.bfloat16
 
 
 MESH = pl.DeviceIdType.MESH
-LAND_SLOTS = 8
-RESULT_SLOTS = 12
+LAND_SLOTS = 12
+RESULT_SLOTS = 16
 SUM_SEMS = 8
-SUM_HOP = 2
+SUM_HOP = 3
 
 
 def bits_of(size):
@@ -278,7 +277,7 @@
         + engine_scratch(tile, seg_bits),
         cost_estimate=pl.CostEstimate(flops=0, bytes_accessed=moved * 60, transcendentals=0),
         compiler_params=pltpu.CompilerParams(
-            collective_id=cid, has_side_effects=True, vmem_limit_bytes=48 * 2**20
+            collective_id=cid, has_side_effects=True, vmem_limit_bytes=60 * 2**20
         ),
     )(small, *arrays)
 
@@ -440,15 +439,183 @@
     ]
 
 
+GATHER_PARTS = 4
+
+
+def gather_kernel(
+    token_hbm, gain_ref, w_query_hbm, w_key_hbm, w_value_hbm,
+    all_ref, normed_ref, query_ref, key_ref, value_ref,
+    land, normed, w_query, w_key, w_value,
+    own_sem, load_sem, all_sem, normed_sem, up_send, up_recv, down_send, down_recv,
+):
+    size = lax.axis_size("head")
+    place = lax.axis_index("head")
+    last = size - 1
+    own_rows = token_hbm.shape[0]
+    chunk = own_rows // GATHER_PARTS
+    loads = [
+        pltpu.make_async_copy(source, target, load_sem.at[i])
+        for i, (source, target) in enumerate(
+            ((w_key_hbm, w_key), (w_value_hbm, w_value), (w_query_hbm, w_query))
+        )
+    ]
+
+    def shard_rows(shard):
+        return pl.ds(pl.multiple_of(shard * own_rows, own_rows), own_rows)
+
+    own = pltpu.make_async_copy(token_hbm, land.at[shard_rows(place)], own_sem)
+    own.start()
+    for load in loads:
+        load.start()
+    line_barrier()
+
+    def chunk_copy(shard, i, send_sem, recv_sem, target):
+        first = pl.multiple_of(shard * own_rows + lax.rem(i, GATHER_PARTS) * chunk, chunk)
+        ref = land.at[pl.ds(first, chunk)]
+        return pltpu.make_async_remote_copy(
+            src_ref=ref,
+            dst_ref=ref,
+            send_sem=send_sem.at[i],
+            recv_sem=recv_sem.at[i],
+            device_id={"head": target},
+            device_id_type=MESH,
+        )
+
+    above, below = lax.rem(place + 1, size), lax.rem(place + last, size)
+
+    def up_copy(i, first_shard):
+        return chunk_copy(first_shard - i // GATHER_PARTS, i, up_send, up_recv, above)
+
+    def down_copy(i, first_shard):
+        return chunk_copy(first_shard + i // GATHER_PARTS, i, down_send, down_recv, below)
+
+    own.wait()
+    for i in range(GATHER_PARTS):
+
+        @pl.when(place < last)
+        def _(i=i):
+            up_copy(i, place).start()
+
+        @pl.when(place > 0)
+        def _(i=i):
+            down_copy(i, place).start()
+
+    def stores(shard):
+        rows = shard_rows(shard)
+        return (
+            pltpu.make_async_copy(land.at[rows], all_ref.at[rows], all_sem.at[shard]),
+            pltpu.make_async_copy(normed.at[rows], normed_ref.at[rows], normed_sem.at[shard]),
+        )
+
+    def project(shard):
+        rows = shard_rows(shard)
+        value = land[rows].astype(F32)
+        normed[rows] = (value * inverse_rms(value) * gain_ref[...]).astype(BF16)
+        for copy in stores(shard):
+            copy.start()
+        for weight, target in ((w_key, key_ref), (w_value, value_ref), (w_query, query_ref)):
+            target[rows] = dot(normed[rows], weight[...], NN).astype(BF16)
+
+    for load in loads:
+        load.wait()
+    project(place)
+
+    def step(i, carry):
+        @pl.when(i < place * GATHER_PARTS)
+        def _():
+            up_copy(i, place - 1).wait_recv()
+
+            @pl.when(place < last)
+            def _():
+                up_copy(i + GATHER_PARTS, place).start()
+
+        @pl.when(i < (last - place) * GATHER_PARTS)
+        def _():
+            down_copy(i, place + 1).wait_recv()
+
+            @pl.when(place > 0)
+            def _():
+                down_copy(i + GATHER_PARTS, place).start()
+
+        distance = (i + 1) // GATHER_PARTS
+        whole = lax.rem(i + 1, GATHER_PARTS) == 0
+
+        @pl.when(whole & (place >= distance))
+        def _():
+            project(place - distance)
+
+        @pl.when(whole & (place + distance <= last))
+        def _():
+            project(place + distance)
+
+        return carry
+
+    lax.fori_loop(0, last * GATHER_PARTS, step, 0)
+
+    def drain(i, carry):
+        @pl.when((place < last) & (i < (place + 1) * GATHER_PARTS))
+        def _():
+            up_copy(i, place).wait_send()
+
+        @pl.when((place > 0) & (i < (size - place) * GATHER_PARTS))
+        def _():
+            down_copy(i, place).wait_send()
+
+        return carry
+
+    lax.fori_loop(0, size * GATHER_PARTS, drain, 0)
+    for shard in range(size):
+        for copy in stores(shard):
+            copy.wait()
+
+
+def gather_project(tokens, gain, w_query, w_key, w_value, size, cid):
+    own_rows, width = tokens.shape
+    rows, cols = own_rows * size, w_query.shape[1]
+    vmem, any_ = pl.BlockSpec(memory_space=pltpu.VMEM), pl.BlockSpec(memory_space=pltpu.HBM)
+    weight = pltpu.VMEM((width, cols), BF16)
+    hops = pltpu.SemaphoreType.DMA((size * GATHER_PARTS,))
+    return pl.pallas_call(
+        gather_kernel,
+        in_specs=[any_, vmem] + [any_] * 3,
+        out_specs=[any_, any_, vmem, vmem, vmem],
+        out_shape=[jax.ShapeDtypeStruct((rows, width), BF16)] * 2
+        + [jax.ShapeDtypeStruct((rows, cols), BF16)] * 3,
+        scratch_shapes=[
+            pltpu.VMEM((rows, width), BF16),
+            pltpu.VMEM((rows, width), BF16),
+            weight,
+            weight,
+            weight,
+            pltpu.SemaphoreType.DMA(()),
+            pltpu.SemaphoreType.DMA((3,)),
+            pltpu.SemaphoreType.DMA((size,)),
+            pltpu.SemaphoreType.DMA((size,)),
+            hops,
+            hops,
+            hops,
+            hops,
+        ],
+        cost_estimate=pl.CostEstimate(
+            flops=6 * rows * width * cols, bytes_accessed=150 * 2**20, transcendentals=0
+        ),
+        compiler_params=pltpu.CompilerParams(
+            collective_id=cid, has_side_effects=True, vmem_limit_bytes=48 * 2**20
+        ),
+    )(tokens, gain.reshape(1, width), w_query, w_key, w_value)
+
+
 def attn_out_kernel(
-    mixed_ref, weight_ref, token_ref, gain_ref, w_gate_hbm, w_up_hbm,
-    hidden_ref, normed_ref, silu_ref, slope_ref, act_ref,
-    hidden, normed, w_gate, w_up, silu, slope, act,
-    hidden_sem, normed_sem, load_sem, out_sem, *scratch
+    mixed_ref, weight_ref, token_ref, gain_ref, w_gate_hbm, w_up_hbm, w_down_hbm,
+    hidden_ref, flip_ref, silu_ref, slope_ref, act_ref, part_ref,
+    hidden, normed, w_gate, w_up, w_down, silu, slope, act, flip, part, part_out,
+    hidden_sem, load_sem, out_sem, block_sem, *scratch
 ):
     loads = [
         pltpu.make_async_copy(source, target, load_sem.at[i])
-        for i, (source, target) in enumerate(((w_gate_hbm, w_gate), (w_up_hbm, w_up)))
+        for i, (source, target) in enumerate(
+            ((w_gate_hbm, w_gate), (w_up_hbm, w_up), (w_down_hbm, w_down))
+        )
     ]
     for load in loads:
         load.start()
@@ -476,8 +643,24 @@
     def unit_cols(u):
         return pl.ds(pl.multiple_of(lax.rem(u, groups) * UNIT_GROUP, UNIT_GROUP), UNIT_GROUP)
 
+    def flip_copy(b):
+        return pltpu.make_async_copy(flip, flip_ref.at[:, block_rows(b)], block_sem.at[0])
+
+    def part_copy(b):
+        return pltpu.make_async_copy(part_out, part_ref.at[block_rows(b)], block_sem.at[1])
+
     def forward(u):
         slot = lax.rem(u, slots)
+        b, group = u // groups, lax.rem(u, groups)
+
+        @pl.when(group == 0)
+        def _():
+            @pl.when(b > 0)
+            def _():
+                flip_copy(b - 1).wait()
+
+            flip[...] = normed[block_rows(b)].T
+            flip_copy(b).start()
 
         @pl.when(u >= slots)
         def _():
@@ -494,6 +677,24 @@
         act[slot] = (silu_gate * up_proj).astype(BF16)
         for copy in unit_copies(u):
             copy.start()
+        share = dot(act[slot], w_down[cols], NN)
+
+        @pl.when(group == 0)
+        def _():
+            part[...] = share
+
+        @pl.when(group > 0)
+        def _():
+            part[...] += share
+
+        @pl.when(group == groups - 1)
+        def _():
+            @pl.when(b > 0)
+            def _():
+                part_copy(b - 1).wait()
+
+            part_out[...] = part[...].astype(BF16)
+            part_copy(b).start()
 
     def before(t):
         @pl.when((lax.rem(t, per_block) == 0) & (t < blocks * per_block))
@@ -513,12 +714,9 @@
         def _():
             forward(late // pace)
 
-    def stores(b):
+    def store(b):
         rows = block_rows(b)
-        return (
-            pltpu.make_async_copy(hidden.at[rows], hidden_ref.at[rows], hidden_sem.at[b]),
-            pltpu.make_async_copy(normed.at[rows], normed_ref.at[rows], normed_sem.at[b]),
-        )
+        return pltpu.make_async_copy(hidden.at[rows], hidden_ref.at[rows], hidden_sem.at[b])
 
     def finish(k, total):
         rows = pl.ds(pl.multiple_of(k * ROWS, ROWS), ROWS)
@@ -528,63 +726,69 @@
 
         @pl.when(lax.rem(k, per_block) == per_block - 1)
         def _():
-            for copy in stores(k // per_block):
-                copy.start()
+            store(k // per_block).start()
 
     line_exchange(hidden, finish, before, scratch, after, lag + blocks * per_block)
     for b in range(blocks):
-        for copy in stores(b):
-            copy.wait()
+        store(b).wait()
+    flip_copy(blocks - 1).wait()
+    part_copy(blocks - 1).wait()
     for u in range(blocks * groups - slots, blocks * groups):
         for copy in unit_copies(u):
             copy.wait()
 
 
-def attn_out_sum(mixed, weight, tokens, gain, w_gate, w_up, size, cid):
+def attn_out_sum(mixed, weight, tokens, gain, w_gate, w_up, w_down, size, cid):
     rows, width = tokens.shape
     units = w_gate.shape[1]
     vmem, any_ = pl.BlockSpec(memory_space=pltpu.VMEM), pl.BlockSpec(memory_space=pltpu.HBM)
     blocks, slots = rows // BLOCK_ROWS, 2
     return pl.pallas_call(
         attn_out_kernel,
-        in_specs=[vmem] * 4 + [any_] * 2,
-        out_specs=[any_] * 5,
+        in_specs=[vmem] * 4 + [any_] * 3,
+        out_specs=[any_] * 6,
         out_shape=[
             jax.ShapeDtypeStruct((rows, width), F32),
-            jax.ShapeDtypeStruct((rows, width), BF16),
+            jax.ShapeDtypeStruct((width, rows), BF16),
             jax.ShapeDtypeStruct((rows, units), F32),
             jax.ShapeDtypeStruct((rows, units), F32),
             jax.ShapeDtypeStruct((rows, units), BF16),
+            jax.ShapeDtypeStruct((rows, width), BF16),
         ],
         scratch_shapes=[
             pltpu.VMEM((rows, width), F32),
             pltpu.VMEM((rows, width), BF16),
             pltpu.VMEM((width, units), BF16),
             pltpu.VMEM((width, units), BF16),
+            pltpu.VMEM((units, width), BF16),
             pltpu.VMEM((slots, BLOCK_ROWS, UNIT_GROUP), F32),
             pltpu.VMEM((slots, BLOCK_ROWS, UNIT_GROUP), F32),
             pltpu.VMEM((slots, BLOCK_ROWS, UNIT_GROUP), BF16),
+            pltpu.VMEM((width, BLOCK_ROWS), BF16),
+            pltpu.VMEM((BLOCK_ROWS, width), F32),
+            pltpu.VMEM((BLOCK_ROWS, width), BF16),
             pltpu.SemaphoreType.DMA((blocks,)),
-            pltpu.SemaphoreType.DMA((blocks,)),
+            pltpu.SemaphoreType.DMA((3,)),
+            pltpu.SemaphoreType.DMA((3, slots)),
             pltpu.SemaphoreType.DMA((2,)),
-            pltpu.SemaphoreType.DMA((3, slots)),
         ]
         + line_scratch(size, width),
         cost_estimate=pl.CostEstimate(
-            flops=2 * rows * width * (mixed.shape[1] + 2 * units),
+            flops=2 * rows * width * (mixed.shape[1] + 3 * units),
             bytes_accessed=250 * 2**20,
             transcendentals=rows * units,
         ),
         compiler_params=pltpu.CompilerParams(
             collective_id=cid, has_side_effects=True, vmem_limit_bytes=60 * 2**20
         ),
-    )(mixed, weight, tokens, gain.reshape(1, width), w_gate, w_up)
+    )(mixed, weight, tokens, gain.reshape(1, width), w_gate, w_up, w_down)
 
 
 def mlp_back_kernel(
     tile, seg_bits,
-    d_gate_hbm, d_up_hbm, w_gate_hbm, w_up_hbm, hidden_hbm, grad_hbm, gain_ref, sum_in,
-    d_out_ref, d_own_ref, gain_part_ref, sum_out,
+    d_gate_a, d_gate_b, d_up_a, d_up_b, w_gate_hbm, w_up_hbm, hidden_hbm, grad_hbm, gain_ref,
+    down_in, gate_in,
+    d_out_ref, d_own_ref, gain_part_ref, down_out, gate_out,
     d_gate, d_up, w_gate, w_up, hidden, grad, own, load_sem, store_sem, *scratch
 ):
     per_block = BLOCK_ROWS // ROWS
@@ -592,10 +796,13 @@
     size = lax.axis_size("head")
     place = lax.axis_index("head")
     per_device = own.shape[0] // ROWS // size
+    half = d_gate.shape[1] // 2
+    low, high = pl.ds(0, half), pl.ds(half, half)
     loads = [
         pltpu.make_async_copy(source, target, load_sem.at[i])
         for i, (source, target) in enumerate(
-            ((d_gate_hbm, d_gate), (w_gate_hbm, w_gate), (d_up_hbm, d_up), (w_up_hbm, w_up),
+            ((d_gate_a, d_gate.at[:, low]), (d_gate_b, d_gate.at[:, high]), (w_gate_hbm, w_gate),
+             (d_up_a, d_up.at[:, low]), (d_up_b, d_up.at[:, high]), (w_up_hbm, w_up),
              (hidden_hbm, hidden), (grad_hbm, grad))
         )
     ]
@@ -605,13 +812,13 @@
     greet_seg(seg_bits)
     line_barrier(seg_bits)
     engine_step, steps = sum_engine(
-        [sum_in], [sum_out], tile, seg_bits, scratch[LINE_REFS:]
+        [down_in, gate_in], [down_out, gate_out], tile, seg_bits, scratch[LINE_REFS:]
     )
 
     def block_rows(b):
         return pl.ds(pl.multiple_of(b * BLOCK_ROWS, BLOCK_ROWS), BLOCK_ROWS)
 
-    for load in loads[:4]:
+    for load in loads[:6]:
         load.wait()
 
     def before(t):
@@ -622,7 +829,7 @@
 
         @pl.when(t == 0)
         def _():
-            for load in loads[4:]:
+            for load in loads[6:]:
                 load.wait()
 
     def store(b):
@@ -654,22 +861,24 @@
         store(b).wait()
 
 
-def mlp_back_sum(d_gate, d_up, w_gate, w_up, hidden, grad, gain, summed, tile, seg_size, size, cid):
+def mlp_back_sum(
+    d_gate, d_up, w_gate, w_up, hidden, grad, gain, summed, tile, seg_size, size, cid
+):
     rows, width = hidden.shape
-    units = d_gate.shape[1]
+    units = w_gate.shape[1]
     seg_bits = bits_of(seg_size)
     vmem, any_ = pl.BlockSpec(memory_space=pltpu.VMEM), pl.BlockSpec(memory_space=pltpu.HBM)
     blocks = rows // BLOCK_ROWS
     return pl.pallas_call(
         functools.partial(mlp_back_kernel, tile, seg_bits),
-        in_specs=[any_] * 6 + [vmem, any_],
-        out_specs=[any_, vmem, vmem, any_],
+        in_specs=[any_] * 8 + [vmem, any_, any_],
+        out_specs=[any_, vmem, vmem, any_, any_],
         out_shape=[
             jax.ShapeDtypeStruct((rows, width), BF16),
             jax.ShapeDtypeStruct((rows // size, width), F32),
             jax.ShapeDtypeStruct((8, width), F32),
-            jax.ShapeDtypeStruct(summed.shape, BF16),
-        ],
+        ]
+        + [jax.ShapeDtypeStruct(array.shape, BF16) for array in summed],
         scratch_shapes=[
             pltpu.VMEM((rows, units), BF16),
             pltpu.VMEM((rows, units), BF16),
@@ -678,7 +887,7 @@
             pltpu.VMEM((rows, width), F32),
             pltpu.VMEM((rows, width), BF16),
             pltpu.VMEM((rows, width), F32),
-            pltpu.SemaphoreType.DMA((6,)),
+            pltpu.SemaphoreType.DMA((8,)),
             pltpu.SemaphoreType.DMA((blocks,)),
         ]
         + line_scratch(size, width)
@@ -689,79 +898,63 @@
         compiler_params=pltpu.CompilerParams(
             collective_id=cid, has_side_effects=True, vmem_limit_bytes=62 * 2**20
         ),
-    )(d_gate, d_up, w_gate, w_up, hidden, grad, gain.reshape(1, width), summed)
-
-
-MLP_BLOCK = 256
+    )(*d_gate, *d_up, w_gate, w_up, hidden, grad, gain.reshape(1, width), *summed)
+
+
+MLP_BLOCK = 512
 
 
 def mlp_kernel(
-    rows_ref, grad_ref, silu_ref, slope_ref, act_ref, w_down_ref,
-    d_gate_ref, d_up_ref, grad_gate_ref, grad_up_top, grad_up_low, grad_down_ref, out_ref,
-    flipped, total,
+    flip_ref, grad_ref, silu_ref, slope_ref, act_ref, w_down_ref,
+    d_gate_ref, d_up_ref, grad_gate_ref, grad_up_ref, grad_down_ref,
 ):
-    width = rows_ref.shape[1]
-    first = pl.program_id(0) == 0
-    last = pl.program_id(0) == pl.num_programs(0) - 1
-    half = width // 2
-
-    @pl.when(first)
-    def _():
-        total[...] = jnp.zeros_like(total)
-        for i in range(2):
-            part = slice(i * half, (i + 1) * half)
-            flipped[part] = rows_ref[:, part].T
-
+    width = flip_ref.shape[0]
     d_act = dot(grad_ref[...], w_down_ref[...], NT)
     d_gate_ref[...] = (d_act * slope_ref[...]).astype(BF16)
     d_up_ref[...] = (d_act * silu_ref[...]).astype(BF16)
-    total[...] += dot(act_ref[...], w_down_ref[...], NN)
+    half = width // 2
     for i in range(2):
         part = slice(i * half, (i + 1) * half)
-        grad_gate_ref[part] = dot(flipped[part], d_gate_ref[...], NN).astype(BF16)
+        grad_gate_ref[part] = dot(flip_ref[part], d_gate_ref[...], NN).astype(BF16)
+        grad_up_ref[part] = dot(flip_ref[part], d_up_ref[...], NN).astype(BF16)
         grad_down_ref[:, part] = dot(act_ref[...], grad_ref[:, part], TN).astype(BF16)
-    top = grad_up_top.shape[0]
-    grad_up_top[...] = dot(flipped[:top], d_up_ref[...], NN).astype(BF16)
-    grad_up_low[...] = dot(flipped[top:], d_up_ref[...], NN).astype(BF16)
-
-    @pl.when(last)
-    def _():
-        out_ref[...] = total[...].astype(BF16)
-
-
-def mlp_both(rows, grad, silu, slope, act, w_down):
-    count, width = rows.shape
-    units = act.shape[1]
+
+
+def mlp_half(flip, grad, silu, slope, act, w_down, which):
+    width, count = flip.shape
+    units = act.shape[1] // 2
     block = min(MLP_BLOCK, units)
+    first = which * (units // block)
     once = pl.Buffered(1)
-    whole = pl.BlockSpec((count, width), lambda j: (0, 0), pipeline_mode=once)
-    side = pl.BlockSpec((count, block), lambda j: (0, j))
+    side = pl.BlockSpec((count, block), lambda j: (0, first + j))
+    side_out = pl.BlockSpec((count, block), lambda j: (0, j))
     tall = pl.BlockSpec((width, block), lambda j: (0, j))
-    wide = pl.BlockSpec((block, width), lambda j: (j, 0))
-    top = width // 4
-    parts = [pl.BlockSpec((rows, block), lambda j: (0, j)) for rows in (top, width - top)]
     return pl.pallas_call(
         mlp_kernel,
         grid=(units // block,),
-        in_specs=[whole, whole, side, side, side, wide],
-        out_specs=[side, side, tall, *parts, wide, whole],
+        in_specs=[
+            pl.BlockSpec((width, count), lambda j: (0, 0), pipeline_mode=once),
+            pl.BlockSpec((count, width), lambda j: (0, 0), pipeline_mode=once),
+            side,
+            side,
+            side,
+            pl.BlockSpec((block, width), lambda j: (first + j, 0)),
+        ],
+        out_specs=[side_out, side_out, tall, tall, pl.BlockSpec((block, width), lambda j: (j, 0))],
         out_shape=[
             jax.ShapeDtypeStruct((count, units), BF16),
             jax.ShapeDtypeStruct((count, units), BF16),
             jax.ShapeDtypeStruct((width, units), BF16),
-            jax.ShapeDtypeStruct((top, units), BF16),
-            jax.ShapeDtypeStruct((width - top, units), BF16),
+            jax.ShapeDtypeStruct((width, units), BF16),
             jax.ShapeDtypeStruct((units, width), BF16),
-            jax.ShapeDtypeStruct((count, width), BF16),
         ],
-        scratch_shapes=[pltpu.VMEM((width, count), BF16), pltpu.VMEM((count, width), F32)],
         cost_estimate=pl.CostEstimate(
-            flops=10 * count * width * units,
-            bytes_accessed=2 * (3 * count * width + 4 * width * units + 7 * count * units),
+            flops=8 * count * width * units,
+            bytes_accessed=2 * (2 * count * width + 4 * width * units + 7 * count * units),
             transcendentals=0,
         ),
         compiler_params=pltpu.CompilerParams(vmem_limit_bytes=56 * 2**20),
-    )(rows, grad, silu, slope, act, w_down)
+    )(flip, grad, silu, slope, act, w_down)
 
 
 WIDEN_SLOTS = 4
@@ -793,10 +986,11 @@
 
     def store(k, i, where):
         slot = lax.rem(k, WIDEN_SLOTS)
-        target, first = places[i]
-        rows = pl.ds(pl.multiple_of(first + where[0].start, high), high)
+        target, row, col = places[i]
+        rows = pl.ds(pl.multiple_of(row + where[0].start, high), high)
+        cols = pl.ds(pl.multiple_of(col + where[1].start, broad), broad)
         return pltpu.make_async_copy(
-            wide.at[slot], targets[target].at[rows, where[1]], store_sem.at[slot]
+            wide.at[slot], targets[target].at[rows, cols], store_sem.at[slot]
         )
 
     zero = (pl.ds(0, high), pl.ds(0, broad))
@@ -826,13 +1020,14 @@
 
 def widen(groups, tile):
     arrays, places, targets = [], [], []
-    for group in groups:
-        rows = 0
+    for axis, *group in groups:
+        shape = [0, 0]
+        shape[1 - axis] = group[0].shape[1 - axis]
         for value in group:
             arrays.append(value)
-            places.append((len(targets), rows))
-            rows += value.shape[0]
-        targets.append((rows, group[0].shape[1]))
+            places.append((len(targets), *((shape[0], 0) if axis == 0 else (0, shape[1]))))
+            shape[axis] += value.shape[axis]
+        targets.append(tuple(shape))
     shapes = [value.shape for value in arrays]
     any_ = pl.BlockSpec(memory_space=pltpu.HBM)
     return pl.pallas_call(
@@ -849,7 +1044,7 @@
         cost_estimate=pl.CostEstimate(
             flops=0, bytes_accessed=6 * sum(r * c for r, c in shapes), transcendentals=0
         ),
-        compiler_params=pltpu.CompilerParams(vmem_limit_bytes=40 * 2**20),
+        compiler_params=pltpu.CompilerParams(vmem_limit_bytes=60 * 2**20),
     )(*arrays)
 
 
@@ -936,10 +1131,25 @@
     return grad_in
 
 
-def dot(left, right, dims, precision=None):
-    return lax.dot_general(
-        left, right, (dims, ((), ())), precision=precision, preferred_element_type=F32
-    )
+def dot(left, right, dims):
+    return lax.dot_general(left, right, (dims, ((), ())), preferred_element_type=F32)
+
+
+def in_two(values):
+    if values.dtype == BF16:
+        return (values,)
+    top = values.astype(BF16)
+    return top, (values - top.astype(F32)).astype(BF16)
+
+
+def fine_dot(left, right, dims):
+    lefts, rights = in_two(left), in_two(right)
+    total = dot(lefts[0], rights[0], dims)
+    for low in rights[1:]:
+        total = total + dot(lefts[0], low, dims)
+    for low in lefts[1:]:
+        total = total + dot(low, rights[0], dims)
+    return total
 
 
 NN = ((1,), (0,))
@@ -953,7 +1163,7 @@
 
 def update_kernel(valid_ref, key_ref, value_ref, out_ref):
     key_feat = elu_plus(key_ref[...].astype(F32)) * valid_column(valid_ref[0])
-    out_ref[0, :DH] = dot(key_feat, value_ref[...].astype(F32), TN, highest)
+    out_ref[0, :DH] = fine_dot(key_feat, value_ref[...], TN)
     out_ref[0, DH:] = jnp.broadcast_to(
         jnp.sum(key_feat, axis=0, keepdims=True), (MEM_ROWS - DH, DH)
     )
@@ -978,7 +1188,7 @@
 
 
 def retrieve(query_feat, memory, normal):
-    numerator = dot(query_feat, memory, NN, highest)
+    numerator = fine_dot(query_feat, memory, NN)
     denominator = jnp.sum(query_feat * normal, axis=-1, keepdims=True) + 1.0
     return numerator / denominator, denominator
 
@@ -1048,9 +1258,9 @@
         d_retrieved = gate * d_head
         d_numerator = d_retrieved / denominator
         d_denominator = -jnp.sum(d_retrieved * retrieved, axis=-1, keepdims=True) / denominator
-        d_feat = dot(d_numerator, memory, NT, highest) + d_denominator * normal
+        d_feat = fine_dot(d_numerator, memory, NT) + d_denominator * normal
         feat[:, cols] = d_feat * elu_slope(query_vals)
-        back[head, :DH] = dot(query_feat, d_numerator, TN, highest).astype(BF16)
+        back[head, :DH] = fine_dot(query_feat, d_numerator, TN).astype(BF16)
         d_normal = jnp.sum(d_denominator * query_feat, axis=0, keepdims=True)
         back[head, DH:] = jnp.broadcast_to(d_normal, (MEM_ROWS - DH, DH)).astype(BF16)
         return carry
@@ -1100,10 +1310,10 @@
         valid = valid_column(valid_len)
         key_vals = key_ref[:, cols].astype(F32)
         memory, normal = update[head, :DH], update[head, DH : DH + 1]
-        d_feat = (dot(value_ref[:, cols].astype(F32), memory, NT, highest) + normal) * valid
+        d_feat = (fine_dot(value_ref[:, cols], memory, NT) + normal) * valid
         d_key_ref[:, cols] = (d_key_sum[:, cols] + d_feat * elu_slope(key_vals)).astype(BF16)
         key_feat = elu_plus(key_vals) * valid
-        d_value = d_value_sum[:, cols] + dot(key_feat, memory, NN, highest)
+        d_value = d_value_sum[:, cols] + fine_dot(key_feat, memory, NN)
         d_value_ref[:, cols] = d_value.astype(BF16)
         return carry
 
@@ -1195,20 +1405,14 @@
     pairs = heads * SEG_LEN * SEG_LEN
 
     token_vals = tokens.astype(F32)
-    gathered_tokens = lax.all_gather(tokens, "head", axis=0, tiled=True)
+    gathered_tokens, gathered_attn, query_rows, key_rows, value_rows = gather_project(
+        tokens, gain_attn, w_query, w_key, w_value, head_groups, 4
+    )
+    cotangent, key_rows = lax.optimization_barrier((cotangent, key_rows))
     gathered_grad = lax.all_gather(cotangent, "head", axis=0, tiled=True)
-    all_tokens = gathered_tokens.astype(F32)
-    gathered_attn = (all_tokens * inverse_rms(all_tokens) * gain_attn).astype(BF16)
-
-    def project(weight):
-        return jnp.dot(gathered_attn, weight, preferred_element_type=F32).astype(BF16)
-
-    key_rows = project(w_key)
-    value_rows = project(w_value)
     update = per_head(update_kernel, heads, [SCALAR, COLUMN, COLUMN], MEMORY, mem_f32, 6 * unit)(
         valid_len, key_rows, value_rows
     )
-    query_rows = project(w_query)
     memory_prev = jnp.zeros_like(update)
     for distance in range(1, SEGS):
         moved = from_behind(update, "seg", distance)
@@ -1223,29 +1427,33 @@
     mixed_attn = per_head(
         mix_kernel, heads, [SCALAR, COLUMN, COLUMN, MEMORY], COLUMN, col_bf16, 6 * unit
     )(mix_sig, query_rows, local_attn, memory_prev)
-    all_hidden, gathered_mlp, silu, slope, act = attn_out_sum(
-        mixed_attn, w_out, gathered_tokens, gain_mlp, w_gate, w_up, head_groups, 1
+    all_hidden, flip_mlp, silu, slope, act, mlp_part = attn_out_sum(
+        mixed_attn, w_out, gathered_tokens, gain_mlp, w_gate, w_up, w_down, head_groups, 1
     )
     own_rows = tokens.shape[0]
     hidden_res = lax.dynamic_slice_in_dim(all_hidden, head_index * own_rows, own_rows, 0)
-    d_gate, d_up, grad_gate, up_top, up_low, grad_down, mlp_part = mlp_both(
-        gathered_mlp, gathered_grad, silu, slope, act, w_down
-    )
-    sum_gate, sum_up_top = lax.psum((grad_gate, up_top), "seg")
-    gathered_hidden, d_hidden, gain_mlp_rows, summed_down = mlp_back_sum(
-        d_gate,
-        d_up,
+    d_gate_a, d_up_a, gate_a, up_a, down_a = mlp_half(
+        flip_mlp, gathered_grad, silu, slope, act, w_down, 0
+    )
+    gate_a, up_a, down_a = lax.psum((gate_a, up_a, down_a), "seg")
+    d_gate_b, d_up_b, gate_b, up_b, down_b = mlp_half(
+        flip_mlp, gathered_grad, silu, slope, act, w_down, 1
+    )
+    gathered_hidden, d_hidden, gain_mlp_rows, down_b, gate_b = mlp_back_sum(
+        (d_gate_a, d_gate_b),
+        (d_up_a, d_up_b),
         w_gate,
         w_up,
         all_hidden,
         gathered_grad,
         gain_mlp,
-        grad_down,
+        (down_b, gate_b),
         (BLOCK, cols),
         seg_size,
         head_groups,
         2,
     )
+    mlp_part, gathered_hidden = lax.optimization_barrier((mlp_part, gathered_hidden))
     mlp_out = lax.psum_scatter(mlp_part, "head", scatter_dimension=0, tiled=True)
     output = (hidden_res + mlp_out.astype(F32)).astype(BF16)
     d_queries, d_keys, d_values, gate_cols = attn_back(
@@ -1286,7 +1494,7 @@
     parts = jnp.pad(parts, (0, lines * DH - parts.shape[0])).reshape(lines, DH)
     small, *late = grad_sum(
         parts,
-        [up_low, grad_out, grad_query, grad_key, grad_value],
+        [up_b, grad_out, grad_query, grad_key, grad_value],
         (cols, cols),
         seg_size,
         head_groups,
@@ -1295,7 +1503,8 @@
     small = small.reshape(-1)
     grad_mem_gate = lax.dynamic_slice(small, (2 * width + head_index * heads,), (heads,))
     grads = widen(
-        [(sum_gate,), (sum_up_top, late[0]), (summed_down,)] + [(grad,) for grad in late[1:]],
+        [(1, gate_a, gate_b), (1, up_a, late[0]), (0, down_a, down_b)]
+        + [(0, grad) for grad in late[1:]],
         (cols, cols),
     )
     return (

time: 739 us -> 705 us (0.954)
  waiting for transfers between devices: 85 us -> 0.64 us
  Pallas kernels: 588 us -> 649 us
    all_gather x1 -> x0, waiting for transfers between devices: 83 us -> none  [per_device(): gathered_tokens = lax.all_gather(tokens, 'head', axis=0, tiled=True)]
    pallas_call x2 -> x4, Pallas kernels: 203 us -> 285 us  [the longest x1 157 us: attn_out_sum(): pl.pallas_call(attn_out_kernel, in_specs=[vmem] * 4 + [any_] * 3, out_spe...]
    pallas_call x1, Pallas kernels: 130 us -> 115 us  [grad_sum(): pl.pallas_call(functools.partial(grad_sum_kernel, count, tile, seg_bits,...]
  transfers between devices with their start and end apart: 8 -> 7, of which waited for: 1 -> 0; matrix products, arithmetic and copies ran while one was open for 2% -> 1% of each run, Pallas kernels for 73% -> 78%
where the time goes in v3:
time: 705 us; the launch traced here: 697 us
  Pallas kernels  649 us (92%)
  between operations  15 us (2%)
  other arithmetic  12 us (2%)
  starting transfers between devices  10.6 us (2%)
  local copies, waits for them, and re-layouts  9.91 us (1%)
    pallas_call x1, Pallas kernels, attn_out_sum(): pl.pallas_call(attn_out_kernel, in_specs=[vmem] * 4 + [any_] * 3, out_spe...  157 us
    pallas_call x1, Pallas kernels, mlp_back_sum(): pl.pallas_call(functools.partial(mlp_back_kernel, tile, seg_bits), in_spe...  151 us
    pallas_call x1, Pallas kernels, grad_sum(): pl.pallas_call(functools.partial(grad_sum_kernel, count, tile, seg_bits,...  115 us
    pallas_call x1, Pallas kernels, gather_project(): pl.pallas_call(gather_kernel, in_specs=[any_, vmem] + [any_] * 3, out_spe...  75.4 us
    pallas_call x2, Pallas kernels, mlp_half(): pl.pallas_call(mlp_kernel, grid=(units // block,), in_specs=[pl.BlockSpec...  52.8 us
    pallas_call x1, Pallas kernels, widen(): pl.pallas_call(functools.partial(widen_kernel, shapes, places, len(target...  34.1 us
    pallas_call x1, Pallas kernels, attn_back(): pl.pallas_call(attn_back_kernel, in_specs=[scalar] * 2 + [vmem] * 7, out_...  29.1 us
    pallas_call x1, Pallas kernels, attn_weights(): pl.pallas_call(attn_weights_kernel, grid=(width // block,), in_specs=[sid...  19.6 us
  transfers between devices with their start and end apart: 7, of which 0 were waited for; matrix products, arithmetic and copies ran while one was open for 1% of the time, Pallas kernels for 78%

profile of v3, /device:TPU:0, one launch (start us, length us, event | category | flops | bytes accessed | tf_op | source)
XLA Modules:
  0.0 697.2 jit_solution(14109586280279345231)
XLA Ops:
  7.2 0.0 all-gather.2.cloned.1.call-start
  7.2 0.0 copy-start
  7.2 1.2 copy-done
  8.5 0.7 copy-done.6
  9.2 75.4 %shard_map.236 = (bf16[1024,2048]{1,0:T(8,128)(2,1)}, bf16[1024,2048]{1,0:T(8,128)(2,1)}, bf16[1024,512]{1,0:T(8,128)(2,1)S(1)}, bf16[1024,512]{1,0:T(8,128)(2,1)S(1)}, bf16[1024,512]{1,0:T(8,128)(2,1)S(1)}) custom-call(bf16[256,2048]{1,0:T(8,128)(2,1)S(1)} %copy-done, f32[1,2048]{1,0:T(1,128)S(1)} %bitcast.13, bf16[2048,512]{1,0:T(8,128)(2,1)} %w_query_ref.1, ...), custom_call_target="tpu_custom_call" | custom-call | flops 6442450944 | bytes 157286400 | tf_op jit(solution)/shard_map/pallas_call | solution.py:578
  84.5 0.0 copy-start.8
  84.6 0.0 copy-start.11
  84.6 0.0 all-gather.2.cloned.1.call-update
  84.6 0.0 all-reduce.4.cloned.1.call-start
  84.7 0.0 copy-done.17
  84.7 0.8 fusion.11
  86.1 2.5 shard_map.238
  88.7 0.0 copy-start.5
  88.7 2.7 collective-permute-start.2
  91.4 4.1 collective-permute-start.1
  95.5 3.2 collective-permute-start
  98.7 0.0 copy-done.8
  98.7 0.0 copy-done.11
  98.7 1.2 copy-done.9
  99.9 1.2 copy-done.12
  101.1 9.7 %shard_map.237.local_ref = f32[1024,512]{1,0:T(8,128)S(1)} custom-call(s32[1]{0:T(128)} %bitcast.1.valid_ref, bf16[1024,512]{1,0:T(8,128)(2,1)S(1)} %get-tuple-element.67.query_ref, bf16[1024,512]{1,0:T(8,128)(2,1)S(1)} %copy-done.9, bf16[1024,512]{1,0:T(8,128)(2,1)S(1)} %copy-done.12), custom_call_target="tpu_custom_call" | custom-call | flops 2147483648 | bytes 8388608 | tf_op jit(solution)/shard_map/pallas_call | solution.py:1420
  110.8 0.0 copy-start.2
  110.8 0.0 copy-done.18
  110.9 0.0 collective-permute-done.2
  110.9 0.0 collective-permute-done.1
  110.9 0.0 copy-done.5
  110.9 0.0 collective-permute-done
  110.9 2.0 fusion.12
  112.9 2.7 shard_map.239.mixed_ref
  115.6 1.0 copy-done.3
  116.6 157.1 %shard_map.240 = (f32[1024,2048]{1,0:T(8,128)}, bf16[2048,1024]{1,0:T(8,128)(2,1)}, f32[1024,2048]{1,0:T(8,128)}, f32[1024,2048]{1,0:T(8,128)}, bf16[1024,2048]{1,0:T(8,128)(2,1)}, /*index=5*/bf16[1024,2048]{1,0:T(8,128)(2,1)}) custom-call(bf16[1024,512]{1,0:T(8,128)(2,1)} %copy-done.3, bf16[512,2048]{1,0:T(8,128)(2,1)} %weight_ref.3, ...), custom_call_target="tpu_custom_call" | custom-call | flops 27917287424 | bytes 262144000 | tf_op jit(solution)/shard_map/pallas_call | solution.py:746
  273.7 0.0 all-gather.2.cloned.1.call-done.grad_ref.grad_hbm
  273.7 27.1 %shard_map.241 = (bf16[1024,1024]{1,0:T(8,128)(2,1)}, bf16[1024,1024]{1,0:T(8,128)(2,1)}, bf16[2048,1024]{1,0:T(8,128)(2,1)}, bf16[2048,1024]{1,0:T(8,128)(2,1)}, bf16[1024,2048]{1,0:T(8,128)(2,1)}) custom-call(bf16[2048,1024]{1,0:T(8,128)(2,1)} %get-tuple-element.74.flip_ref, bf16[1024,2048]{1,0:T(8,128)(2,1)} %all-gather.2.cloned.1.call-done.grad_ref.grad_hbm, ...), custom_call_target="tpu_custom_call" | custom-call | flops 17179869184 | bytes 39845888 | tf_op jit(solution)/shard_map/pallas_call | solution.py:932
  300.9 0.0 all-reduce.4.cloned.1.call-update
  300.9 0.4 reduce-scatter.5.cloned.1.call-start
  301.4 25.6 %shard_map.242 = (bf16[1024,1024]{1,0:T(8,128)(2,1)}, bf16[1024,1024]{1,0:T(8,128)(2,1)}, bf16[2048,1024]{1,0:T(8,128)(2,1)}, bf16[2048,1024]{1,0:T(8,128)(2,1)}, bf16[1024,2048]{1,0:T(8,128)(2,1)}) custom-call(bf16[2048,1024]{1,0:T(8,128)(2,1)} %get-tuple-element.74.flip_ref, bf16[1024,2048]{1,0:T(8,128)(2,1)} %all-gather.2.cloned.1.call-done.grad_ref.grad_hbm, ...), custom_call_target="tpu_custom_call" | custom-call | flops 17179869184 | bytes 39845888 | tf_op jit(solution)/shard_map/pallas_call | solution.py:932
  327.0 151.2 %shard_map.243 = (bf16[1024,2048]{1,0:T(8,128)(2,1)}, f32[256,2048]{1,0:T(8,128)}, f32[8,2048]{1,0:T(8,128)}, bf16[1024,2048]{1,0:T(8,128)(2,1)}, bf16[2048,1024]{1,0:T(8,128)(2,1)}) custom-call(bf16[1024,1024]{1,0:T(8,128)(2,1)} %get-tuple-element.79.d_gate_a, bf16[1024,1024]{1,0:T(8,128)(2,1)} %get-tuple-element.80.d_gate_b, ...), custom_call_target="tpu_custom_call" | custom-call | flops 17179869184 | bytes 262144000 | tf_op jit(solution)/shard_map/pallas_call | solution.py:872
  478.2 0.0 copy-start.10
  478.2 1.2 copy-done.10
  479.4 29.1 %shard_map.244 = (bf16[1024,512]{1,0:T(8,128)(2,1)S(1)}, bf16[1024,512]{1,0:T(8,128)(2,1)S(1)}, bf16[1024,512]{1,0:T(8,128)(2,1)S(1)}, f32[4,8,128]{2,1,0:T(8,128)S(1)}) custom-call(f32[4]{0:T(128)S(1)} %add_divide_fusion.gate_ref, s32[1]{0:T(128)} %bitcast.1.valid_ref, bf16[1024,2048]{1,0:T(8,128)(2,1)} %get-tuple-element.89.d_out_ref, ...), custom_call_target="tpu_custom_call" | custom-call | flops 7516192768 | bytes 104857600 | tf_op jit(solution)/shard_map/pallas_call | solution.py:1329
  508.5 19.6 %shard_map.245 = (bf16[1024,2048]{1,0:T(8,128)(2,1)}, bf16[2048,512]{1,0:T(8,128)(2,1)}, bf16[2048,512]{1,0:T(8,128)(2,1)}, bf16[2048,512]{1,0:T(8,128)(2,1)}, b...) custom-call(bf16[1024,2048]{1,0:T(8,128)(2,1)} %get-tuple-element.88.rows_ref, ...), custom_call_target="tpu_custom_call" | custom-call | flops 15032385536 | bytes 31457280 | tf_op jit(solution)/shard_map/pallas_call | solution.py:1086
  528.1 0.0 reduce-scatter.5.cloned.1.call-update
  528.2 0.0 copy-start.1
  528.2 0.0 copy-start.7
  528.2 0.0 reduce-scatter.3.cloned.1.call-start
  528.2 0.5 reduce-scatter.3.cloned.1.call-update
  528.8 0.6 copy-done.1
  529.4 0.3 fusion.7
  529.7 0.6 slice_multiply_fusion.1
  530.3 0.7 fusion.8
  531.0 0.1 slice_reduce_fusion
  531.1 0.1 broadcast_select_fusion
  531.2 0.1 select_n.65
  531.4 0.6 fusion.9.refs_0_
  532.0 114.9 %shard_map.246 = (f32[40,128]{1,0:T(8,128)}, bf16[2048,1024]{1,0:T(8,128)(2,1)}, bf16[512,2048]{1,0:T(8,128)(2,1)}, bf16[2048,512]{1,0:T(8,128)(2,1)}, bf16[2048...) custom-call(f32[40,128]{1,0:T(8,128)} %fusion.9.refs_0_, bf16[2048,1024]{1,0:T(8,128)(2,1)} %get-tuple-element.97.refs_1_, ...), custom_call_target="tpu_custom_call" | custom-call | bytes 377487360 | tf_op jit(solution)/shard_map/pallas_call | solution.py:265
  646.9 1.3 dynamic_slice.7
  648.2 1.3 slice_bitcast_fusion
  649.5 34.1 %shard_map.247 = (f32[2048,2048]{1,0:T(8,128)}, f32[2048,2048]{1,0:T(8,128)}, f32[2048,2048]{1,0:T(8,128)}, f32[512,2048]{1,0:T(8,128)}, f32[2048,512]{1,0:T(8,1...) custom-call(bf16[2048,1024]{1,0:T(8,128)(2,1)} %get-tuple-element.120.refs_0_, ...), custom_call_target="tpu_custom_call" | custom-call | bytes 100663296 | tf_op jit(solution)/shard_map/pallas_call | solution.py:1033
  683.6 0.0 reduce-scatter.5.cloned.1.call-done
  683.6 1.8 fusion.2
  685.4 0.0 reduce-scatter.3.cloned.1.call-done
  685.5 3.3 add_convert_fusion
  688.8 0.0 copy-done.13
  688.8 1.7 fusion.6
  (26 shorter events, 0.1 us)
Async XLA Ops:
  7.2 266.6 %all-gather.2.cloned.1.call-start = ((), (), s32[]{:S(2)}) async-start(), calls=%async_computation.2 | async-start | bytes 5242880 | tf_op jit(solution)/shard_map/all_gather | solution.py:1412
  7.2 1.2 copy-start
  8.5 0.7 copy-start.6
  9.2 75.5 %copy-start.17 = (s32[2]{0:T(128)S(1)}, s32[2]{0:T(128)}, u32[]{:S(2)}) copy-start(s32[2]{0:T(128)} %param.25) | copy-start | bytes 28
  84.5 14.1 %copy-start.8 = (bf16[1024,512]{1,0:T(8,128)(2,1)}, bf16[1024,512]{1,0:T(8,128)(2,1)S(1)}, u32[]{:S(2)}) copy-start(bf16[1024,512]{1,0:T(8,128)(2,1)S(1)} %get-tuple-element.69.key_ref) | copy-start | bytes 3145732
  84.6 14.1 %copy-start.11 = (bf16[1024,512]{1,0:T(8,128)(2,1)}, bf16[1024,512]{1,0:T(8,128)(2,1)S(1)}, u32[]{:S(2)}) copy-start(bf16[1024,512]{1,0:T(8,128)(2,1)S(1)} %get-tuple-element.70.value_ref) | copy-start | bytes 3145732
  84.6 564.9 %all-reduce.4.cloned.1.call-start = ((), (), s32[]{:S(2)}) async-start(), calls=%async_computation.5 | async-start | bytes 25165824 | tf_op jit(solution)/shard_map/psum | solution.py:1438
  88.7 22.2 %copy-start.5 = (f32[4,144,128]{2,1,0:T(8,128)}, f32[4,144,128]{2,1,0:T(8,128)S(1)}, u32[]{:S(2)}) copy-start(f32[4,144,128]{2,1,0:T(8,128)S(1)} %shard_map.238) | copy-start | bytes 884740
  88.7 22.2 %collective-permute-start.2 = (f32[4,144,128]{2,1,0:T(8,128)S(1)}, f32[4,144,128]{2,1,0:T(8,128)}, u32[]{:S(2)}, u32[]{:S(2)}) collective-permute-start(f32[4,144,128]{2,1,0:T(8,128)S(1)} %shard_map.238), channel_id=1, source_target_pairs={{0,12},{4,16},{8,20},{12,24},{16,28},{1,13},{5,17},{9,21},{13,25},... | collective-permute-start | bytes 884744 | tf_op jit(solution)/shard_map/ppermute | solution.py:1112
  91.4 19.5 %collective-permute-start.1 = (f32[4,144,128]{2,1,0:T(8,128)S(1)}, f32[4,144,128]{2,1,0:T(8,128)}, u32[]{:S(2)}, u32[]{:S(2)}) collective-permute-start(f32[4,144,128]{2,1,0:T(8,128)S(1)} %shard_map.238), channel_id=1, source_target_pairs={{0,8},{4,12},{8,16},{12,20},{16,24},{20,28},{1,9},{5,13},{9,17},{1... | collective-permute-start | bytes 884744 | tf_op jit(solution)/shard_map/ppermute | solution.py:1112
  95.5 15.4 %collective-permute-start = (f32[4,144,128]{2,1,0:T(8,128)S(1)}, f32[4,144,128]{2,1,0:T(8,128)}, u32[]{:S(2)}, u32[]{:S(2)}) collective-permute-start(f32[4,144,128]{2,1,0:T(8,128)S(1)} %shard_map.238), channel_id=1, source_target_pairs={{0,4},{4,8},{8,12},{12,16},{16,20},{20,24},{24,28},{1,5},{5,9},{9,... | collective-permute-start | bytes 884744 | tf_op jit(solution)/shard_map/ppermute | solution.py:1112
  98.7 1.2 copy-start.9
  99.9 1.2 copy-start.12
  101.1 9.7 %copy-start.18 = (f32[4]{0:T(128)S(1)}, f32[4]{0:T(128)}, u32[]{:S(2)}) copy-start(f32[4]{0:T(128)} %param.24) | copy-start | bytes 52
  110.8 4.7 copy-start.2
  115.6 1.0 copy-start.3
  300.9 382.7 %reduce-scatter.5.cloned.1.call-start = ((), (), s32[]{:S(2)}) async-start(), calls=%async_computation.4 | async-start | bytes 5242880 | tf_op jit(solution)/shard_map/reduce_scatter | solution.py:1482
  478.2 1.2 copy-start.10
  479.4 29.1 %copy-start.4 = (bf16[1024,512]{1,0:T(8,128)(2,1)S(1)}, bf16[1024,512]{1,0:T(8,128)(2,1)}, u32[]{:S(2)}) copy-start(bf16[1024,512]{1,0:T(8,128)(2,1)} %copy-done.3) | copy-start | bytes 3145732
  528.2 1.2 copy-start.1
  528.2 1.5 copy-start.15
  528.2 3.1 copy-start.16
  528.2 3.2 copy-start.7
  528.2 157.2 %reduce-scatter.3.cloned.1.call-start = ((), (), s32[]{:S(2)}) async-start(), calls=%async_computation.3 | async-start | bytes 5242880 | tf_op jit(solution)/shard_map/reduce_scatter | solution.py:1457
  685.4 3.4 copy-start.13
  685.5 3.3 copy-start.14
Sparse Core Ops, SparseCore 0:
  84.7 113.6 all-gather.1
  301.0 225.3 all-reduce.3
  528.8 76.8 reduce-scatter.4
  607.9 77.2 reduce-scatter.2

commit v4 on v3

--- a/solution.py
+++ b/solution.py
@@ -283,14 +283,15 @@
 
 
 ROWS = 32
-HOP = 2
+FIRST_HOP = 2
+SECOND_HOP = 3
 SEND_SLOTS = 4
 BLOCK_ROWS = 256
 UNIT_GROUP = 512
 LINE_REFS = 8
 
 
-def line_exchange(own, finish, before, scratch, extra=None, extra_steps=0):
+def line_exchange(own, finish, before, scratch, hop, extra, extra_steps):
     up_land, down_land, up_send, down_send, up_recv_sem, down_recv_sem, up_send_sem, down_send_sem = scratch
     size = lax.axis_size("head")
     place = lax.axis_index("head")
@@ -348,19 +349,19 @@
 
     def step(t, carry):
         before(t)
-        down = t - (last - place) * HOP
+        down = t - (last - place) * hop
 
         @pl.when((down >= 0) & (down < chunks))
         def _():
             pass_on(down, down_copy, down_land, down_send, place < last, place > 0)
 
-        up = t - place * HOP
+        up = t - place * hop
 
         @pl.when((up >= 0) & (up < chunks))
         def _():
             pass_on(up, up_copy, up_land, up_send, place > 0, place < last)
 
-        k = t - far * HOP
+        k = t - far * hop
 
         @pl.when((k >= 0) & (k < chunks))
         def _():
@@ -381,11 +382,10 @@
                     own[rows_of(k)] + up_land[slot].astype(F32) + down_land[slot].astype(F32),
                 )
 
-        if extra is not None:
-            extra(t)
+        extra(t)
         return carry
 
-    lax.fori_loop(0, max(chunks + last * HOP, extra_steps), step, 0)
+    lax.fori_loop(0, max(chunks + last * hop, extra_steps), step, 0)
     for k in range(chunks - SEND_SLOTS, chunks):
 
         @pl.when(place < last)
@@ -425,8 +425,8 @@
         pl.semaphore_wait(barrier, 1 + others)
 
 
-def line_scratch(size, width):
-    slots = (size - 1) * HOP + 2
+def line_scratch(size, width, hop):
+    slots = (size - 1) * hop + 2
     return [
         pltpu.VMEM((slots, ROWS, width), BF16),
         pltpu.VMEM((slots, ROWS, width), BF16),
@@ -624,7 +624,7 @@
     blocks = hidden.shape[0] // BLOCK_ROWS
     groups = w_gate.shape[1] // UNIT_GROUP
     slots = act.shape[0]
-    lag = per_block + (lax.axis_size("head") - 1) * HOP
+    lag = per_block + (lax.axis_size("head") - 1) * FIRST_HOP
     pace = per_block // groups
 
     def block_rows(b):
@@ -647,7 +647,8 @@
         return pltpu.make_async_copy(flip, flip_ref.at[:, block_rows(b)], block_sem.at[0])
 
     def part_copy(b):
-        return pltpu.make_async_copy(part_out, part_ref.at[block_rows(b)], block_sem.at[1])
+        where = (block_rows(b), pl.ds(0, part_out.shape[1]))
+        return pltpu.make_async_copy(part_out, part_ref.at[where], block_sem.at[1])
 
     def forward(u):
         slot = lax.rem(u, slots)
@@ -728,7 +729,7 @@
         def _():
             store(k // per_block).start()
 
-    line_exchange(hidden, finish, before, scratch, after, lag + blocks * per_block)
+    line_exchange(hidden, finish, before, scratch, FIRST_HOP, after, lag + blocks * per_block)
     for b in range(blocks):
         store(b).wait()
     flip_copy(blocks - 1).wait()
@@ -753,7 +754,7 @@
             jax.ShapeDtypeStruct((rows, units), F32),
             jax.ShapeDtypeStruct((rows, units), F32),
             jax.ShapeDtypeStruct((rows, units), BF16),
-            jax.ShapeDtypeStruct((rows, width), BF16),
+            jax.ShapeDtypeStruct((rows, 2 * width), BF16),
         ],
         scratch_shapes=[
             pltpu.VMEM((rows, width), F32),
@@ -772,7 +773,7 @@
             pltpu.SemaphoreType.DMA((3, slots)),
             pltpu.SemaphoreType.DMA((2,)),
         ]
-        + line_scratch(size, width),
+        + line_scratch(size, width, FIRST_HOP),
         cost_estimate=pl.CostEstimate(
             flops=2 * rows * width * (mixed.shape[1] + 3 * units),
             bytes_accessed=250 * 2**20,
@@ -856,7 +857,7 @@
         def _():
             store(k // per_block).start()
 
-    line_exchange(own, finish, before, scratch[:LINE_REFS], engine_step, steps)
+    line_exchange(own, finish, before, scratch[:LINE_REFS], SECOND_HOP, engine_step, steps)
     for b in range(blocks):
         store(b).wait()
 
@@ -890,7 +891,7 @@
             pltpu.SemaphoreType.DMA((8,)),
             pltpu.SemaphoreType.DMA((blocks,)),
         ]
-        + line_scratch(size, width)
+        + line_scratch(size, width, SECOND_HOP)
         + engine_scratch(tile, seg_bits),
         cost_estimate=pl.CostEstimate(
             flops=4 * rows * width * units, bytes_accessed=250 * 2**20, transcendentals=0
@@ -1050,7 +1051,7 @@
 
 def attn_weights_kernel(
     rows_ref, d_out_ref, mixed_ref, d_query_ref, d_key_ref, d_value_ref,
-    w_query_ref, w_key_ref, w_value_ref,
+    w_query_ref, w_key_ref, w_value_ref, pair_ref,
     d_rows_ref, grad_query_ref, grad_key_ref, grad_value_ref, grad_out_ref, gain_part_ref,
     flipped_mixed, flipped_rows,
 ):
@@ -1073,29 +1074,32 @@
     grad_out_ref[...] = dot(flipped_mixed[...], d_out_ref[...], NN).astype(BF16)
 
 
-def attn_weights(rows, d_out, mixed, d_query, d_key, d_value, w_query, w_key, w_value):
+def attn_weights(rows, d_out, mixed, d_query, d_key, d_value, w_query, w_key, w_value, pair):
     count, width = rows.shape
     cols = mixed.shape[1]
     block = 512
     once = pl.Buffered(1)
     slim = pl.BlockSpec((count, cols), lambda j: (0, 0), pipeline_mode=once)
     side = pl.BlockSpec((count, block), lambda j: (0, j))
+    right = pl.BlockSpec((count, block), lambda j: (0, width // block + j))
     tall = pl.BlockSpec((block, cols), lambda j: (j, 0))
     wide = pl.BlockSpec((cols, block), lambda j: (0, j))
     tall_type = jax.ShapeDtypeStruct((width, cols), BF16)
     return pl.pallas_call(
         attn_weights_kernel,
         grid=(width // block,),
-        in_specs=[side, side, slim, slim, slim, slim, tall, tall, tall],
-        out_specs=[side, tall, tall, tall, wide, pl.BlockSpec((8, block), lambda j: (0, j))],
+        in_specs=[side, side, slim, slim, slim, slim, tall, tall, tall]
+        + [pl.BlockSpec(memory_space=pltpu.HBM)],
+        out_specs=[right, tall, tall, tall, wide, pl.BlockSpec((8, block), lambda j: (0, j))],
         out_shape=[
-            jax.ShapeDtypeStruct((count, width), BF16),
+            jax.ShapeDtypeStruct(pair.shape, BF16),
             tall_type,
             tall_type,
             tall_type,
             jax.ShapeDtypeStruct((cols, width), BF16),
             jax.ShapeDtypeStruct((8, width), F32),
         ],
+        input_output_aliases={9: 0},
         scratch_shapes=[pltpu.VMEM((cols, count), BF16), pltpu.VMEM((block, count), BF16)],
         cost_estimate=pl.CostEstimate(
             flops=14 * count * width * cols,
@@ -1103,13 +1107,7 @@
             transcendentals=0,
         ),
         compiler_params=pltpu.CompilerParams(vmem_limit_bytes=48 * 2**20),
-    )(rows, d_out, mixed, d_query, d_key, d_value, w_query, w_key, w_value)
-
-
-def from_behind(value, axis, steps):
-    count = lax.axis_size(axis)
-    initial, last = (max(0, -steps), min(count, count - steps))
-    return lax.ppermute(value, axis, [(source, source + steps) for source in range(initial, last)])
+    )(rows, d_out, mixed, d_query, d_key, d_value, w_query, w_key, w_value, pair)
 
 
 def elu_plus(values):
@@ -1161,14 +1159,6 @@
     return (lax.broadcasted_iota(jnp.int32, (SEG_LEN, 1), 0) < valid_len).astype(F32)
 
 
-def update_kernel(valid_ref, key_ref, value_ref, out_ref):
-    key_feat = elu_plus(key_ref[...].astype(F32)) * valid_column(valid_ref[0])
-    out_ref[0, :DH] = fine_dot(key_feat, value_ref[...], TN)
-    out_ref[0, DH:] = jnp.broadcast_to(
-        jnp.sum(key_feat, axis=0, keepdims=True), (MEM_ROWS - DH, DH)
-    )
-
-
 def block_probs(query_block, key_rows, start, valid_len):
     scores = dot(query_block, key_rows, NT) * (DH**-0.5)
     row_pos = start + lax.broadcasted_iota(jnp.int32, scores.shape, 0)
@@ -1179,25 +1169,10 @@
     return weights / jnp.sum(weights, axis=-1, keepdims=True)
 
 
-def local_kernel(valid_ref, query_ref, key_ref, value_ref, out_ref):
-    for start in range(0, SEG_LEN, BLOCK):
-        rows = slice(start, start + BLOCK)
-        key_rows = key_ref[: start + BLOCK]
-        probs = block_probs(query_ref[rows], key_rows, start, valid_ref[0])
-        out_ref[rows] = dot(probs.astype(BF16), value_ref[: start + BLOCK], NN)
-
-
 def retrieve(query_feat, memory, normal):
     numerator = fine_dot(query_feat, memory, NN)
     denominator = jnp.sum(query_feat * normal, axis=-1, keepdims=True) + 1.0
     return numerator / denominator, denominator
-
-
-def mix_kernel(gate_ref, query_ref, local_ref, memory_ref, out_ref):
-    gate = gate_ref[pl.program_id(0)]
-    query_feat = elu_plus(query_ref[...].astype(F32))
-    retrieved, _ = retrieve(query_feat, memory_ref[0, :DH], memory_ref[0, DH : DH + 1])
-    out_ref[...] = (gate * retrieved + (1.0 - gate) * local_ref[...]).astype(BF16)
 
 
 def greet_sequence():
@@ -1231,6 +1206,93 @@
 
 def head_cols(head):
     return pl.ds(pl.multiple_of(head * DH, DH), DH)
+
+
+def attn_front_kernel(
+    gate_ref, valid_ref, query_ref, key_ref, value_ref,
+    mixed_ref, local_ref, before_ref, update_ref,
+    land, send_sem, recv_sem,
+):
+    heads = update_ref.shape[0]
+    valid_len = valid_ref[0]
+    greet_sequence()
+    copies = sequence_copies(update_ref, land, send_sem, recv_sem, 1)
+
+    def make_update(head, carry):
+        cols = head_cols(head)
+        key_feat = elu_plus(key_ref[:, cols].astype(F32)) * valid_column(valid_len)
+        update_ref[head, :DH] = fine_dot(key_feat, value_ref[:, cols], TN)
+        normal = jnp.sum(key_feat, axis=0, keepdims=True)
+        update_ref[head, DH:] = jnp.broadcast_to(normal, (MEM_ROWS - DH, DH))
+        return carry
+
+    lax.fori_loop(0, heads, make_update, 0)
+    for copy, sends, _ in copies:
+
+        @pl.when(sends)
+        def _(copy=copy):
+            copy.start()
+
+    def local(head, carry):
+        cols = head_cols(head)
+        for start in range(0, SEG_LEN, BLOCK):
+            rows, seen = slice(start, start + BLOCK), slice(0, start + BLOCK)
+            probs = block_probs(query_ref[rows, cols], key_ref[seen, cols], start, valid_len)
+            local_ref[rows, cols] = dot(probs.astype(BF16), value_ref[seen, cols], NN)
+        return carry
+
+    lax.fori_loop(0, heads, local, 0)
+    before_ref[...] = jnp.zeros_like(before_ref)
+    for distance, (copy, sends, gets) in enumerate(copies):
+
+        @pl.when(sends)
+        def _(copy=copy):
+            copy.wait_send()
+
+        @pl.when(gets)
+        def _(copy=copy, distance=distance):
+            copy.wait_recv()
+            before_ref[...] += land[distance]
+
+    def mix(head, carry):
+        cols = head_cols(head)
+        gate = gate_ref[head]
+        query_feat = elu_plus(query_ref[:, cols].astype(F32))
+        memory, normal = before_ref[head, :DH], before_ref[head, DH : DH + 1]
+        retrieved, _ = retrieve(query_feat, memory, normal)
+        mixed_ref[:, cols] = (gate * retrieved + (1.0 - gate) * local_ref[:, cols]).astype(BF16)
+        return carry
+
+    lax.fori_loop(0, heads, mix, 0)
+
+
+def attn_front(gate, valid, query, key, value, cid):
+    rows, cols = query.shape
+    heads = cols // DH
+    scalar, vmem = pl.BlockSpec(memory_space=pltpu.SMEM), pl.BlockSpec(memory_space=pltpu.VMEM)
+    memory = jax.ShapeDtypeStruct((heads, MEM_ROWS, DH), F32)
+    return pl.pallas_call(
+        attn_front_kernel,
+        in_specs=[scalar] * 2 + [vmem] * 3,
+        out_specs=[vmem] * 4,
+        out_shape=[
+            jax.ShapeDtypeStruct((rows, cols), BF16),
+            jax.ShapeDtypeStruct((rows, cols), F32),
+            memory,
+            memory,
+        ],
+        scratch_shapes=[
+            pltpu.VMEM((SEGS - 1, heads, MEM_ROWS, DH), F32),
+            pltpu.SemaphoreType.DMA((SEGS - 1,)),
+            pltpu.SemaphoreType.DMA((SEGS - 1,)),
+        ],
+        cost_estimate=pl.CostEstimate(
+            flops=4 * rows * rows * cols, bytes_accessed=60 * 2**20, transcendentals=rows * rows * heads
+        ),
+        compiler_params=pltpu.CompilerParams(
+            collective_id=cid, has_side_effects=True, vmem_limit_bytes=40 * 2**20
+        ),
+    )(gate, valid, query, key, value)
 
 
 def attn_back_kernel(
@@ -1353,26 +1415,6 @@
     )(gate, valid, d_out, weight, query, key, value, local, memory)
 
 
-SCALAR = pl.BlockSpec(memory_space=pltpu.SMEM)
-COLUMN = pl.BlockSpec((SEG_LEN, DH), lambda head: (0, head))
-MEMORY = pl.BlockSpec((1, MEM_ROWS, DH), lambda head: (head, 0, 0))
-
-
-def per_head(kernel, heads, in_specs, out_specs, out_types, flops, transcendentals=0):
-    moved = heads * SEG_LEN * DH * 4 * len(in_specs)
-    return pl.pallas_call(
-        kernel,
-        grid=(heads,),
-        in_specs=in_specs,
-        out_specs=out_specs,
-        out_shape=out_types,
-        cost_estimate=pl.CostEstimate(
-            flops=flops, bytes_accessed=moved, transcendentals=transcendentals
-        ),
-        compiler_params=pltpu.CompilerParams(vmem_limit_bytes=40 * 1024 * 1024),
-    )
-
-
 def per_device(
     tokens,
     cotangent,
@@ -1398,11 +1440,6 @@
     valid_len = jnp.where(position == SEGS - 1, seq_length, SEG_LEN).reshape(1)
     heads = mem_gate.shape[0]
     cols = heads * DH
-    col_f32 = jax.ShapeDtypeStruct((SEG_LEN, cols), F32)
-    col_bf16 = jax.ShapeDtypeStruct((SEG_LEN, cols), BF16)
-    mem_f32 = jax.ShapeDtypeStruct((heads, MEM_ROWS, DH), F32)
-    unit = 2 * heads * SEG_LEN * DH * DH
-    pairs = heads * SEG_LEN * SEG_LEN
 
     token_vals = tokens.astype(F32)
     gathered_tokens, gathered_attn, query_rows, key_rows, value_rows = gather_project(
@@ -1410,24 +1447,14 @@
     )
     cotangent, key_rows = lax.optimization_barrier((cotangent, key_rows))
     gathered_grad = lax.all_gather(cotangent, "head", axis=0, tiled=True)
-    update = per_head(update_kernel, heads, [SCALAR, COLUMN, COLUMN], MEMORY, mem_f32, 6 * unit)(
-        valid_len, key_rows, value_rows
+    mix_sig = jax.nn.sigmoid(mem_gate)
+    mixed_attn, local_attn, memory_prev, update = attn_front(
+        mix_sig, valid_len, query_rows, key_rows, value_rows, 5
     )
-    memory_prev = jnp.zeros_like(update)
-    for distance in range(1, SEGS):
-        moved = from_behind(update, "seg", distance)
-        memory_prev = memory_prev + jnp.where(position >= distance, moved, 0.0)
-    local_attn = per_head(
-        local_kernel, heads, [SCALAR, COLUMN, COLUMN, COLUMN], COLUMN, col_f32, 4 * pairs * DH, pairs
-    )(valid_len, query_rows, key_rows, value_rows)
     after = memory_prev + update
     memory_after = (after[:, :DH] * SEG_LEN ** (-0.5))[None]
     normal_after = (after[:, DH] / SEG_LEN)[None]
-    mix_sig = jax.nn.sigmoid(mem_gate)
-    mixed_attn = per_head(
-        mix_kernel, heads, [SCALAR, COLUMN, COLUMN, MEMORY], COLUMN, col_bf16, 6 * unit
-    )(mix_sig, query_rows, local_attn, memory_prev)
-    all_hidden, flip_mlp, silu, slope, act, mlp_part = attn_out_sum(
+    all_hidden, flip_mlp, silu, slope, act, pair = attn_out_sum(
         mixed_attn, w_out, gathered_tokens, gain_mlp, w_gate, w_up, w_down, head_groups, 1
     )
     own_rows = tokens.shape[0]
@@ -1453,9 +1480,6 @@
         head_groups,
         2,
     )
-    mlp_part, gathered_hidden = lax.optimization_barrier((mlp_part, gathered_hidden))
-    mlp_out = lax.psum_scatter(mlp_part, "head", scatter_dimension=0, tiled=True)
-    output = (hidden_res + mlp_out.astype(F32)).astype(BF16)
     d_queries, d_keys, d_values, gate_cols = attn_back(
         mix_sig,
         valid_len,
@@ -1468,7 +1492,7 @@
         memory_prev,
         3,
     )
-    d_part, grad_query, grad_key, grad_value, grad_out, gain_attn_rows = attn_weights(
+    pair, grad_query, grad_key, grad_value, grad_out, gain_attn_rows = attn_weights(
         gathered_attn,
         gathered_hidden,
         mixed_attn,
@@ -1478,15 +1502,18 @@
         w_query,
         w_key,
         w_value,
+        pair,
     )
-    d_normed_attn = lax.psum_scatter(d_part, "head", scatter_dimension=0, tiled=True).astype(F32)
+    width = gain_attn.shape[0]
+    pair = lax.psum_scatter(pair, "head", scatter_dimension=0, tiled=True).astype(F32)
+    output = (hidden_res + pair[:, :width]).astype(BF16)
+    d_normed_attn = pair[:, width:]
     grad_in_attn = norm_backward(token_vals, inverse_rms(token_vals), gain_attn, d_normed_attn)
     grad_tokens = (d_hidden + grad_in_attn).astype(BF16)
     gate_part = mix_sig * (1.0 - mix_sig) * jnp.sum(gate_cols[:, 0], axis=-1)
     slots = jnp.where(
         (lax.iota(jnp.int32, head_groups) == head_index)[:, None], gate_part[None], 0.0
     )
-    width = gain_attn.shape[0]
     gain_attn_part = jnp.sum(gain_attn_rows, axis=0) / gain_attn
     gain_mlp_part = jnp.sum(gain_mlp_rows, axis=0)
     parts = jnp.concatenate([gain_attn_part, gain_mlp_part, slots.reshape(-1)])

time: 705 us -> 700 us (level)
  starting transfers between devices: 10.6 us -> 0.33 us
    ppermute x3 -> x0, starting transfers between devices: 10 us -> none  [from_behind(): lax.ppermute(value, axis, [(source, source + steps) for source in range(i...]
    pallas_call x1, Pallas kernels: 151 us -> 141 us  [mlp_back_sum(): pl.pallas_call(functools.partial(mlp_back_kernel, tile, seg_bits), in_spe...]
    pallas_call x1, Pallas kernels: 157 us -> 167 us  [attn_out_sum(): pl.pallas_call(attn_out_kernel, in_specs=[vmem] * 4 + [any_] * 3, out_spe...]
    pallas_call x3 -> x1, Pallas kernels: 14.9 us -> 19 us  [attn_front(): pl.pallas_call(attn_front_kernel, in_specs=[scalar] * 2 + [vmem] * 3, out...]
  transfers between devices with their start and end apart: 7 -> 3, of which waited for: 0 -> 0; matrix products, arithmetic and copies ran while one was open for 1% -> 1% of each run, Pallas kernels for 78% -> 80%
where the time goes in v4:
time: 700 us; the launch traced here: 692 us
  Pallas kernels  654 us (93%)
  between operations  15.2 us (2%)
  local copies, waits for them, and re-layouts  12.5 us (2%)
  other arithmetic  9.42 us (1%)
    pallas_call x1, Pallas kernels, attn_out_sum(): pl.pallas_call(attn_out_kernel, in_specs=[vmem] * 4 + [any_] * 3, out_spe...  167 us
    pallas_call x1, Pallas kernels, mlp_back_sum(): pl.pallas_call(functools.partial(mlp_back_kernel, tile, seg_bits), in_spe...  141 us
    pallas_call x1, Pallas kernels, grad_sum(): pl.pallas_call(functools.partial(grad_sum_kernel, count, tile, seg_bits,...  115 us
    pallas_call x1, Pallas kernels, gather_project(): pl.pallas_call(gather_kernel, in_specs=[any_, vmem] + [any_] * 3, out_spe...  75.4 us
    pallas_call x2, Pallas kernels, mlp_half(): pl.pallas_call(mlp_kernel, grid=(units // block,), in_specs=[pl.BlockSpec...  53.6 us
    pallas_call x1, Pallas kernels, widen(): pl.pallas_call(functools.partial(widen_kernel, shapes, places, len(target...  34.2 us
    pallas_call x1, Pallas kernels, attn_back(): pl.pallas_call(attn_back_kernel, in_specs=[scalar] * 2 + [vmem] * 7, out_...  29.1 us
    pallas_call x1, Pallas kernels, attn_weights(): pl.pallas_call(attn_weights_kernel, grid=(width // block,), in_specs=[sid...  19.5 us
  transfers between devices with their start and end apart: 3, of which 0 were waited for; matrix products, arithmetic and copies ran while one was open for 1% of the time, Pallas kernels for 80%

profile of v4, /device:TPU:0, one launch (start us, length us, event | category | flops | bytes accessed | tf_op | source)
XLA Modules:
  0.0 691.8 jit_solution(9085138461294819519)
XLA Ops:
  7.2 0.0 all-gather.2.cloned.1.call-start
  7.2 0.0 copy-start
  7.2 1.2 copy-done
  8.5 0.0 copy-start.2
  8.5 0.7 copy-done.2
  9.2 0.0 copy-start.13
  9.2 0.0 copy-start.14
  9.2 75.4 %shard_map.236 = (bf16[1024,2048]{1,0:T(8,128)(2,1)}, bf16[1024,2048]{1,0:T(8,128)(2,1)}, bf16[1024,512]{1,0:T(8,128)(2,1)S(1)}, bf16[1024,512]{1,0:T(8,128)(2,1)S(1)}, bf16[1024,512]{1,0:T(8,128)(2,1)S(1)}) custom-call(bf16[256,2048]{1,0:T(8,128)(2,1)S(1)} %copy-done, f32[1,2048]{1,0:T(1,128)S(1)} %bitcast.13, bf16[2048,512]{1,0:T(8,128)(2,1)} %w_query_ref.1, ...), custom_call_target="tpu_custom_call" | custom-call | flops 6442450944 | bytes 157286400 | tf_op jit(solution)/shard_map/pallas_call | solution.py:578
  84.5 0.0 copy-start.7
  84.6 1.0 copy-done.7
  85.5 0.0 copy-start.5
  85.5 0.0 all-gather.2.cloned.1.call-update
  85.5 0.0 all-reduce.4.cloned.1.call-start
  85.6 0.0 copy-done.13
  85.6 0.7 fusion.12
  87.0 0.0 copy-done.14
  87.1 0.0 copy-start.8
  87.1 1.2 copy-done.8
  88.3 19.0 %shard_map.237 = (bf16[1024,512]{1,0:T(8,128)(2,1)S(1)}, f32[1024,512]{1,0:T(8,128)S(1)}, f32[4,144,128]{2,1,0:T(8,128)S(1)}, f32[4,144,128]{2,1,0:T(8,128)S(1)}) custom-call(f32[4]{0:T(128)S(1)} %add_divide_fusion.gate_ref, s32[1]{0:T(128)} %bitcast.valid_ref, bf16[1024,512]{1,0:T(8,128)(2,1)S(1)} %get-tuple-element.69.query_ref, ...), custom_call_target="tpu_custom_call" | custom-call | flops 2147483648 | bytes 62914560 | tf_op jit(solution)/shard_map/pallas_call | solution.py:1274
  107.3 0.0 copy-done.5
  107.3 0.0 copy-start.4
  107.3 1.3 copy-done.4
  108.7 0.0 copy-start.9
  108.7 1.0 copy-done.9
  109.6 166.7 %shard_map.238 = (f32[1024,2048]{1,0:T(8,128)}, bf16[2048,1024]{1,0:T(8,128)(2,1)}, f32[1024,2048]{1,0:T(8,128)}, f32[1024,2048]{1,0:T(8,128)}, bf16[1024,2048]{1,0:T(8,128)(2,1)}, /*index=5*/bf16[1024,4096]{1,0:T(8,128)(2,1)}) custom-call(bf16[1024,512]{1,0:T(8,128)(2,1)} %copy-done.9, bf16[512,2048]{1,0:T(8,128)(2,1)} %weight_ref.3, ...), custom_call_target="tpu_custom_call" | custom-call | flops 27917287424 | bytes 262144000 | tf_op jit(solution)/shard_map/pallas_call | solution.py:747
  276.4 0.0 all-gather.2.cloned.1.call-done.grad_ref.grad_hbm
  276.4 27.1 %shard_map.239 = (bf16[1024,1024]{1,0:T(8,128)(2,1)}, bf16[1024,1024]{1,0:T(8,128)(2,1)}, bf16[2048,1024]{1,0:T(8,128)(2,1)}, bf16[2048,1024]{1,0:T(8,128)(2,1)}, bf16[1024,2048]{1,0:T(8,128)(2,1)}) custom-call(bf16[2048,1024]{1,0:T(8,128)(2,1)} %get-tuple-element.77.flip_ref, bf16[1024,2048]{1,0:T(8,128)(2,1)} %all-gather.2.cloned.1.call-done.grad_ref.grad_hbm, ...), custom_call_target="tpu_custom_call" | custom-call | flops 17179869184 | bytes 39845888 | tf_op jit(solution)/shard_map/pallas_call | solution.py:933
  303.5 0.0 all-reduce.4.cloned.1.call-update
  303.6 0.3 reduce-scatter.2.cloned.1.call-start
  303.8 26.5 %shard_map.240 = (bf16[1024,1024]{1,0:T(8,128)(2,1)}, bf16[1024,1024]{1,0:T(8,128)(2,1)}, bf16[2048,1024]{1,0:T(8,128)(2,1)}, bf16[2048,1024]{1,0:T(8,128)(2,1)}, bf16[1024,2048]{1,0:T(8,128)(2,1)}) custom-call(bf16[2048,1024]{1,0:T(8,128)(2,1)} %get-tuple-element.77.flip_ref, bf16[1024,2048]{1,0:T(8,128)(2,1)} %all-gather.2.cloned.1.call-done.grad_ref.grad_hbm, ...), custom_call_target="tpu_custom_call" | custom-call | flops 17179869184 | bytes 39845888 | tf_op jit(solution)/shard_map/pallas_call | solution.py:933
  330.3 141.4 %shard_map.241 = (bf16[1024,2048]{1,0:T(8,128)(2,1)}, f32[256,2048]{1,0:T(8,128)}, f32[8,2048]{1,0:T(8,128)}, bf16[1024,2048]{1,0:T(8,128)(2,1)}, bf16[2048,1024]{1,0:T(8,128)(2,1)}) custom-call(bf16[1024,1024]{1,0:T(8,128)(2,1)} %get-tuple-element.82.d_gate_a, bf16[1024,1024]{1,0:T(8,128)(2,1)} %get-tuple-element.83.d_gate_b, ...), custom_call_target="tpu_custom_call" | custom-call | flops 17179869184 | bytes 262144000 | tf_op jit(solution)/shard_map/pallas_call | solution.py:873
  471.7 0.0 copy-start.6
  471.7 1.2 copy-done.6
  472.9 0.0 copy-start.10
  472.9 29.1 %shard_map.242 = (bf16[1024,512]{1,0:T(8,128)(2,1)S(1)}, bf16[1024,512]{1,0:T(8,128)(2,1)S(1)}, bf16[1024,512]{1,0:T(8,128)(2,1)S(1)}, f32[4,8,128]{2,1,0:T(8,128)S(1)}) custom-call(f32[4]{0:T(128)S(1)} %add_divide_fusion.gate_ref, s32[1]{0:T(128)} %bitcast.valid_ref, bf16[1024,2048]{1,0:T(8,128)(2,1)} %get-tuple-element.88.d_out_ref, ...), custom_call_target="tpu_custom_call" | custom-call | flops 7516192768 | bytes 104857600 | tf_op jit(solution)/shard_map/pallas_call | solution.py:1391
  502.1 0.0 copy-done.10
  502.1 19.5 %shard_map.243 = (bf16[1024,4096]{1,0:T(8,128)(2,1)}, bf16[2048,512]{1,0:T(8,128)(2,1)}, bf16[2048,512]{1,0:T(8,128)(2,1)}, bf16[2048,512]{1,0:T(8,128)(2,1)}, b...) custom-call(bf16[1024,2048]{1,0:T(8,128)(2,1)} %get-tuple-element.76.rows_ref, ...), custom_call_target="tpu_custom_call", output_to_operand_aliasing={{0}: (9, {})} | custom-call | flops 15032385536 | bytes 31457280 | tf_op jit(solution)/shard_map/pallas_call | solution.py:1088
  521.6 0.0 copy-start.1
  521.6 0.0 reduce-scatter.2.cloned.1.call-update
  521.7 0.0 copy-start.12
  521.7 0.0 copy-start.3
  521.7 1.1 copy-done.1
  522.9 0.3 fusion.7
  523.2 0.6 slice_multiply_fusion.2
  523.7 0.7 fusion.9
  524.5 0.1 slice_reduce_fusion
  524.6 0.1 broadcast_select_fusion
  524.7 0.1 select_n.39
  524.8 0.0 copy-done.12
  524.8 0.0 copy-done.3
  524.8 0.6 fusion.10.refs_0_
  525.5 115.2 %shard_map.244 = (f32[40,128]{1,0:T(8,128)}, bf16[2048,1024]{1,0:T(8,128)(2,1)}, bf16[512,2048]{1,0:T(8,128)(2,1)}, bf16[2048,512]{1,0:T(8,128)(2,1)}, bf16[2048...) custom-call(f32[40,128]{1,0:T(8,128)} %fusion.10.refs_0_, bf16[2048,1024]{1,0:T(8,128)(2,1)} %get-tuple-element.101.refs_1_, ...), custom_call_target="tpu_custom_call" | custom-call | bytes 377487360 | tf_op jit(solution)/shard_map/pallas_call | solution.py:265
  640.7 1.3 dynamic_slice.7
  641.9 1.3 slice_bitcast_fusion
  643.2 0.0 all-reduce.4.cloned.1.call-done
  643.3 34.2 %shard_map.245 = (f32[2048,2048]{1,0:T(8,128)}, f32[2048,2048]{1,0:T(8,128)}, f32[2048,2048]{1,0:T(8,128)}, f32[512,2048]{1,0:T(8,128)}, f32[2048,512]{1,0:T(8,1...) custom-call(bf16[2048,1024]{1,0:T(8,128)(2,1)} %get-tuple-element.124.refs_0_, ...), custom_call_target="tpu_custom_call" | custom-call | bytes 100663296 | tf_op jit(solution)/shard_map/pallas_call | solution.py:1034
  677.5 0.0 reduce-scatter.2.cloned.1.call-done
  677.5 2.1 convert_element_type.14
  679.6 0.0 copy-start.11
  679.6 0.5 fusion.2
  680.1 1.1 copy-done.11
  681.2 3.6 fusion.6
  (9 shorter events, 0.1 us)
Async XLA Ops:
  7.2 269.2 %all-gather.2.cloned.1.call-start = ((), (), s32[]{:S(2)}) async-start(), calls=%async_computation.1 | async-start | bytes 5242880 | tf_op jit(solution)/shard_map/all_gather | solution.py:1449
  7.2 1.2 copy-start
  8.5 0.7 copy-start.2
  9.2 76.5 %copy-start.13 = (s32[2]{0:T(128)S(1)}, s32[2]{0:T(128)}, u32[]{:S(2)}) copy-start(s32[2]{0:T(128)} %param.25) | copy-start | bytes 28
  9.2 77.9 %copy-start.14 = (f32[4]{0:T(128)S(1)}, f32[4]{0:T(128)}, u32[]{:S(2)}) copy-start(f32[4]{0:T(128)} %param.24) | copy-start | bytes 52
  84.5 1.0 copy-start.7
  85.5 21.8 %copy-start.5 = (bf16[1024,512]{1,0:T(8,128)(2,1)}, bf16[1024,512]{1,0:T(8,128)(2,1)S(1)}, u32[]{:S(2)}) copy-start(bf16[1024,512]{1,0:T(8,128)(2,1)S(1)} %get-tuple-element.71.key_ref) | copy-start | bytes 3145732
  85.5 557.7 %all-reduce.4.cloned.1.call-start = ((), (), s32[]{:S(2)}) async-start(), calls=%async_computation.3 | async-start | bytes 25165824 | tf_op jit(solution)/shard_map/psum | solution.py:1465
  87.1 1.2 copy-start.8
  107.3 1.3 copy-start.4
  108.7 1.0 copy-start.9
  303.6 373.9 %reduce-scatter.2.cloned.1.call-start = ((), (), s32[]{:S(2)}) async-start(), calls=%async_computation.2 | async-start | bytes 10485760 | tf_op jit(solution)/shard_map/reduce_scatter | solution.py:1508
  471.7 1.2 copy-start.6
  472.9 29.1 %copy-start.10 = (bf16[1024,512]{1,0:T(8,128)(2,1)S(1)}, bf16[1024,512]{1,0:T(8,128)(2,1)}, u32[]{:S(2)}) copy-start(bf16[1024,512]{1,0:T(8,128)(2,1)} %copy-done.9) | copy-start | bytes 3145732
  521.6 1.2 copy-start.1
  521.7 3.1 copy-start.12
  521.7 3.1 copy-start.3
  679.6 1.6 copy-start.11
Sparse Core Ops, SparseCore 0:
  85.7 118.3 all-gather.1
  303.7 223.7 all-reduce.3
  529.9 145.2 reduce-scatter.1

commit v5 on v4

--- a/solution.py
+++ b/solution.py
@@ -287,6 +287,7 @@
 SECOND_HOP = 3
 SEND_SLOTS = 4
 BLOCK_ROWS = 256
+FORWARD_ROWS = 128
 UNIT_GROUP = 512
 LINE_REFS = 8
 
@@ -620,15 +621,15 @@
     for load in loads:
         load.start()
     line_barrier()
-    per_block = BLOCK_ROWS // ROWS
-    blocks = hidden.shape[0] // BLOCK_ROWS
+    per_block = FORWARD_ROWS // ROWS
+    blocks = hidden.shape[0] // FORWARD_ROWS
     groups = w_gate.shape[1] // UNIT_GROUP
     slots = act.shape[0]
     lag = per_block + (lax.axis_size("head") - 1) * FIRST_HOP
     pace = per_block // groups
 
     def block_rows(b):
-        return pl.ds(pl.multiple_of(b * BLOCK_ROWS, BLOCK_ROWS), BLOCK_ROWS)
+        return pl.ds(pl.multiple_of(b * FORWARD_ROWS, FORWARD_ROWS), FORWARD_ROWS)
 
     def unit_copies(u):
         slot = lax.rem(u, slots)
@@ -743,7 +744,7 @@
     rows, width = tokens.shape
     units = w_gate.shape[1]
     vmem, any_ = pl.BlockSpec(memory_space=pltpu.VMEM), pl.BlockSpec(memory_space=pltpu.HBM)
-    blocks, slots = rows // BLOCK_ROWS, 2
+    blocks, slots = rows // FORWARD_ROWS, 2
     return pl.pallas_call(
         attn_out_kernel,
         in_specs=[vmem] * 4 + [any_] * 3,
@@ -762,12 +763,12 @@
             pltpu.VMEM((width, units), BF16),
             pltpu.VMEM((width, units), BF16),
             pltpu.VMEM((units, width), BF16),
-            pltpu.VMEM((slots, BLOCK_ROWS, UNIT_GROUP), F32),
-            pltpu.VMEM((slots, BLOCK_ROWS, UNIT_GROUP), F32),
-            pltpu.VMEM((slots, BLOCK_ROWS, UNIT_GROUP), BF16),
-            pltpu.VMEM((width, BLOCK_ROWS), BF16),
-            pltpu.VMEM((BLOCK_ROWS, width), F32),
-            pltpu.VMEM((BLOCK_ROWS, width), BF16),
+            pltpu.VMEM((slots, FORWARD_ROWS, UNIT_GROUP), F32),
+            pltpu.VMEM((slots, FORWARD_ROWS, UNIT_GROUP), F32),
+            pltpu.VMEM((slots, FORWARD_ROWS, UNIT_GROUP), BF16),
+            pltpu.VMEM((width, FORWARD_ROWS), BF16),
+            pltpu.VMEM((FORWARD_ROWS, width), F32),
+            pltpu.VMEM((FORWARD_ROWS, width), BF16),
             pltpu.SemaphoreType.DMA((blocks,)),
             pltpu.SemaphoreType.DMA((3,)),
             pltpu.SemaphoreType.DMA((3, slots)),
@@ -819,16 +820,23 @@
     def block_rows(b):
         return pl.ds(pl.multiple_of(b * BLOCK_ROWS, BLOCK_ROWS), BLOCK_ROWS)
 
-    for load in loads[:6]:
+    for load in loads[:3]:
         load.wait()
 
     def before(t):
         @pl.when((lax.rem(t, per_block) == 0) & (t < blocks * per_block))
         def _():
             rows = block_rows(t // per_block)
-            own[rows] = dot(d_gate[rows], w_gate[...], NT) + dot(d_up[rows], w_up[...], NT)
-
-        @pl.when(t == 0)
+            own[rows] = dot(d_gate[rows], w_gate[...], NT)
+
+            @pl.when(t == 0)
+            def _():
+                for load in loads[3:6]:
+                    load.wait()
+
+            own[rows] += dot(d_up[rows], w_up[...], NT)
+
+        @pl.when(t == 1)
         def _():
             for load in loads[6:]:
                 load.wait()
@@ -1505,9 +1513,9 @@
         pair,
     )
     width = gain_attn.shape[0]
-    pair = lax.psum_scatter(pair, "head", scatter_dimension=0, tiled=True).astype(F32)
-    output = (hidden_res + pair[:, :width]).astype(BF16)
-    d_normed_attn = pair[:, width:]
+    pair = lax.psum_scatter(pair, "head", scatter_dimension=0, tiled=True)
+    output = (hidden_res + pair[:, :width].astype(F32)).astype(BF16)
+    d_normed_attn = pair[:, width:].astype(F32)
     grad_in_attn = norm_backward(token_vals, inverse_rms(token_vals), gain_attn, d_normed_attn)
     grad_tokens = (d_hidden + grad_in_attn).astype(BF16)
     gate_part = mix_sig * (1.0 - mix_sig) * jnp.sum(gate_cols[:, 0], axis=-1)

time: 700 us -> 694 us (level)
  transfers between devices with their start and end apart: 3 -> 3, of which waited for: 0 -> 1; matrix products, arithmetic and copies ran while one was open for 1% -> 1% of each run, Pallas kernels for 80% -> 80%
where the time goes in v5:
time: 694 us; the launch traced here: 686 us
  Pallas kernels  650 us (94%)
  between operations  14.9 us (2%)
  local copies, waits for them, and re-layouts  11.6 us (2%)
  other arithmetic  9.25 us (1%)
    pallas_call x1, Pallas kernels, attn_out_sum(): pl.pallas_call(attn_out_kernel, in_specs=[vmem] * 4 + [any_] * 3, out_spe...  163 us
    pallas_call x1, Pallas kernels, mlp_back_sum(): pl.pallas_call(functools.partial(mlp_back_kernel, tile, seg_bits), in_spe...  142 us
    pallas_call x1, Pallas kernels, grad_sum(): pl.pallas_call(functools.partial(grad_sum_kernel, count, tile, seg_bits,...  114 us
    pallas_call x1, Pallas kernels, gather_project(): pl.pallas_call(gather_kernel, in_specs=[any_, vmem] + [any_] * 3, out_spe...  75.4 us
    pallas_call x2, Pallas kernels, mlp_half(): pl.pallas_call(mlp_kernel, grid=(units // block,), in_specs=[pl.BlockSpec...  53.5 us
    pallas_call x1, Pallas kernels, widen(): pl.pallas_call(functools.partial(widen_kernel, shapes, places, len(target...  34.3 us
    pallas_call x1, Pallas kernels, attn_back(): pl.pallas_call(attn_back_kernel, in_specs=[scalar] * 2 + [vmem] * 7, out_...  29.1 us
    pallas_call x1, Pallas kernels, attn_weights(): pl.pallas_call(attn_weights_kernel, grid=(width // block,), in_specs=[sid...  19.5 us
  transfers between devices with their start and end apart: 3, of which 1 were waited for; matrix products, arithmetic and copies ran while one was open for 1% of the time, Pallas kernels for 80%

profile of v5, /device:TPU:0, one launch (start us, length us, event | category | flops | bytes accessed | tf_op | source)
XLA Modules:
  0.0 686.1 jit_solution(6960232989062808569)
XLA Ops:
  7.2 0.0 all-gather.2.cloned.1.call-start
  7.2 0.0 copy-start
  7.2 1.2 copy-done
  8.5 0.0 copy-start.2
  8.5 0.7 copy-done.2
  9.2 0.0 copy-start.14
  9.2 0.0 copy-start.15
  9.2 75.4 %shard_map.236 = (bf16[1024,2048]{1,0:T(8,128)(2,1)}, bf16[1024,2048]{1,0:T(8,128)(2,1)}, bf16[1024,512]{1,0:T(8,128)(2,1)S(1)}, bf16[1024,512]{1,0:T(8,128)(2,1)S(1)}, bf16[1024,512]{1,0:T(8,128)(2,1)S(1)}) custom-call(bf16[256,2048]{1,0:T(8,128)(2,1)S(1)} %copy-done, f32[1,2048]{1,0:T(1,128)S(1)} %bitcast.13, bf16[2048,512]{1,0:T(8,128)(2,1)} %w_query_ref.1, ...), custom_call_target="tpu_custom_call" | custom-call | flops 6442450944 | bytes 157286400 | tf_op jit(solution)/shard_map/pallas_call | solution.py:579
  84.5 0.0 copy-start.7
  84.6 1.0 copy-done.7
  85.5 0.0 copy-start.5
  85.5 0.0 all-gather.2.cloned.1.call-update
  85.5 0.0 all-reduce.4.cloned.1.call-start
  85.6 0.0 copy-done.14
  85.6 0.7 fusion.11
  87.0 0.0 copy-done.15
  87.1 0.0 copy-start.8
  87.1 1.2 copy-done.8
  88.3 19.0 %shard_map.237 = (bf16[1024,512]{1,0:T(8,128)(2,1)S(1)}, f32[1024,512]{1,0:T(8,128)S(1)}, f32[4,144,128]{2,1,0:T(8,128)S(1)}, f32[4,144,128]{2,1,0:T(8,128)S(1)}) custom-call(f32[4]{0:T(128)S(1)} %add_divide_fusion.gate_ref, s32[1]{0:T(128)} %bitcast.valid_ref, bf16[1024,512]{1,0:T(8,128)(2,1)S(1)} %get-tuple-element.69.query_ref, ...), custom_call_target="tpu_custom_call" | custom-call | flops 2147483648 | bytes 62914560 | tf_op jit(solution)/shard_map/pallas_call | solution.py:1282
  107.3 0.0 copy-done.5
  107.3 0.0 copy-start.4
  107.3 1.4 copy-done.4
  108.7 0.0 copy-start.9
  108.7 1.0 copy-done.9
  109.7 163.1 %shard_map.238 = (f32[1024,2048]{1,0:T(8,128)}, bf16[2048,1024]{1,0:T(8,128)(2,1)}, f32[1024,2048]{1,0:T(8,128)}, f32[1024,2048]{1,0:T(8,128)}, bf16[1024,2048]{1,0:T(8,128)(2,1)}, /*index=5*/bf16[1024,4096]{1,0:T(8,128)(2,1)}) custom-call(bf16[1024,512]{1,0:T(8,128)(2,1)} %copy-done.9, bf16[512,2048]{1,0:T(8,128)(2,1)} %weight_ref.3, ...), custom_call_target="tpu_custom_call" | custom-call | flops 27917287424 | bytes 262144000 | tf_op jit(solution)/shard_map/pallas_call | solution.py:748
  272.8 0.0 all-gather.2.cloned.1.call-done.grad_ref.grad_hbm
  272.8 27.1 %shard_map.239 = (bf16[1024,1024]{1,0:T(8,128)(2,1)}, bf16[1024,1024]{1,0:T(8,128)(2,1)}, bf16[2048,1024]{1,0:T(8,128)(2,1)}, bf16[2048,1024]{1,0:T(8,128)(2,1)}, bf16[1024,2048]{1,0:T(8,128)(2,1)}) custom-call(bf16[2048,1024]{1,0:T(8,128)(2,1)} %get-tuple-element.77.flip_ref, bf16[1024,2048]{1,0:T(8,128)(2,1)} %all-gather.2.cloned.1.call-done.grad_ref.grad_hbm, ...), custom_call_target="tpu_custom_call" | custom-call | flops 17179869184 | bytes 39845888 | tf_op jit(solution)/shard_map/pallas_call | solution.py:941
  300.0 0.0 all-reduce.4.cloned.1.call-update
  300.0 0.2 reduce-scatter.2.cloned.1.call-start
  300.2 26.3 %shard_map.240 = (bf16[1024,1024]{1,0:T(8,128)(2,1)}, bf16[1024,1024]{1,0:T(8,128)(2,1)}, bf16[2048,1024]{1,0:T(8,128)(2,1)}, bf16[2048,1024]{1,0:T(8,128)(2,1)}, bf16[1024,2048]{1,0:T(8,128)(2,1)}) custom-call(bf16[2048,1024]{1,0:T(8,128)(2,1)} %get-tuple-element.77.flip_ref, bf16[1024,2048]{1,0:T(8,128)(2,1)} %all-gather.2.cloned.1.call-done.grad_ref.grad_hbm, ...), custom_call_target="tpu_custom_call" | custom-call | flops 17179869184 | bytes 39845888 | tf_op jit(solution)/shard_map/pallas_call | solution.py:941
  326.6 141.7 %shard_map.241 = (bf16[1024,2048]{1,0:T(8,128)(2,1)}, f32[256,2048]{1,0:T(8,128)}, f32[8,2048]{1,0:T(8,128)}, bf16[1024,2048]{1,0:T(8,128)(2,1)}, bf16[2048,1024]{1,0:T(8,128)(2,1)}) custom-call(bf16[1024,1024]{1,0:T(8,128)(2,1)} %get-tuple-element.82.d_gate_a, bf16[1024,1024]{1,0:T(8,128)(2,1)} %get-tuple-element.83.d_gate_b, ...), custom_call_target="tpu_custom_call" | custom-call | flops 17179869184 | bytes 262144000 | tf_op jit(solution)/shard_map/pallas_call | solution.py:881
  468.3 0.0 copy-start.6
  468.3 1.3 copy-done.6
  469.5 0.0 copy-start.10
  469.5 29.1 %shard_map.242 = (bf16[1024,512]{1,0:T(8,128)(2,1)S(1)}, bf16[1024,512]{1,0:T(8,128)(2,1)S(1)}, bf16[1024,512]{1,0:T(8,128)(2,1)S(1)}, f32[4,8,128]{2,1,0:T(8,128)S(1)}) custom-call(f32[4]{0:T(128)S(1)} %add_divide_fusion.gate_ref, s32[1]{0:T(128)} %bitcast.valid_ref, bf16[1024,2048]{1,0:T(8,128)(2,1)} %get-tuple-element.88.d_out_ref, ...), custom_call_target="tpu_custom_call" | custom-call | flops 7516192768 | bytes 104857600 | tf_op jit(solution)/shard_map/pallas_call | solution.py:1399
  498.6 0.0 copy-done.10
  498.6 19.5 %shard_map.243 = (bf16[1024,4096]{1,0:T(8,128)(2,1)}, bf16[2048,512]{1,0:T(8,128)(2,1)}, bf16[2048,512]{1,0:T(8,128)(2,1)}, bf16[2048,512]{1,0:T(8,128)(2,1)}, b...) custom-call(bf16[1024,2048]{1,0:T(8,128)(2,1)} %get-tuple-element.76.rows_ref, ...), custom_call_target="tpu_custom_call", output_to_operand_aliasing={{0}: (9, {})} | custom-call | flops 15032385536 | bytes 31457280 | tf_op jit(solution)/shard_map/pallas_call | solution.py:1096
  518.1 0.0 copy-start.1
  518.1 0.0 reduce-scatter.2.cloned.1.call-update
  518.2 0.0 copy-start.13
  518.2 0.0 copy-start.3
  518.2 1.1 copy-done.1
  519.4 0.3 fusion.7
  519.7 0.6 slice_multiply_fusion.1
  520.2 0.7 fusion.8
  521.0 0.1 slice_reduce_fusion
  521.1 0.1 broadcast_select_fusion
  521.2 0.1 select_n.39
  521.3 0.0 copy-done.13
  521.3 0.0 copy-done.3
  521.3 0.6 fusion.9.refs_0_
  522.0 114.3 %shard_map.244 = (f32[40,128]{1,0:T(8,128)}, bf16[2048,1024]{1,0:T(8,128)(2,1)}, bf16[512,2048]{1,0:T(8,128)(2,1)}, bf16[2048,512]{1,0:T(8,128)(2,1)}, bf16[2048...) custom-call(f32[40,128]{1,0:T(8,128)} %fusion.9.refs_0_, bf16[2048,1024]{1,0:T(8,128)(2,1)} %get-tuple-element.101.refs_1_, ...), custom_call_target="tpu_custom_call" | custom-call | bytes 377487360 | tf_op jit(solution)/shard_map/pallas_call | solution.py:265
  636.2 1.3 dynamic_slice.7
  637.5 1.3 slice_bitcast_fusion
  638.8 0.0 all-reduce.4.cloned.1.call-done
  638.8 0.0 copy-start.12
  638.8 34.3 %shard_map.245 = (f32[2048,2048]{1,0:T(8,128)}, f32[2048,2048]{1,0:T(8,128)}, f32[2048,2048]{1,0:T(8,128)}, f32[512,2048]{1,0:T(8,128)}, f32[2048,512]{1,0:T(8,1...) custom-call(bf16[2048,1024]{1,0:T(8,128)(2,1)} %get-tuple-element.124.refs_0_, ...), custom_call_target="tpu_custom_call" | custom-call | bytes 100663296 | tf_op jit(solution)/shard_map/pallas_call | solution.py:1042
  673.1 0.2 reduce-scatter.2.cloned.1.call-done
  673.3 0.0 copy-start.11
  673.3 1.9 fusion.2
  675.2 0.0 copy-done.12
  675.2 0.0 copy-done.11
  675.2 4.1 fusion.6
  (9 shorter events, 0.1 us)
Async XLA Ops:
  7.2 265.7 %all-gather.2.cloned.1.call-start = ((), (), s32[]{:S(2)}) async-start(), calls=%async_computation.1 | async-start | bytes 5242880 | tf_op jit(solution)/shard_map/all_gather | solution.py:1457
  7.2 1.2 copy-start
  8.5 0.7 copy-start.2
  9.2 76.5 %copy-start.14 = (s32[2]{0:T(128)S(1)}, s32[2]{0:T(128)}, u32[]{:S(2)}) copy-start(s32[2]{0:T(128)} %param.25) | copy-start | bytes 28
  9.2 77.9 %copy-start.15 = (f32[4]{0:T(128)S(1)}, f32[4]{0:T(128)}, u32[]{:S(2)}) copy-start(f32[4]{0:T(128)} %param.24) | copy-start | bytes 52
  84.5 1.0 copy-start.7
  85.5 21.8 %copy-start.5 = (bf16[1024,512]{1,0:T(8,128)(2,1)}, bf16[1024,512]{1,0:T(8,128)(2,1)S(1)}, u32[]{:S(2)}) copy-start(bf16[1024,512]{1,0:T(8,128)(2,1)S(1)} %get-tuple-element.71.key_ref) | copy-start | bytes 3145732
  85.5 553.3 %all-reduce.4.cloned.1.call-start = ((), (), s32[]{:S(2)}) async-start(), calls=%async_computation.3 | async-start | bytes 25165824 | tf_op jit(solution)/shard_map/psum | solution.py:1473
  87.1 1.2 copy-start.8
  107.3 1.4 copy-start.4
  108.7 1.0 copy-start.9
  300.0 373.3 %reduce-scatter.2.cloned.1.call-start = ((), (), s32[]{:S(2)}) async-start(), calls=%async_computation.2 | async-start | bytes 10485760 | tf_op jit(solution)/shard_map/reduce_scatter | solution.py:1516
  468.3 1.3 copy-start.6
  469.5 29.1 %copy-start.10 = (bf16[1024,512]{1,0:T(8,128)(2,1)S(1)}, bf16[1024,512]{1,0:T(8,128)(2,1)}, u32[]{:S(2)}) copy-start(bf16[1024,512]{1,0:T(8,128)(2,1)} %copy-done.9) | copy-start | bytes 3145732
  518.1 1.2 copy-start.1
  518.2 3.1 copy-start.13
  518.2 3.2 copy-start.3
  638.8 36.4 %copy-start.12 = (f32[256,2048]{1,0:T(8,128)S(1)}, f32[256,2048]{1,0:T(8,128)}, u32[]{:S(2)}) copy-start(f32[256,2048]{1,0:T(8,128)} %get-tuple-element.96) | copy-start | bytes 6291460
  673.3 1.9 copy-start.11
Sparse Core Ops, SparseCore 0:
  85.7 118.2 all-gather.1
  300.1 225.3 all-reduce.3
  528.0 145.2 reduce-scatter.1

commit v6 on v5

--- a/solution.py
+++ b/solution.py
@@ -284,11 +284,11 @@
 
 ROWS = 32
 FIRST_HOP = 2
-SECOND_HOP = 3
-SEND_SLOTS = 4
+SECOND_HOP = 4
+SEND_SLOTS = 6
 BLOCK_ROWS = 256
 FORWARD_ROWS = 128
-UNIT_GROUP = 512
+UNIT_GROUP = 1024
 LINE_REFS = 8
 
 

time: 694 us -> 694 us (level)
  transfers between devices with their start and end apart: 3 -> 3, of which waited for: 1 -> 1; matrix products, arithmetic and copies ran while one was open for 1% -> 1% of each run, Pallas kernels for 80% -> 79%
where the time goes in v6:
time: 694 us; the launch traced here: 687 us
  Pallas kernels  649 us (94%)
  between operations  15.2 us (2%)
  local copies, waits for them, and re-layouts  11.6 us (2%)
  other arithmetic  9.26 us (1%)
    pallas_call x1, Pallas kernels, attn_out_sum(): pl.pallas_call(attn_out_kernel, in_specs=[vmem] * 4 + [any_] * 3, out_spe...  161 us
    pallas_call x1, Pallas kernels, mlp_back_sum(): pl.pallas_call(functools.partial(mlp_back_kernel, tile, seg_bits), in_spe...  142 us
    pallas_call x1, Pallas kernels, grad_sum(): pl.pallas_call(functools.partial(grad_sum_kernel, count, tile, seg_bits,...  115 us
    pallas_call x1, Pallas kernels, gather_project(): pl.pallas_call(gather_kernel, in_specs=[any_, vmem] + [any_] * 3, out_spe...  75.4 us
    pallas_call x2, Pallas kernels, mlp_half(): pl.pallas_call(mlp_kernel, grid=(units // block,), in_specs=[pl.BlockSpec...  52.8 us
    pallas_call x1, Pallas kernels, widen(): pl.pallas_call(functools.partial(widen_kernel, shapes, places, len(target...  34.4 us
    pallas_call x1, Pallas kernels, attn_back(): pl.pallas_call(attn_back_kernel, in_specs=[scalar] * 2 + [vmem] * 7, out_...  29.5 us
    pallas_call x1, Pallas kernels, attn_weights(): pl.pallas_call(attn_weights_kernel, grid=(width // block,), in_specs=[sid...  19.6 us
  transfers between devices with their start and end apart: 3, of which 1 were waited for; matrix products, arithmetic and copies ran while one was open for 1% of the time, Pallas kernels for 79%

profile of v6, /device:TPU:0, one launch (start us, length us, event | category | flops | bytes accessed | tf_op | source)
XLA Modules:
  0.0 687.2 jit_solution(14142560502126842365)
XLA Ops:
  7.2 0.0 all-gather.2.cloned.1.call-start
  7.2 0.0 copy-start
  7.2 1.2 copy-done
  8.5 0.0 copy-start.2
  8.5 0.7 copy-done.2
  9.2 0.0 copy-start.14
  9.2 0.0 copy-start.15
  9.2 75.4 %shard_map.236 = (bf16[1024,2048]{1,0:T(8,128)(2,1)}, bf16[1024,2048]{1,0:T(8,128)(2,1)}, bf16[1024,512]{1,0:T(8,128)(2,1)S(1)}, bf16[1024,512]{1,0:T(8,128)(2,1)S(1)}, bf16[1024,512]{1,0:T(8,128)(2,1)S(1)}) custom-call(bf16[256,2048]{1,0:T(8,128)(2,1)S(1)} %copy-done, f32[1,2048]{1,0:T(1,128)S(1)} %bitcast.13, bf16[2048,512]{1,0:T(8,128)(2,1)} %w_query_ref.1, ...), custom_call_target="tpu_custom_call" | custom-call | flops 6442450944 | bytes 157286400 | tf_op jit(solution)/shard_map/pallas_call | solution.py:579
  84.5 0.0 copy-start.7
  84.6 1.0 copy-done.7
  85.5 0.0 copy-start.5
  85.5 0.0 all-gather.2.cloned.1.call-update
  85.5 0.0 all-reduce.4.cloned.1.call-start
  85.6 0.0 copy-done.14
  85.6 0.7 fusion.11
  87.0 0.0 copy-done.15
  87.1 0.0 copy-start.8
  87.1 1.2 copy-done.8
  88.3 19.0 %shard_map.237 = (bf16[1024,512]{1,0:T(8,128)(2,1)S(1)}, f32[1024,512]{1,0:T(8,128)S(1)}, f32[4,144,128]{2,1,0:T(8,128)S(1)}, f32[4,144,128]{2,1,0:T(8,128)S(1)}) custom-call(f32[4]{0:T(128)S(1)} %add_divide_fusion.gate_ref, s32[1]{0:T(128)} %bitcast.valid_ref, bf16[1024,512]{1,0:T(8,128)(2,1)S(1)} %get-tuple-element.69.query_ref, ...), custom_call_target="tpu_custom_call" | custom-call | flops 2147483648 | bytes 62914560 | tf_op jit(solution)/shard_map/pallas_call | solution.py:1282
  107.3 0.0 copy-done.5
  107.3 0.0 copy-start.4
  107.3 1.4 copy-done.4
  108.7 0.0 copy-start.9
  108.7 1.0 copy-done.9
  109.7 161.3 %shard_map.238 = (f32[1024,2048]{1,0:T(8,128)}, bf16[2048,1024]{1,0:T(8,128)(2,1)}, f32[1024,2048]{1,0:T(8,128)}, f32[1024,2048]{1,0:T(8,128)}, bf16[1024,2048]{1,0:T(8,128)(2,1)}, /*index=5*/bf16[1024,4096]{1,0:T(8,128)(2,1)}) custom-call(bf16[1024,512]{1,0:T(8,128)(2,1)} %copy-done.9, bf16[512,2048]{1,0:T(8,128)(2,1)} %weight_ref.3, ...), custom_call_target="tpu_custom_call" | custom-call | flops 27917287424 | bytes 262144000 | tf_op jit(solution)/shard_map/pallas_call | solution.py:748
  271.0 0.0 all-gather.2.cloned.1.call-done.grad_ref.grad_hbm
  271.0 27.1 %shard_map.239 = (bf16[1024,1024]{1,0:T(8,128)(2,1)}, bf16[1024,1024]{1,0:T(8,128)(2,1)}, bf16[2048,1024]{1,0:T(8,128)(2,1)}, bf16[2048,1024]{1,0:T(8,128)(2,1)}, bf16[1024,2048]{1,0:T(8,128)(2,1)}) custom-call(bf16[2048,1024]{1,0:T(8,128)(2,1)} %get-tuple-element.77.flip_ref, bf16[1024,2048]{1,0:T(8,128)(2,1)} %all-gather.2.cloned.1.call-done.grad_ref.grad_hbm, ...), custom_call_target="tpu_custom_call" | custom-call | flops 17179869184 | bytes 39845888 | tf_op jit(solution)/shard_map/pallas_call | solution.py:941
  298.1 0.0 all-reduce.4.cloned.1.call-update
  298.2 0.3 reduce-scatter.2.cloned.1.call-start
  298.4 25.6 %shard_map.240 = (bf16[1024,1024]{1,0:T(8,128)(2,1)}, bf16[1024,1024]{1,0:T(8,128)(2,1)}, bf16[2048,1024]{1,0:T(8,128)(2,1)}, bf16[2048,1024]{1,0:T(8,128)(2,1)}, bf16[1024,2048]{1,0:T(8,128)(2,1)}) custom-call(bf16[2048,1024]{1,0:T(8,128)(2,1)} %get-tuple-element.77.flip_ref, bf16[1024,2048]{1,0:T(8,128)(2,1)} %all-gather.2.cloned.1.call-done.grad_ref.grad_hbm, ...), custom_call_target="tpu_custom_call" | custom-call | flops 17179869184 | bytes 39845888 | tf_op jit(solution)/shard_map/pallas_call | solution.py:941
  324.1 141.9 %shard_map.241 = (bf16[1024,2048]{1,0:T(8,128)(2,1)}, f32[256,2048]{1,0:T(8,128)}, f32[8,2048]{1,0:T(8,128)}, bf16[1024,2048]{1,0:T(8,128)(2,1)}, bf16[2048,1024]{1,0:T(8,128)(2,1)}) custom-call(bf16[1024,1024]{1,0:T(8,128)(2,1)} %get-tuple-element.82.d_gate_a, bf16[1024,1024]{1,0:T(8,128)(2,1)} %get-tuple-element.83.d_gate_b, ...), custom_call_target="tpu_custom_call" | custom-call | flops 17179869184 | bytes 262144000 | tf_op jit(solution)/shard_map/pallas_call | solution.py:881
  466.0 0.0 copy-start.6
  466.0 1.4 copy-done.6
  467.4 0.0 copy-start.10
  467.4 29.5 %shard_map.242 = (bf16[1024,512]{1,0:T(8,128)(2,1)S(1)}, bf16[1024,512]{1,0:T(8,128)(2,1)S(1)}, bf16[1024,512]{1,0:T(8,128)(2,1)S(1)}, f32[4,8,128]{2,1,0:T(8,128)S(1)}) custom-call(f32[4]{0:T(128)S(1)} %add_divide_fusion.gate_ref, s32[1]{0:T(128)} %bitcast.valid_ref, bf16[1024,2048]{1,0:T(8,128)(2,1)} %get-tuple-element.88.d_out_ref, ...), custom_call_target="tpu_custom_call" | custom-call | flops 7516192768 | bytes 104857600 | tf_op jit(solution)/shard_map/pallas_call | solution.py:1399
  496.9 0.0 copy-done.10
  496.9 19.6 %shard_map.243 = (bf16[1024,4096]{1,0:T(8,128)(2,1)}, bf16[2048,512]{1,0:T(8,128)(2,1)}, bf16[2048,512]{1,0:T(8,128)(2,1)}, bf16[2048,512]{1,0:T(8,128)(2,1)}, b...) custom-call(bf16[1024,2048]{1,0:T(8,128)(2,1)} %get-tuple-element.76.rows_ref, ...), custom_call_target="tpu_custom_call", output_to_operand_aliasing={{0}: (9, {})} | custom-call | flops 15032385536 | bytes 31457280 | tf_op jit(solution)/shard_map/pallas_call | solution.py:1096
  516.5 0.0 copy-start.1
  516.5 0.0 reduce-scatter.2.cloned.1.call-update
  516.5 0.0 copy-start.13
  516.5 0.0 copy-start.3
  516.6 1.1 copy-done.1
  517.7 0.3 fusion.7
  518.0 0.6 slice_multiply_fusion.1
  518.6 0.7 fusion.8
  519.3 0.1 slice_reduce_fusion
  519.5 0.1 broadcast_select_fusion
  519.5 0.1 select_n.39
  519.6 0.0 copy-done.13
  519.7 0.0 copy-done.3
  519.7 0.6 fusion.9.refs_0_
  520.3 114.8 %shard_map.244 = (f32[40,128]{1,0:T(8,128)}, bf16[2048,1024]{1,0:T(8,128)(2,1)}, bf16[512,2048]{1,0:T(8,128)(2,1)}, bf16[2048,512]{1,0:T(8,128)(2,1)}, bf16[2048...) custom-call(f32[40,128]{1,0:T(8,128)} %fusion.9.refs_0_, bf16[2048,1024]{1,0:T(8,128)(2,1)} %get-tuple-element.101.refs_1_, ...), custom_call_target="tpu_custom_call" | custom-call | bytes 377487360 | tf_op jit(solution)/shard_map/pallas_call | solution.py:265
  635.1 1.3 dynamic_slice.7
  636.4 1.3 slice_bitcast_fusion
  637.7 0.0 all-reduce.4.cloned.1.call-done
  637.7 0.0 copy-start.12
  637.7 34.4 %shard_map.245 = (f32[2048,2048]{1,0:T(8,128)}, f32[2048,2048]{1,0:T(8,128)}, f32[2048,2048]{1,0:T(8,128)}, f32[512,2048]{1,0:T(8,128)}, f32[2048,512]{1,0:T(8,1...) custom-call(bf16[2048,1024]{1,0:T(8,128)(2,1)} %get-tuple-element.124.refs_0_, ...), custom_call_target="tpu_custom_call" | custom-call | bytes 100663296 | tf_op jit(solution)/shard_map/pallas_call | solution.py:1042
  672.1 2.0 reduce-scatter.2.cloned.1.call-done
  674.1 0.0 copy-start.11
  674.1 1.9 fusion.2
  676.1 0.0 copy-done.12
  676.1 0.0 copy-done.11
  676.1 4.1 fusion.6
  (9 shorter events, 0.1 us)
Async XLA Ops:
  7.2 263.8 %all-gather.2.cloned.1.call-start = ((), (), s32[]{:S(2)}) async-start(), calls=%async_computation.1 | async-start | bytes 5242880 | tf_op jit(solution)/shard_map/all_gather | solution.py:1457
  7.2 1.2 copy-start
  8.5 0.7 copy-start.2
  9.2 76.5 %copy-start.14 = (s32[2]{0:T(128)S(1)}, s32[2]{0:T(128)}, u32[]{:S(2)}) copy-start(s32[2]{0:T(128)} %param.25) | copy-start | bytes 28
  9.2 77.9 %copy-start.15 = (f32[4]{0:T(128)S(1)}, f32[4]{0:T(128)}, u32[]{:S(2)}) copy-start(f32[4]{0:T(128)} %param.24) | copy-start | bytes 52
  84.5 1.0 copy-start.7
  85.5 21.8 %copy-start.5 = (bf16[1024,512]{1,0:T(8,128)(2,1)}, bf16[1024,512]{1,0:T(8,128)(2,1)S(1)}, u32[]{:S(2)}) copy-start(bf16[1024,512]{1,0:T(8,128)(2,1)S(1)} %get-tuple-element.71.key_ref) | copy-start | bytes 3145732
  85.5 552.2 %all-reduce.4.cloned.1.call-start = ((), (), s32[]{:S(2)}) async-start(), calls=%async_computation.3 | async-start | bytes 25165824 | tf_op jit(solution)/shard_map/psum | solution.py:1473
  87.1 1.2 copy-start.8
  107.3 1.4 copy-start.4
  108.7 1.0 copy-start.9
  298.2 376.0 %reduce-scatter.2.cloned.1.call-start = ((), (), s32[]{:S(2)}) async-start(), calls=%async_computation.2 | async-start | bytes 10485760 | tf_op jit(solution)/shard_map/reduce_scatter | solution.py:1516
  466.0 1.4 copy-start.6
  467.4 29.5 %copy-start.10 = (bf16[1024,512]{1,0:T(8,128)(2,1)S(1)}, bf16[1024,512]{1,0:T(8,128)(2,1)}, u32[]{:S(2)}) copy-start(bf16[1024,512]{1,0:T(8,128)(2,1)} %copy-done.9) | copy-start | bytes 3145732
  516.5 1.2 copy-start.1
  516.5 3.1 copy-start.13
  516.5 3.2 copy-start.3
  637.7 38.3 %copy-start.12 = (f32[256,2048]{1,0:T(8,128)S(1)}, f32[256,2048]{1,0:T(8,128)}, u32[]{:S(2)}) copy-start(f32[256,2048]{1,0:T(8,128)} %get-tuple-element.96) | copy-start | bytes 6291460
  674.1 1.9 copy-start.11
Sparse Core Ops, SparseCore 0:
  85.7 118.4 all-gather.1
  298.3 227.8 all-reduce.3
  528.7 145.4 reduce-scatter.1

commit v7 on v6

--- a/solution.py
+++ b/solution.py
@@ -674,8 +674,9 @@
         up_proj = dot(rows, w_up[:, cols], NN)
         gate_sig = jax.nn.sigmoid(gate_pre)
         silu_gate = gate_pre * gate_sig
-        silu[slot] = silu_gate
-        slope[slot] = up_proj * gate_sig * (1.0 + gate_pre * (1.0 - gate_sig))
+        silu[slot] = silu_gate.astype(BF16)
+        factor = up_proj * gate_sig * (1.0 + gate_pre * (1.0 - gate_sig))
+        slope[slot] = factor.astype(BF16)
         act[slot] = (silu_gate * up_proj).astype(BF16)
         for copy in unit_copies(u):
             copy.start()
@@ -752,8 +753,8 @@
         out_shape=[
             jax.ShapeDtypeStruct((rows, width), F32),
             jax.ShapeDtypeStruct((width, rows), BF16),
-            jax.ShapeDtypeStruct((rows, units), F32),
-            jax.ShapeDtypeStruct((rows, units), F32),
+            jax.ShapeDtypeStruct((rows, units), BF16),
+            jax.ShapeDtypeStruct((rows, units), BF16),
             jax.ShapeDtypeStruct((rows, units), BF16),
             jax.ShapeDtypeStruct((rows, 2 * width), BF16),
         ],
@@ -763,8 +764,8 @@
             pltpu.VMEM((width, units), BF16),
             pltpu.VMEM((width, units), BF16),
             pltpu.VMEM((units, width), BF16),
-            pltpu.VMEM((slots, FORWARD_ROWS, UNIT_GROUP), F32),
-            pltpu.VMEM((slots, FORWARD_ROWS, UNIT_GROUP), F32),
+            pltpu.VMEM((slots, FORWARD_ROWS, UNIT_GROUP), BF16),
+            pltpu.VMEM((slots, FORWARD_ROWS, UNIT_GROUP), BF16),
             pltpu.VMEM((slots, FORWARD_ROWS, UNIT_GROUP), BF16),
             pltpu.VMEM((width, FORWARD_ROWS), BF16),
             pltpu.VMEM((FORWARD_ROWS, width), F32),
@@ -919,8 +920,8 @@
 ):
     width = flip_ref.shape[0]
     d_act = dot(grad_ref[...], w_down_ref[...], NT)
-    d_gate_ref[...] = (d_act * slope_ref[...]).astype(BF16)
-    d_up_ref[...] = (d_act * silu_ref[...]).astype(BF16)
+    d_gate_ref[...] = (d_act * slope_ref[...].astype(F32)).astype(BF16)
+    d_up_ref[...] = (d_act * silu_ref[...].astype(F32)).astype(BF16)
     half = width // 2
     for i in range(2):
         part = slice(i * half, (i + 1) * half)

time: 694 us -> 693 us (level)
  transfers between devices with their start and end apart: 3 -> 3, of which waited for: 1 -> 1; matrix products, arithmetic and copies ran while one was open for 1% -> 1% of each run, Pallas kernels for 79% -> 80%
where the time goes in v7:
time: 693 us; the launch traced here: 686 us
  Pallas kernels  646 us (93%)
  between operations  15.1 us (2%)
  local copies, waits for them, and re-layouts  11.7 us (2%)
  other arithmetic  9.26 us (1%)
    pallas_call x1, Pallas kernels, attn_out_sum(): pl.pallas_call(attn_out_kernel, in_specs=[vmem] * 4 + [any_] * 3, out_spe...  161 us
    pallas_call x1, Pallas kernels, mlp_back_sum(): pl.pallas_call(functools.partial(mlp_back_kernel, tile, seg_bits), in_spe...  143 us
    pallas_call x1, Pallas kernels, grad_sum(): pl.pallas_call(functools.partial(grad_sum_kernel, count, tile, seg_bits,...  114 us
    pallas_call x1, Pallas kernels, gather_project(): pl.pallas_call(gather_kernel, in_specs=[any_, vmem] + [any_] * 3, out_spe...  75.4 us
    pallas_call x2, Pallas kernels, mlp_half(): pl.pallas_call(mlp_kernel, grid=(units // block,), in_specs=[pl.BlockSpec...  49.8 us
    pallas_call x1, Pallas kernels, widen(): pl.pallas_call(functools.partial(widen_kernel, shapes, places, len(target...  34.3 us
    pallas_call x1, Pallas kernels, attn_back(): pl.pallas_call(attn_back_kernel, in_specs=[scalar] * 2 + [vmem] * 7, out_...  29.5 us
    pallas_call x1, Pallas kernels, attn_weights(): pl.pallas_call(attn_weights_kernel, grid=(width // block,), in_specs=[sid...  19.7 us
  transfers between devices with their start and end apart: 3, of which 1 were waited for; matrix products, arithmetic and copies ran while one was open for 1% of the time, Pallas kernels for 80%

profile of v7, /device:TPU:0, one launch (start us, length us, event | category | flops | bytes accessed | tf_op | source)
XLA Modules:
  0.0 686.1 jit_solution(11955532383971481037)
XLA Ops:
  7.2 0.0 all-gather.2.cloned.1.call-start
  7.2 0.0 copy-start
  7.2 1.2 copy-done
  8.5 0.0 copy-start.2
  8.5 0.7 copy-done.2
  9.2 0.0 copy-start.14
  9.2 0.0 copy-start.15
  9.2 75.4 %shard_map.236 = (bf16[1024,2048]{1,0:T(8,128)(2,1)}, bf16[1024,2048]{1,0:T(8,128)(2,1)}, bf16[1024,512]{1,0:T(8,128)(2,1)S(1)}, bf16[1024,512]{1,0:T(8,128)(2,1)S(1)}, bf16[1024,512]{1,0:T(8,128)(2,1)S(1)}) custom-call(bf16[256,2048]{1,0:T(8,128)(2,1)S(1)} %copy-done, f32[1,2048]{1,0:T(1,128)S(1)} %bitcast.13, bf16[2048,512]{1,0:T(8,128)(2,1)} %w_query_ref.1, ...), custom_call_target="tpu_custom_call" | custom-call | flops 6442450944 | bytes 157286400 | tf_op jit(solution)/shard_map/pallas_call | solution.py:579
  84.5 0.0 copy-start.7
  84.6 1.0 copy-done.7
  85.5 0.0 copy-start.5
  85.5 0.0 all-gather.2.cloned.1.call-update
  85.5 0.0 all-reduce.4.cloned.1.call-start
  85.6 0.0 copy-done.14
  85.6 0.7 fusion.11
  87.0 0.0 copy-done.15
  87.1 0.0 copy-start.8
  87.1 1.2 copy-done.8
  88.3 19.0 %shard_map.237 = (bf16[1024,512]{1,0:T(8,128)(2,1)S(1)}, f32[1024,512]{1,0:T(8,128)S(1)}, f32[4,144,128]{2,1,0:T(8,128)S(1)}, f32[4,144,128]{2,1,0:T(8,128)S(1)}) custom-call(f32[4]{0:T(128)S(1)} %add_divide_fusion.gate_ref, s32[1]{0:T(128)} %bitcast.valid_ref, bf16[1024,512]{1,0:T(8,128)(2,1)S(1)} %get-tuple-element.69.query_ref, ...), custom_call_target="tpu_custom_call" | custom-call | flops 2147483648 | bytes 62914560 | tf_op jit(solution)/shard_map/pallas_call | solution.py:1283
  107.3 0.0 copy-done.5
  107.3 0.0 copy-start.4
  107.3 1.3 copy-done.4
  108.6 0.0 copy-start.9
  108.7 1.0 copy-done.9
  109.6 161.3 %shard_map.238 = (f32[1024,2048]{1,0:T(8,128)}, bf16[2048,1024]{1,0:T(8,128)(2,1)}, bf16[1024,2048]{1,0:T(8,128)(2,1)}, bf16[1024,2048]{1,0:T(8,128)(2,1)}, bf16...) custom-call(bf16[1024,512]{1,0:T(8,128)(2,1)} %copy-done.9, bf16[512,2048]{1,0:T(8,128)(2,1)} %weight_ref.3, ...), custom_call_target="tpu_custom_call" | custom-call | flops 27917287424 | bytes 262144000 | tf_op jit(solution)/shard_map/pallas_call | solution.py:749
  270.9 0.0 all-gather.2.cloned.1.call-done.grad_ref.grad_hbm
  270.9 24.9 %shard_map.239 = (bf16[1024,1024]{1,0:T(8,128)(2,1)}, bf16[1024,1024]{1,0:T(8,128)(2,1)}, bf16[2048,1024]{1,0:T(8,128)(2,1)}, bf16[2048,1024]{1,0:T(8,128)(2,1)}, bf16[1024,2048]{1,0:T(8,128)(2,1)}) custom-call(bf16[2048,1024]{1,0:T(8,128)(2,1)} %get-tuple-element.77.flip_ref, bf16[1024,2048]{1,0:T(8,128)(2,1)} %all-gather.2.cloned.1.call-done.grad_ref.grad_hbm, ...), custom_call_target="tpu_custom_call" | custom-call | flops 17179869184 | bytes 39845888 | tf_op jit(solution)/shard_map/pallas_call | solution.py:942
  295.8 0.0 all-reduce.4.cloned.1.call-update
  295.8 0.0 reduce-scatter.2.cloned.1.call-start
  295.9 24.9 %shard_map.240 = (bf16[1024,1024]{1,0:T(8,128)(2,1)}, bf16[1024,1024]{1,0:T(8,128)(2,1)}, bf16[2048,1024]{1,0:T(8,128)(2,1)}, bf16[2048,1024]{1,0:T(8,128)(2,1)}, bf16[1024,2048]{1,0:T(8,128)(2,1)}) custom-call(bf16[2048,1024]{1,0:T(8,128)(2,1)} %get-tuple-element.77.flip_ref, bf16[1024,2048]{1,0:T(8,128)(2,1)} %all-gather.2.cloned.1.call-done.grad_ref.grad_hbm, ...), custom_call_target="tpu_custom_call" | custom-call | flops 17179869184 | bytes 39845888 | tf_op jit(solution)/shard_map/pallas_call | solution.py:942
  320.8 142.9 %shard_map.241 = (bf16[1024,2048]{1,0:T(8,128)(2,1)}, f32[256,2048]{1,0:T(8,128)}, f32[8,2048]{1,0:T(8,128)}, bf16[1024,2048]{1,0:T(8,128)(2,1)}, bf16[2048,1024]{1,0:T(8,128)(2,1)}) custom-call(bf16[1024,1024]{1,0:T(8,128)(2,1)} %get-tuple-element.82.d_gate_a, bf16[1024,1024]{1,0:T(8,128)(2,1)} %get-tuple-element.83.d_gate_b, ...), custom_call_target="tpu_custom_call" | custom-call | flops 17179869184 | bytes 262144000 | tf_op jit(solution)/shard_map/pallas_call | solution.py:882
  463.7 0.0 copy-start.6
  463.7 1.5 copy-done.6
  465.2 0.0 copy-start.10
  465.2 29.5 %shard_map.242 = (bf16[1024,512]{1,0:T(8,128)(2,1)S(1)}, bf16[1024,512]{1,0:T(8,128)(2,1)S(1)}, bf16[1024,512]{1,0:T(8,128)(2,1)S(1)}, f32[4,8,128]{2,1,0:T(8,128)S(1)}) custom-call(f32[4]{0:T(128)S(1)} %add_divide_fusion.gate_ref, s32[1]{0:T(128)} %bitcast.valid_ref, bf16[1024,2048]{1,0:T(8,128)(2,1)} %get-tuple-element.88.d_out_ref, ...), custom_call_target="tpu_custom_call" | custom-call | flops 7516192768 | bytes 104857600 | tf_op jit(solution)/shard_map/pallas_call | solution.py:1400
  494.7 0.0 copy-done.10
  494.7 19.7 %shard_map.243 = (bf16[1024,4096]{1,0:T(8,128)(2,1)}, bf16[2048,512]{1,0:T(8,128)(2,1)}, bf16[2048,512]{1,0:T(8,128)(2,1)}, bf16[2048,512]{1,0:T(8,128)(2,1)}, b...) custom-call(bf16[1024,2048]{1,0:T(8,128)(2,1)} %get-tuple-element.76.rows_ref, ...), custom_call_target="tpu_custom_call", output_to_operand_aliasing={{0}: (9, {})} | custom-call | flops 15032385536 | bytes 31457280 | tf_op jit(solution)/shard_map/pallas_call | solution.py:1097
  514.5 0.0 copy-start.1
  514.5 0.0 reduce-scatter.2.cloned.1.call-update
  514.5 0.0 copy-start.13
  514.5 0.0 copy-start.3
  514.6 1.1 copy-done.1
  515.7 0.3 fusion.7
  516.0 0.6 slice_multiply_fusion.1
  516.6 0.7 fusion.8
  517.3 0.1 slice_reduce_fusion
  517.4 0.1 broadcast_select_fusion
  517.5 0.1 select_n.39
  517.6 0.0 copy-done.13
  517.7 0.0 copy-done.3
  517.7 0.6 fusion.9.refs_0_
  518.3 114.3 %shard_map.244 = (f32[40,128]{1,0:T(8,128)}, bf16[2048,1024]{1,0:T(8,128)(2,1)}, bf16[512,2048]{1,0:T(8,128)(2,1)}, bf16[2048,512]{1,0:T(8,128)(2,1)}, bf16[2048...) custom-call(f32[40,128]{1,0:T(8,128)} %fusion.9.refs_0_, bf16[2048,1024]{1,0:T(8,128)(2,1)} %get-tuple-element.101.refs_1_, ...), custom_call_target="tpu_custom_call" | custom-call | bytes 377487360 | tf_op jit(solution)/shard_map/pallas_call | solution.py:265
  632.7 1.3 dynamic_slice.7
  633.9 1.3 slice_bitcast_fusion
  635.3 0.0 all-reduce.4.cloned.1.call-done
  635.3 0.0 copy-start.12
  635.3 34.3 %shard_map.245 = (f32[2048,2048]{1,0:T(8,128)}, f32[2048,2048]{1,0:T(8,128)}, f32[2048,2048]{1,0:T(8,128)}, f32[512,2048]{1,0:T(8,128)}, f32[2048,512]{1,0:T(8,1...) custom-call(bf16[2048,1024]{1,0:T(8,128)(2,1)} %get-tuple-element.124.refs_0_, ...), custom_call_target="tpu_custom_call" | custom-call | bytes 100663296 | tf_op jit(solution)/shard_map/pallas_call | solution.py:1043
  669.6 3.6 reduce-scatter.2.cloned.1.call-done
  673.2 0.0 copy-start.11
  673.2 1.9 fusion.2
  675.1 0.0 copy-done.12
  675.1 0.0 copy-done.11
  675.1 4.1 fusion.6
  (9 shorter events, 0.1 us)
Async XLA Ops:
  7.2 263.7 %all-gather.2.cloned.1.call-start = ((), (), s32[]{:S(2)}) async-start(), calls=%async_computation.1 | async-start | bytes 5242880 | tf_op jit(solution)/shard_map/all_gather | solution.py:1458
  7.2 1.2 copy-start
  8.5 0.7 copy-start.2
  9.2 76.5 %copy-start.14 = (s32[2]{0:T(128)S(1)}, s32[2]{0:T(128)}, u32[]{:S(2)}) copy-start(s32[2]{0:T(128)} %param.25) | copy-start | bytes 28
  9.2 77.9 %copy-start.15 = (f32[4]{0:T(128)S(1)}, f32[4]{0:T(128)}, u32[]{:S(2)}) copy-start(f32[4]{0:T(128)} %param.24) | copy-start | bytes 52
  84.5 1.0 copy-start.7
  85.5 21.8 %copy-start.5 = (bf16[1024,512]{1,0:T(8,128)(2,1)}, bf16[1024,512]{1,0:T(8,128)(2,1)S(1)}, u32[]{:S(2)}) copy-start(bf16[1024,512]{1,0:T(8,128)(2,1)S(1)} %get-tuple-element.71.key_ref) | copy-start | bytes 3145732
  85.5 549.7 %all-reduce.4.cloned.1.call-start = ((), (), s32[]{:S(2)}) async-start(), calls=%async_computation.3 | async-start | bytes 25165824 | tf_op jit(solution)/shard_map/psum | solution.py:1474
  87.1 1.2 copy-start.8
  107.3 1.3 copy-start.4
  108.6 1.0 copy-start.9
  295.8 377.3 %reduce-scatter.2.cloned.1.call-start = ((), (), s32[]{:S(2)}) async-start(), calls=%async_computation.2 | async-start | bytes 10485760 | tf_op jit(solution)/shard_map/reduce_scatter | solution.py:1517
  463.7 1.5 copy-start.6
  465.2 29.5 %copy-start.10 = (bf16[1024,512]{1,0:T(8,128)(2,1)S(1)}, bf16[1024,512]{1,0:T(8,128)(2,1)}, u32[]{:S(2)}) copy-start(bf16[1024,512]{1,0:T(8,128)(2,1)} %copy-done.9) | copy-start | bytes 3145732
  514.5 1.2 copy-start.1
  514.5 3.1 copy-start.13
  514.5 3.2 copy-start.3
  635.3 39.8 %copy-start.12 = (f32[256,2048]{1,0:T(8,128)S(1)}, f32[256,2048]{1,0:T(8,128)}, u32[]{:S(2)}) copy-start(f32[256,2048]{1,0:T(8,128)} %get-tuple-element.96) | copy-start | bytes 6291460
  673.2 1.9 copy-start.11
Sparse Core Ops, SparseCore 0:
  85.7 118.5 all-gather.1
  296.0 228.4 all-reduce.3
  526.9 146.1 reduce-scatter.1
